TPU v7x, 512 devices: a whole 4x8x8 slice. The times are simulated.
512 devices in a mesh: lon: 32 (over x, y_hi, core), head: 16 (over z, y_lo).
Axes of the slice: x: 4, y: 8 (y_hi: 4, y_lo: 2; y = y_hi * 2 + y_lo), z: 8, core: 2. Of those that a mesh axis runs over, the one named last changes fastest.
Arguments:
- latents: bfloat16 [3, 48, 256, 1024], P(None, 'head', 'lon'), may hold values from -16 to 16
- out_grad: bfloat16 [3, 48, 256, 1024], P(None, 'head', 'lon'), may hold values from -6 to 6
- qkv_weight: bfloat16 [16, 1024, 192], P('head'), as said below
- out_weight: bfloat16 [16, 64, 1024], replicated, may hold values from -0.1875 to 0.1875
Outputs:
- mixed: bfloat16 [3, 48, 256, 1024], P(None, 'head', 'lon')
- latent_grad: bfloat16 [3, 48, 256, 1024], P(None, 'head', 'lon')
- qkv_grad: float32 [16, 1024, 192], P('head')
Inputs may be any that keep to these rules, and one draw needn't show every extreme that they name: `qkv_weight`: entries lie within -14 / sqrt(1024) and 14 / sqrt(1024).
All inputs are finite; a program needn't handle non-finite values.
Results may differ from a plain program's by a relative error of at most 0.024.
The roundings to bfloat16 on the way count: a program that leaves them out, or rounds other values in their place, can miss the bound.
Values may be sent and summed in bfloat16 or wider, within the bound.
No kernel may reach another device: no remote copies, remote signals or barrier semaphores. Data moves between devices by JAX's collectives and lax.ppermute only.
A program may use at most 64 MiB of HBM per device.

v0:
```python
import jax
import jax.numpy as jnp
from jax import lax
from jax.experimental import pallas as pl
from jax.experimental.pallas import tpu as pltpu
from jax.sharding import Mesh, PartitionSpec as P

HD = 64
RANKS = 16
TOK = 72
HEAD = ("z", "yl")
LON = ("x", "yh", "core")
F32 = jnp.float32
BF16 = jnp.bfloat16


def dot_nt(a, b):
    return lax.dot_general(a, b, (((1,), (1,)), ((), ())), preferred_element_type=F32)


def dot_nn(a, b):
    return lax.dot_general(a, b, (((1,), (0,)), ((), ())), preferred_element_type=F32)


def dot_tn(a, b):
    return lax.dot_general(a, b, (((0,), (0,)), ((), ())), preferred_element_type=F32)


def call(body, outs, scratch=(), smem=(), n_in=1, flops=0, moved=0):
    specs = [
        pl.BlockSpec(memory_space=pltpu.SMEM if i in smem else pltpu.VMEM) for i in range(n_in)
    ]
    return pl.pallas_call(
        body,
        out_shape=[jax.ShapeDtypeStruct(s, d) for s, d in outs],
        in_specs=specs,
        out_specs=[pl.BlockSpec(memory_space=pltpu.VMEM) for _ in outs],
        scratch_shapes=list(scratch),
        cost_estimate=pl.CostEstimate(flops=flops, bytes_accessed=moved, transcendentals=0),
        compiler_params=pltpu.CompilerParams(vmem_limit_bytes=56 << 20),
    )


def low_half(shape):
    return lax.broadcasted_iota(jnp.int32, shape, len(shape) - 2) % 8 < 4


def pack_pair(value):
    half = value.shape[0] // 2
    groups = value.reshape(2, half * TOK // 8, 8, 128)
    first, second = groups[0], groups[1]
    low = low_half(first.shape)
    west = jnp.where(low, first, pltpu.roll(second, 4, 1))
    east = jnp.where(low, pltpu.roll(first, 4, 1), second)
    return west.reshape(half, TOK, 128), east.reshape(half, TOK, 128)


def unpack_pair(west, east):
    half = west.shape[0]
    west = west.reshape(half * TOK // 8, 8, 128)
    east = east.reshape(half * TOK // 8, 8, 128)
    low = low_half(west.shape)
    first = jnp.where(low, west, pltpu.roll(east, 4, 1))
    second = jnp.where(low, pltpu.roll(west, 4, 1), east)
    return first.reshape(half, TOK, 128), second.reshape(half, TOK, 128)


def fold_rows(value):
    rest = jnp.concatenate([value[40:], jnp.zeros((8, HD), F32)], axis=0)
    return jnp.concatenate([value[:40], rest], axis=1)


def unfold_rows(value):
    return jnp.concatenate([value[:, :HD], value[:32, HD:]], axis=0)


def turned(ref):
    return jnp.concatenate([ref[HD : 3 * HD], ref[0:HD]], axis=0)


def token_grad_kernel(grad_ref, weight_ref, out_ref):
    for pair in range(RANKS // 2):
        rows = weight_ref[2 * pair : 2 * pair + 2].reshape(2 * HD, -1)
        both = dot_nt(grad_ref[...], rows)
        out_ref[2 * pair] = fold_rows(both[:, :HD]).astype(BF16)
        out_ref[2 * pair + 1] = fold_rows(both[:, HD:]).astype(BF16)


def project_kernel(
    table_ref, tokens_ref, own_ref, other_ref,
    kv_ref, q_ref, swap_ref, west_ref, east_ref, west2_ref, east2_ref,
    kv32, kv32b,
):
    own, other = turned(own_ref), turned(other_ref)
    for chunk in range(2):
        rows = tokens_ref[chunk * 288 : (chunk + 1) * 288, :]
        proj = dot_nt(rows, own).astype(BF16).astype(F32)
        proj2 = dot_nt(rows, other).astype(BF16).astype(F32)
        for part in range(4):
            row = table_ref[chunk * 4 + part]
            piece = proj[part * TOK : (part + 1) * TOK]
            kv32[row] = piece[:, :128]
            kv_ref[row] = piece[:, :128].astype(BF16)
            q_ref[row] = piece[:, 128:].astype(BF16)
            piece = proj2[part * TOK : (part + 1) * TOK]
            kv32b[row] = piece[:, :128]
            swap_ref[row] = piece.astype(BF16)
    west, east = pack_pair(kv32[...])
    west_ref[...] = west.astype(BF16)
    east_ref[...] = east.astype(BF16)
    west, east = pack_pair(kv32b[...])
    west2_ref[...] = west.astype(BF16)
    east2_ref[...] = east.astype(BF16)


def attend_kernel(
    place_ref, kv_ref, q_ref, swapped_ref, grad_ref, from_e_ref, from_w_ref, from_e2_ref, from_w2_ref,
    out_ref, dq_ref, dkv_ref, to_e_ref, to_w_ref,
    keys, queries, halo, dhalo,
):
    scale = HD ** (-0.5)
    yl = place_ref[0]
    side = unpack_pair(from_e_ref[...].astype(F32), from_w_ref[...].astype(F32))
    side2 = unpack_pair(from_e2_ref[...].astype(F32), from_w2_ref[...].astype(F32))
    for row in range(8):
        mine, theirs = 2 * row + yl, 2 * row + 1 - yl
        keys[mine] = kv_ref[row].astype(F32)
        queries[mine] = q_ref[row].astype(F32)
        both = swapped_ref[row].astype(F32)
        keys[theirs] = both[:, :128]
        queries[theirs] = both[:, 128:]
        halo[mine] = side[row // 4][row % 4]
        halo[theirs] = side2[row // 4][row % 4]
    zeros = jnp.zeros((2 * TOK, HD), F32)
    windows = RANKS // 2
    for w in range(windows):
        lo, hi = max(2 * w - 1, 0), min(2 * w + 3, RANKS)
        count = (hi - lo) * TOK
        query = queries[2 * w : 2 * w + 2].reshape(2 * TOK, HD) * scale
        outer = jnp.concatenate(
            [unfold_rows(grad_ref[2 * w + i].astype(F32)) for i in range(2)], axis=0
        )
        lhs = jnp.concatenate(
            [
                jnp.concatenate([query, zeros], axis=1),
                jnp.concatenate([zeros, outer], axis=1),
            ],
            axis=0,
        ).astype(BF16)
        pairs = jnp.concatenate(
            [keys[lo:hi].reshape(count, 128), halo[lo:hi].reshape(count, 128)], axis=0
        ).astype(BF16)
        both = dot_nt(lhs, pairs)
        score, prob_grad = both[: 2 * TOK], both[2 * TOK :]
        powers = jnp.exp(score - jnp.max(score, axis=-1, keepdims=True))
        probs = powers * (1.0 / jnp.sum(powers, axis=-1, keepdims=True))
        centre = jnp.sum(probs * prob_grad, axis=-1, keepdims=True)
        score_grad = (probs * (prob_grad - centre)).astype(BF16)
        stack = jnp.concatenate([score_grad, probs.astype(BF16)], axis=0)
        mixed = dot_nn(stack, pairs)
        dq_ref[2 * w : 2 * w + 2] = (mixed[: 2 * TOK, :HD] * scale).reshape(2, TOK, HD)
        for i in range(2):
            rows = mixed[(2 + i) * TOK : (3 + i) * TOK, HD:]
            out_ref[2 * w + i] = fold_rows(rows).astype(BF16)
        grads = dot_tn(stack, lhs)
        own = grads[:count].reshape(hi - lo, TOK, 128)
        side = grads[count:].reshape(hi - lo, TOK, 128)
        for i, rank in enumerate(range(lo, hi)):
            seen = w > 0 and rank <= 2 * w
            if seen:
                dkv_ref[rank] += own[i]
                dhalo[rank] += side[i]
            else:
                dkv_ref[rank] = own[i]
                dhalo[rank] = side[i]
    to_e, to_w = pack_pair(dhalo[...])
    to_e_ref[...] = to_e.astype(BF16)
    to_w_ref[...] = to_w.astype(BF16)


def combine_kernel(
    place_ref, dq_ref, dkv_ref, got_w_ref, got_e_ref, pg_ref, mine_ref, swap_ref, pg32
):
    yl = place_ref[0]
    first, second = unpack_pair(got_w_ref[...].astype(F32), got_e_ref[...].astype(F32))
    for half, add in ((0, first), (1, second)):
        span = slice(8 * half, 8 * half + 8)
        pg32[span, :, 0:128] = dkv_ref[span] + add
        pg32[span, :, 128:192] = dq_ref[span]
    pg_ref[...] = pg32[...].astype(BF16)
    for row in range(8):
        mine_ref[row] = pg32[2 * row + yl].astype(BF16)
        swap_ref[row] = pg32[2 * row + 1 - yl].astype(BF16)


def share_kernel(table_ref, mine_ref, got_ref, own_ref, other_ref, *out_refs):
    own, other = turned(own_ref), turned(other_ref)
    for chunk in range(2):
        picks = [table_ref[4 * chunk + i] for i in range(4)]
        rows = jnp.concatenate([mine_ref[p].astype(F32) for p in picks], axis=0).astype(BF16)
        rows2 = jnp.concatenate([got_ref[p].astype(F32) for p in picks], axis=0).astype(BF16)
        part = dot_nn(rows, own) + dot_nn(rows2, other)
        for i in range(4):
            out_refs[4 * chunk + i][...] = part[i * TOK : (i + 1) * TOK].astype(BF16)


def weight_grad_kernel(table_ref, tokens_ref, tokens2_ref, pg_ref, piece_ref):
    total = None
    for chunk in range(4):
        rows = jnp.concatenate(
            [pg_ref[table_ref[4 * chunk + i]].astype(F32) for i in range(4)], axis=0
        ).astype(BF16)
        source = tokens_ref if chunk < 2 else tokens2_ref
        span = slice((chunk % 2) * 288, (chunk % 2) * 288 + 288)
        part = dot_tn(rows, source[span, :])
        total = part if total is None else total + part
    total = jnp.concatenate([total[128:192], total[0:128]], axis=0).astype(BF16)
    for g in range(4):
        for j in range(8):
            piece_ref[8 * g + j] = total[48 * g : 48 * g + 48, 128 * j : 128 * j + 128]


def mix_kernel(att_ref, weight_ref, out_ref):
    rows = [unfold_rows(att_ref[h].astype(F32)) for h in range(RANKS)]
    rows = jnp.concatenate(rows, axis=1).astype(BF16)
    out_ref[...] = dot_nn(rows, weight_ref[...]).astype(BF16)


def shift(value, axis, size, distance):
    return lax.ppermute(value, axis, [(i, (i + distance) % size) for i in range(size)])


def exchange(value, axis):
    return lax.all_to_all(value, axis, 0, 0, tiled=True)


def step(latents, out_grad, qkv_weight, out_weight):
    width = latents.shape[-1]
    z, yl = lax.axis_index("z"), lax.axis_index("yl")
    mine = latents.reshape(TOK, width)
    own = jnp.swapaxes(qkv_weight[0], 0, 1)
    d1, d7, d2, d6 = (shift(mine, "z", 8, d) for d in (1, 7, 2, 6))
    other = shift(own, "yl", 2, 1)
    d3, d5 = shift(d2, "z", 8, 1), shift(d6, "z", 8, -1)
    d4 = shift(d2, "z", 8, 2)
    tokens = jnp.concatenate([mine, d1, d7, d2, d6, d3, d5, d4], axis=0)
    distance = jnp.array([0, 1, 7, 2, 6, 3, 5, 4], jnp.int32)
    rows = ((z - distance) % 8).astype(jnp.int32)
    place = yl.astype(jnp.int32).reshape(1)

    (token_grad,) = call(
        token_grad_kernel, [((RANKS, 40, 128), BF16)], n_in=2, flops=2 * TOK * width * width
    )(out_grad.reshape(TOK, width), out_weight)
    band_grad = exchange(token_grad, HEAD)

    kv, query, swap, to_w, to_e, to_w2, to_e2 = call(
        project_kernel,
        [((8, TOK, 128), BF16), ((8, TOK, HD), BF16), ((8, TOK, 3 * HD), BF16)]
        + [((4, TOK, 128), BF16)] * 4,
        scratch=[pltpu.VMEM((8, TOK, 128), F32)] * 2,
        smem=(0,),
        n_in=4,
        flops=2 * 1152 * 192 * width,
    )(rows, tokens, own, other)
    from_e = shift(to_w, LON, 32, -1)
    from_w = shift(to_e, LON, 32, 1)
    from_e2 = lax.ppermute(to_w2, LON + ("yl",), across(-1))
    from_w2 = lax.ppermute(to_e2, LON + ("yl",), across(1))
    swapped = shift(swap, "yl", 2, 1)
    late, from_e, from_w, from_e2, from_w2, swapped = lax.optimization_barrier(
        (tokens, from_e, from_w, from_e2, from_w2, swapped)
    )
    tokens2 = shift(late, "yl", 2, 1)
    attended, dq, dkv, grad_east, grad_west = call(
        attend_kernel,
        [
            ((RANKS, 40, 128), BF16),
            ((RANKS, TOK, HD), F32),
            ((RANKS, TOK, 128), F32),
            ((8, TOK, 128), BF16),
            ((8, TOK, 128), BF16),
        ],
        scratch=[
            pltpu.VMEM((RANKS, TOK, 128), F32),
            pltpu.VMEM((RANKS, TOK, HD), F32),
            pltpu.VMEM((RANKS, TOK, 128), F32),
            pltpu.VMEM((RANKS, TOK, 128), F32),
        ],
        smem=(0,),
        n_in=9,
        flops=8 * 6 * 2 * 144 * 576 * 128,
    )(place, kv, query, swapped, band_grad, from_e, from_w, from_e2, from_w2)
    got_west = shift(grad_east, LON, 32, 1)
    got_east = shift(grad_west, LON, 32, -1)
    token_att = exchange(attended, HEAD)

    pg, pg_mine, pg_swap = call(
        combine_kernel,
        [((RANKS, TOK, 3 * HD), BF16), ((8, TOK, 3 * HD), BF16), ((8, TOK, 3 * HD), BF16)],
        scratch=[pltpu.VMEM((RANKS, TOK, 3 * HD), F32)],
        smem=(0,),
        n_in=5,
        flops=1 << 20,
    )(place, dq, dkv, got_west, got_east)
    pg_got = shift(pg_swap, "yl", 2, 1)
    (pieces,) = call(
        weight_grad_kernel,
        [((32, 48, 128), BF16)],
        smem=(0,),
        n_in=4,
        flops=2 * 1152 * 192 * width,
    )(
        jnp.concatenate([2 * rows + yl, 2 * rows + 1 - yl]).astype(jnp.int32),
        tokens, tokens2, pg,
    )
    pieces = exchange(pieces, LON)
    reach = (4, 3, 5, 2, 6, 1, 7, 0)
    shares = call(
        share_kernel,
        [((TOK, width), BF16)] * 8,
        smem=(0,),
        n_in=5,
        flops=2 * 576 * 384 * width,
    )(((z + jnp.array(reach, jnp.int32)) % 8).astype(jnp.int32), pg_mine, pg_got, own, other)
    shares = [shift(s, "z", 8, d) if d else s for s, d in zip(shares, reach)]
    summed = jnp.sum(pieces.astype(F32), axis=0).astype(BF16)
    copies = exchange(jnp.broadcast_to(summed[None], (32, 48, 128)), LON)
    (mixed,) = call(mix_kernel, [((TOK, width), BF16)], n_in=2, flops=2 * TOK * width * width)(
        token_att, out_weight.reshape(width, width)
    )
    latent_grad = sum(s.astype(F32) for s in shares).astype(BF16)
    grad = copies.reshape(4, 8, 48, 128).transpose(0, 2, 1, 3).reshape(3 * HD, width)
    qkv_grad = jnp.swapaxes(grad, 0, 1).astype(F32)[None]
    return mixed.reshape(latents.shape), latent_grad.reshape(latents.shape), qkv_grad


def across(distance):
    return [(2 * i + j, 2 * ((i + distance) % 32) + 1 - j) for i in range(32) for j in range(2)]


def solution(mesh):
    split = Mesh(mesh.devices.reshape(4, 4, 2, 8, 2), LON + HEAD)
    rows = P(None, HEAD, LON, None)
    return jax.shard_map(
        step,
        mesh=split,
        in_specs=(rows, rows, P(HEAD, None, None), P()),
        out_specs=(rows, rows, P(HEAD, None, None)),
        check_vma=False,
    )
```

profile of v0, /device:TPU:1, one launch (start us, length us, event | category | flops | bytes accessed | tf_op | source)
XLA Modules:
  0.0 216.3 jit_solution(867655143500503206)
XLA Ops:
  0.6 11.5 %collective-permute-start.3 = (bf16[72,1024]{1,0:T(8,128)(2,1)}, bf16[72,1024]{1,0:T(8,128)(2,1)S(1)}, u32[]{:S(2)}, u32[]{:S(2)}) collective-permute-start(bf16[72,1024]{1,0:T(8,128)(2,1)} %bitcast.32), channel_id=1, source_target_pairs={{0,12},{2,14},{4,0},{6,2},{8,4},{10,6},{12,8},{14,10},{1,13},{3,15... | collective-permute-start | bytes 442376 | tf_op jit(solution)/shard_map/ppermute | solution.py:230
  14.0 5.5 %collective-permute-start.1 = (bf16[72,1024]{1,0:T(8,128)(2,1)}, bf16[72,1024]{1,0:T(8,128)(2,1)S(1)}, u32[]{:S(2)}, u32[]{:S(2)}) collective-permute-start(bf16[72,1024]{1,0:T(8,128)(2,1)} %bitcast.34), channel_id=1, source_target_pairs={{0,14},{2,0},{4,2},{6,4},{8,6},{10,8},{12,10},{14,12},{1,15},{3,1}... | collective-permute-start | bytes 442376 | tf_op jit(solution)/shard_map/ppermute | solution.py:230
  21.5 3.2 %collective-permute-start.7 = (bf16[192,1024]{1,0:T(8,128)(2,1)}, bf16[192,1024]{1,0:T(8,128)(2,1)S(1)}, u32[]{:S(2)}, u32[]{:S(2)}) collective-permute-start(bf16[192,1024]{1,0:T(8,128)(2,1)} %bitcast.27), channel_id=1, source_target_pairs={{0,1},{1,0},{2,3},{3,2},{4,5},{5,4},{6,7},{7,6},{8,9},{9,8},{10,11... | collective-permute-start | bytes 1179656 | tf_op jit(solution)/shard_map/ppermute | solution.py:230
  31.3 4.1 %collective-permute-start.5 = (bf16[72,1024]{1,0:T(8,128)(2,1)S(1)}, bf16[72,1024]{1,0:T(8,128)(2,1)S(1)}, u32[]{:S(2)}, u32[]{:S(2)}) collective-permute-start(bf16[72,1024]{1,0:T(8,128)(2,1)S(1)} %collective-permute-done.3), channel_id=1, source_target_pairs={{0,14},{2,0},{4,2},{6,4},{8,6},{10,8},{12,10},{14,12},{1,15},{3,1}... | collective-permute-start | bytes 442376 | tf_op jit(solution)/shard_map/ppermute | solution.py:230
  35.4 5.5 %collective-permute-done.4 = bf16[72,1024]{1,0:T(8,128)(2,1)S(1)} collective-permute-done((bf16[72,1024]{1,0:T(8,128)(2,1)S(1)}, bf16[72,1024]{1,0:T(8,128)(2,1)S(1)}, u32[]{:S(2)}, u32[]{:S(2)}) %collective-permute-start.4) | collective-permute-done | bytes 147488 | tf_op jit(solution)/shard_map/ppermute | solution.py:230
  42.1 3.2 %shard_map.85 = (bf16[8,72,128]{2,1,0:T(8,128)(2,1)}, bf16[8,72,64]{2,1,0:T(8,128)(2,1)}, bf16[8,72,192]{2,1,0:T(8,128)(2,1)}, bf16[4,72,128]{2,1,0:T(8,128)(2,1...) custom-call(s32[8]{0:T(128)} %get-tuple-element.62.table_ref, ...), custom_call_target="tpu_custom_call" | custom-call | flops 452984832 | tf_op jit(solution)/shard_map/pallas_call | solution.py:256
  47.4 3.9 %collective-permute-start.8 = (bf16[4,72,128]{2,1,0:T(8,128)(2,1)}, bf16[4,72,128]{2,1,0:T(8,128)(2,1)S(1)}, u32[]{:S(2)}, u32[]{:S(2)}) collective-permute-start(bf16[4,72,128]{2,1,0:T(8,128)(2,1)} %get-tuple-element.34), channel_id=1, source_target_pairs={{0,496},{16,0},{32,16},{48,32},{64,48},{80,64},{96,80},{112,96},{1... | collective-permute-start | bytes 221192 | tf_op jit(solution)/shard_map/ppermute | solution.py:230
  51.2 4.1 %collective-permute-start.9 = (bf16[4,72,128]{2,1,0:T(8,128)(2,1)}, bf16[4,72,128]{2,1,0:T(8,128)(2,1)S(1)}, u32[]{:S(2)}, u32[]{:S(2)}) collective-permute-start(bf16[4,72,128]{2,1,0:T(8,128)(2,1)} %get-tuple-element.35), channel_id=1, source_target_pairs={{0,16},{16,32},{32,48},{48,64},{64,80},{80,96},{96,112},{112,128},... | collective-permute-start | bytes 221192 | tf_op jit(solution)/shard_map/ppermute | solution.py:230
  55.4 4.6 %collective-permute-start.10 = (bf16[4,72,128]{2,1,0:T(8,128)(2,1)}, bf16[4,72,128]{2,1,0:T(8,128)(2,1)S(1)}, u32[]{:S(2)}, u32[]{:S(2)}) collective-permute-start(bf16[4,72,128]{2,1,0:T(8,128)(2,1)} %get-tuple-element.36), channel_id=1, source_target_pairs={{0,497},{1,496},{16,1},{17,0},{32,17},{33,16},{48,33},{49,32},{64,... | collective-permute-start | bytes 221192 | tf_op jit(solution)/shard_map/ppermute | solution.py:267
  60.0 2.7 %collective-permute-start.11 = (bf16[4,72,128]{2,1,0:T(8,128)(2,1)}, bf16[4,72,128]{2,1,0:T(8,128)(2,1)S(1)}, u32[]{:S(2)}, u32[]{:S(2)}) collective-permute-start(bf16[4,72,128]{2,1,0:T(8,128)(2,1)} %get-tuple-element.37), channel_id=1, source_target_pairs={{0,17},{1,16},{16,33},{17,32},{32,49},{33,48},{48,65},{49,64},{64,... | collective-permute-start | bytes 221192 | tf_op jit(solution)/shard_map/ppermute | solution.py:268
  63.7 7.1 %collective-permute-done.11.from_w2_ref = bf16[4,72,128]{2,1,0:T(8,128)(2,1)S(1)} collective-permute-done((bf16[4,72,128]{2,1,0:T(8,128)(2,1)}, bf16[4,72,128]{2,1,0:T(8,128)(2,1)S(1)}, u32[]{:S(2)}, u32[]{:S(2)}) %collective-permute-start.11) | collective-permute-done | bytes 73760 | tf_op jit(solution)/shard_map/ppermute | solution.py:268
  72.8 3.3 %shard_map.86 = bf16[16,40,128]{2,1,0:T(8,128)(2,1)} custom-call(bf16[72,1024]{1,0:T(8,128)(2,1)} %bitcast.30, bf16[16,64,1024]{2,1,0:T(8,128)(2,1)} %weight_ref.1), custom_call_target="tpu_custom_call" | custom-call | flops 150994944 | tf_op jit(solution)/shard_map/pallas_call | solution.py:251
  76.1 21.4 %all_to_all.20.grad_ref = bf16[16,40,128]{2,1,0:T(8,128)(2,1)} all-to-all(bf16[16,40,128]{2,1,0:T(8,128)(2,1)} %shard_map.86), channel_id=1, replica_groups=mesh['x'=4,'yh'=4,'core'=2,'z'=8,'yl'=2] {'z','yl'}, dimensions={0} | all-to-all | bytes 327680 | tf_op jit(solution)/shard_map/all_to_all | solution.py:234
  97.5 8.3 %shard_map.87 = (bf16[16,40,128]{2,1,0:T(8,128)(2,1)}, f32[16,72,64]{2,1,0:T(8,128)}, f32[16,72,128]{2,1,0:T(8,128)}, bf16[8,72,128]{2,1,0:T(8,128)(2,1)}, bf16[8,72,128]{2,1,0:T(8,128)(2,1)}) custom-call(s32[1]{0:T(128)} %bitcast.place_ref, bf16[8,72,128]{2,1,0:T(8,128)(2,1)} %get-tuple-element.32.kv_ref, bf16[8,72,64]{2,1,0:T(8,128)(2,1)} %get-tuple-element.33.q_ref, ...), custom_call_target="tpu_custom_call" | custom-call | flops 1019215872 | tf_op jit(solution)/shard_map/pallas_call | solution.py:274
  105.8 5.3 %collective-permute-start.13 = (bf16[8,72,128]{2,1,0:T(8,128)(2,1)}, bf16[8,72,128]{2,1,0:T(8,128)(2,1)S(1)}, u32[]{:S(2)}, u32[]{:S(2)}) collective-permute-start(bf16[8,72,128]{2,1,0:T(8,128)(2,1)} %get-tuple-element.47), channel_id=1, source_target_pairs={{0,16},{16,32},{32,48},{48,64},{64,80},{80,96},{96,112},{112,128},... | collective-permute-start | bytes 442376 | tf_op jit(solution)/shard_map/ppermute | solution.py:230
  111.1 5.4 %collective-permute-start.14 = (bf16[8,72,128]{2,1,0:T(8,128)(2,1)}, bf16[8,72,128]{2,1,0:T(8,128)(2,1)S(1)}, u32[]{:S(2)}, u32[]{:S(2)}) collective-permute-start(bf16[8,72,128]{2,1,0:T(8,128)(2,1)} %get-tuple-element.48), channel_id=1, source_target_pairs={{0,496},{16,0},{32,16},{48,32},{64,48},{80,64},{96,80},{112,96},{1... | collective-permute-start | bytes 442376 | tf_op jit(solution)/shard_map/ppermute | solution.py:230
  119.3 2.5 %shard_map.89 = (bf16[16,72,192]{2,1,0:T(8,128)(2,1)}, bf16[8,72,192]{2,1,0:T(8,128)(2,1)}, bf16[8,72,192]{2,1,0:T(8,128)(2,1)}) custom-call(s32[1]{0:T(128)} %bitcast.place_ref, f32[16,72,64]{2,1,0:T(8,128)} %get-tuple-element.45.dq_ref, f32[16,72,128]{2,1,0:T(8,128)} %get-tuple-element.46.dkv_ref, bf16[8,72,128]{2,1,0:T(8,128)(2,1)} %copy-done.5, ...), custom_call_target="tpu_custom_call" | custom-call | flops 1048576 | tf_op jit(solution)/shard_map/pallas_call | solution.py:297
  122.9 3.6 %shard_map.91 = bf16[32,48,128]{2,1,0:T(8,128)(2,1)} custom-call(s32[16]{0:T(128)} %pad_add_fusion.table_ref, bf16[576,1024]{1,0:T(8,128)(2,1)} %copy-done, bf16[576,1024]{1,0:T(8,128)(2,1)} %copy-done.1, bf16[16,72,192]{2,1,0:T(8,128)(2,1)} %get-tuple-element.60.pg_ref), custom_call_target="tpu_custom_call" | custom-call | flops 452984832 | tf_op jit(solution)/shard_map/pallas_call | solution.py:306
  126.5 30.4 %all_to_all.21 = bf16[32,48,128]{2,1,0:T(8,128)(2,1)S(1)} all-to-all(bf16[32,48,128]{2,1,0:T(8,128)(2,1)} %shard_map.91), channel_id=1, replica_groups=mesh['x'=4,'yh'=4,'core'=2,'z'=8,'yl'=2] {'x','yh','core'}, dimensions={0} | all-to-all | bytes 786432 | tf_op jit(solution)/shard_map/all_to_all | solution.py:234
  156.9 4.8 %all-to-all-start.1 = ((bf16[16,40,128]{2,1,0:T(8,128)(2,1)}), bf16[16,40,128]{2,1,0:T(8,128)(2,1)S(1)}, u32[]{:S(2)}, u32[]{:S(2)}) async-start(bf16[16,40,128]{2,1,0:T(8,128)(2,1)} %get-tuple-element.44), calls=%async_computation.1 | async-start | bytes 327680 | tf_op jit(solution)/shard_map/all_to_all | solution.py:234
  161.8 3.3 %collective-permute-start.15 = (bf16[8,72,192]{2,1,0:T(8,128)(2,1)S(1)}, bf16[8,72,192]{2,1,0:T(8,128)(2,1)S(1)}, u32[]{:S(2)}, u32[]{:S(2)}) collective-permute-start(bf16[8,72,192]{2,1,0:T(8,128)(2,1)S(1)} %copy-done.9), channel_id=1, source_target_pairs={{0,1},{1,0},{2,3},{3,2},{4,5},{5,4},{6,7},{7,6},{8,9},{9,8},{10,11... | collective-permute-start | bytes 663560 | tf_op jit(solution)/shard_map/ppermute | solution.py:230
  165.1 4.9 %all-to-all-done.1.att_ref = bf16[16,40,128]{2,1,0:T(8,128)(2,1)S(1)} async-done(((bf16[16,40,128]{2,1,0:T(8,128)(2,1)}), bf16[16,40,128]{2,1,0:T(8,128)(2,1)S(1)}, u32[]{:S(2)}, u32[]{:S(2)}) %all-to-all-start.1) | async-done | bytes 163872 | tf_op jit(solution)/shard_map/all_to_all | solution.py:234
  170.8 6.3 %all-to-all-start.3 = ((bf16[32,48,128]{2,1,0:T(8,128)(2,1)}), bf16[32,48,128]{2,1,0:T(8,128)(2,1)S(1)}, u32[]{:S(2)}, u32[]{:S(2)}) async-start(bf16[32,48,128]{2,1,0:T(8,128)(2,1)} %broadcast_in_dim.12), calls=%async_computation.3 | async-start | bytes 786432 | tf_op jit(solution)/shard_map/all_to_all | solution.py:234
  178.4 2.8 %shard_map.90 = (bf16[72,1024]{1,0:T(8,128)(2,1)}, bf16[72,1024]{1,0:T(8,128)(2,1)}, bf16[72,1024]{1,0:T(8,128)(2,1)}, bf16[72,1024]{1,0:T(8,128)(2,1)}, bf16[72...) custom-call(s32[8]{0:T(128)} %and_select_fusion.table_ref, ...), custom_call_target="tpu_custom_call" | custom-call | flops 452984832 | tf_op jit(solution)/shard_map/pallas_call | solution.py:318
  183.7 4.1 %collective-permute-start.17 = (bf16[72,1024]{1,0:T(8,128)(2,1)}, bf16[72,1024]{1,0:T(8,128)(2,1)S(1)}, u32[]{:S(2)}, u32[]{:S(2)}) collective-permute-start(bf16[72,1024]{1,0:T(8,128)(2,1)} %get-tuple-element.52), channel_id=1, source_target_pairs={{0,6},{2,8},{4,10},{6,12},{8,14},{10,0},{12,2},{14,4},{1,7},{3,9},... | collective-permute-start | bytes 442376 | tf_op jit(solution)/shard_map/ppermute | solution.py:230
  187.8 4.1 %collective-permute-start.18 = (bf16[72,1024]{1,0:T(8,128)(2,1)}, bf16[72,1024]{1,0:T(8,128)(2,1)S(1)}, u32[]{:S(2)}, u32[]{:S(2)}) collective-permute-start(bf16[72,1024]{1,0:T(8,128)(2,1)} %get-tuple-element.53), channel_id=1, source_target_pairs={{0,10},{2,12},{4,14},{6,0},{8,2},{10,4},{12,6},{14,8},{1,11},{3,13... | collective-permute-start | bytes 442376 | tf_op jit(solution)/shard_map/ppermute | solution.py:230
  192.0 3.7 %collective-permute-start.19 = (bf16[72,1024]{1,0:T(8,128)(2,1)}, bf16[72,1024]{1,0:T(8,128)(2,1)S(1)}, u32[]{:S(2)}, u32[]{:S(2)}) collective-permute-start(bf16[72,1024]{1,0:T(8,128)(2,1)} %get-tuple-element.54), channel_id=1, source_target_pairs={{0,4},{2,6},{4,8},{6,10},{8,12},{10,14},{12,0},{14,2},{1,5},{3,7},... | collective-permute-start | bytes 442376 | tf_op jit(solution)/shard_map/ppermute | solution.py:230
  195.7 3.7 %collective-permute-start.20 = (bf16[72,1024]{1,0:T(8,128)(2,1)}, bf16[72,1024]{1,0:T(8,128)(2,1)S(1)}, u32[]{:S(2)}, u32[]{:S(2)}) collective-permute-start(bf16[72,1024]{1,0:T(8,128)(2,1)} %get-tuple-element.55), channel_id=1, source_target_pairs={{0,12},{2,14},{4,0},{6,2},{8,4},{10,6},{12,8},{14,10},{1,13},{3,15... | collective-permute-start | bytes 442376 | tf_op jit(solution)/shard_map/ppermute | solution.py:230
  199.4 2.9 %collective-permute-start.21 = (bf16[72,1024]{1,0:T(8,128)(2,1)}, bf16[72,1024]{1,0:T(8,128)(2,1)S(1)}, u32[]{:S(2)}, u32[]{:S(2)}) collective-permute-start(bf16[72,1024]{1,0:T(8,128)(2,1)} %get-tuple-element.56), channel_id=1, source_target_pairs={{0,2},{2,4},{4,6},{6,8},{8,10},{10,12},{12,14},{14,0},{1,3},{3,5},... | collective-permute-start | bytes 442376 | tf_op jit(solution)/shard_map/ppermute | solution.py:230
  202.4 3.4 %collective-permute-done.17 = bf16[72,1024]{1,0:T(8,128)(2,1)S(1)} collective-permute-done((bf16[72,1024]{1,0:T(8,128)(2,1)}, bf16[72,1024]{1,0:T(8,128)(2,1)S(1)}, u32[]{:S(2)}, u32[]{:S(2)}) %collective-permute-start.17) | collective-permute-done | bytes 147488 | tf_op jit(solution)/shard_map/ppermute | solution.py:230
  207.7 3.0 %shard_map.88 = bf16[72,1024]{1,0:T(8,128)(2,1)} custom-call(bf16[16,40,128]{2,1,0:T(8,128)(2,1)} %copy-done.2, bf16[1024,1024]{1,0:T(8,128)(2,1)} %bitcast.23), custom_call_target="tpu_custom_call" | custom-call | flops 150994944 | tf_op jit(solution)/shard_map/pallas_call | solution.py:328
  210.7 2.7 %collective-permute-done.21 = bf16[72,1024]{1,0:T(8,128)(2,1)S(1)} collective-permute-done((bf16[72,1024]{1,0:T(8,128)(2,1)}, bf16[72,1024]{1,0:T(8,128)(2,1)S(1)}, u32[]{:S(2)}, u32[]{:S(2)}) %collective-permute-start.21) | collective-permute-done | bytes 147488 | tf_op jit(solution)/shard_map/ppermute | solution.py:230
  (79 shorter events, 29.8 us)
Async XLA Ops:
  0.6 28.2 %collective-permute-start.3 = (bf16[72,1024]{1,0:T(8,128)(2,1)}, bf16[72,1024]{1,0:T(8,128)(2,1)S(1)}, u32[]{:S(2)}, u32[]{:S(2)}) collective-permute-start(bf16[72,1024]{1,0:T(8,128)(2,1)} %bitcast.32), channel_id=1, source_target_pairs={{0,12},{2,14},{4,0},{6,2},{8,4},{10,6},{12,8},{14,10},{1,13},{3,15... | collective-permute-start | bytes 442376 | tf_op jit(solution)/shard_map/ppermute | solution.py:230
  12.1 14.7 %collective-permute-start.2 = (bf16[72,1024]{1,0:T(8,128)(2,1)}, bf16[72,1024]{1,0:T(8,128)(2,1)S(1)}, u32[]{:S(2)}, u32[]{:S(2)}) collective-permute-start(bf16[72,1024]{1,0:T(8,128)(2,1)} %bitcast.33), channel_id=1, source_target_pairs={{0,4},{2,6},{4,8},{6,10},{8,12},{10,14},{12,0},{14,2},{1,5},{3,7},... | collective-permute-start | bytes 442376 | tf_op jit(solution)/shard_map/ppermute | solution.py:230
  14.0 21.3 %collective-permute-start.1 = (bf16[72,1024]{1,0:T(8,128)(2,1)}, bf16[72,1024]{1,0:T(8,128)(2,1)S(1)}, u32[]{:S(2)}, u32[]{:S(2)}) collective-permute-start(bf16[72,1024]{1,0:T(8,128)(2,1)} %bitcast.34), channel_id=1, source_target_pairs={{0,14},{2,0},{4,2},{6,4},{8,6},{10,8},{12,10},{14,12},{1,15},{3,1}... | collective-permute-start | bytes 442376 | tf_op jit(solution)/shard_map/ppermute | solution.py:230
  19.5 11.7 %collective-permute-start = (bf16[72,1024]{1,0:T(8,128)(2,1)}, bf16[72,1024]{1,0:T(8,128)(2,1)S(1)}, u32[]{:S(2)}, u32[]{:S(2)}) collective-permute-start(bf16[72,1024]{1,0:T(8,128)(2,1)} %bitcast.35), channel_id=1, source_target_pairs={{0,2},{2,4},{4,6},{6,8},{8,10},{10,12},{12,14},{14,0},{1,3},{3,5},... | collective-permute-start | bytes 442376 | tf_op jit(solution)/shard_map/ppermute | solution.py:230
  21.5 19.5 %collective-permute-start.7 = (bf16[192,1024]{1,0:T(8,128)(2,1)}, bf16[192,1024]{1,0:T(8,128)(2,1)S(1)}, u32[]{:S(2)}, u32[]{:S(2)}) collective-permute-start(bf16[192,1024]{1,0:T(8,128)(2,1)} %bitcast.27), channel_id=1, source_target_pairs={{0,1},{1,0},{2,3},{3,2},{4,5},{5,4},{6,7},{7,6},{8,9},{9,8},{10,11... | collective-permute-start | bytes 1179656 | tf_op jit(solution)/shard_map/ppermute | solution.py:230
  26.9 14.1 %collective-permute-start.6 = (bf16[72,1024]{1,0:T(8,128)(2,1)S(1)}, bf16[72,1024]{1,0:T(8,128)(2,1)S(1)}, u32[]{:S(2)}, u32[]{:S(2)}) collective-permute-start(bf16[72,1024]{1,0:T(8,128)(2,1)S(1)} %collective-permute-done.2), channel_id=1, source_target_pairs={{0,4},{2,6},{4,8},{6,10},{8,12},{10,14},{12,0},{14,2},{1,5},{3,7},... | collective-permute-start | bytes 442376 | tf_op jit(solution)/shard_map/ppermute | solution.py:230
  28.8 12.1 %collective-permute-start.4 = (bf16[72,1024]{1,0:T(8,128)(2,1)S(1)}, bf16[72,1024]{1,0:T(8,128)(2,1)S(1)}, u32[]{:S(2)}, u32[]{:S(2)}) collective-permute-start(bf16[72,1024]{1,0:T(8,128)(2,1)S(1)} %collective-permute-done.2), channel_id=1, source_target_pairs={{0,2},{2,4},{4,6},{6,8},{8,10},{10,12},{12,14},{14,0},{1,3},{3,5},... | collective-permute-start | bytes 442376 | tf_op jit(solution)/shard_map/ppermute | solution.py:230
  31.3 9.6 %collective-permute-start.5 = (bf16[72,1024]{1,0:T(8,128)(2,1)S(1)}, bf16[72,1024]{1,0:T(8,128)(2,1)S(1)}, u32[]{:S(2)}, u32[]{:S(2)}) collective-permute-start(bf16[72,1024]{1,0:T(8,128)(2,1)S(1)} %collective-permute-done.3), channel_id=1, source_target_pairs={{0,14},{2,0},{4,2},{6,4},{8,6},{10,8},{12,10},{14,12},{1,15},{3,1}... | collective-permute-start | bytes 442376 | tf_op jit(solution)/shard_map/ppermute | solution.py:230
  45.3 25.6 %collective-permute-start.12 = (bf16[8,72,192]{2,1,0:T(8,128)(2,1)}, bf16[8,72,192]{2,1,0:T(8,128)(2,1)S(1)}, u32[]{:S(2)}, u32[]{:S(2)}) collective-permute-start(bf16[8,72,192]{2,1,0:T(8,128)(2,1)} %get-tuple-element.38), channel_id=1, source_target_pairs={{0,1},{1,0},{2,3},{3,2},{4,5},{5,4},{6,7},{7,6},{8,9},{9,8},{10,11... | collective-permute-start | bytes 663560 | tf_op jit(solution)/shard_map/ppermute | solution.py:230
  47.4 15.4 %collective-permute-start.8 = (bf16[4,72,128]{2,1,0:T(8,128)(2,1)}, bf16[4,72,128]{2,1,0:T(8,128)(2,1)S(1)}, u32[]{:S(2)}, u32[]{:S(2)}) collective-permute-start(bf16[4,72,128]{2,1,0:T(8,128)(2,1)} %get-tuple-element.34), channel_id=1, source_target_pairs={{0,496},{16,0},{32,16},{48,32},{64,48},{80,64},{96,80},{112,96},{1... | collective-permute-start | bytes 221192 | tf_op jit(solution)/shard_map/ppermute | solution.py:230
  51.2 11.5 %collective-permute-start.9 = (bf16[4,72,128]{2,1,0:T(8,128)(2,1)}, bf16[4,72,128]{2,1,0:T(8,128)(2,1)S(1)}, u32[]{:S(2)}, u32[]{:S(2)}) collective-permute-start(bf16[4,72,128]{2,1,0:T(8,128)(2,1)} %get-tuple-element.35), channel_id=1, source_target_pairs={{0,16},{16,32},{32,48},{48,64},{64,80},{80,96},{96,112},{112,128},... | collective-permute-start | bytes 221192 | tf_op jit(solution)/shard_map/ppermute | solution.py:230
  55.4 8.4 %collective-permute-start.10 = (bf16[4,72,128]{2,1,0:T(8,128)(2,1)}, bf16[4,72,128]{2,1,0:T(8,128)(2,1)S(1)}, u32[]{:S(2)}, u32[]{:S(2)}) collective-permute-start(bf16[4,72,128]{2,1,0:T(8,128)(2,1)} %get-tuple-element.36), channel_id=1, source_target_pairs={{0,497},{1,496},{16,1},{17,0},{32,17},{33,16},{48,33},{49,32},{64,... | collective-permute-start | bytes 221192 | tf_op jit(solution)/shard_map/ppermute | solution.py:267
  60.0 10.9 %collective-permute-start.11 = (bf16[4,72,128]{2,1,0:T(8,128)(2,1)}, bf16[4,72,128]{2,1,0:T(8,128)(2,1)S(1)}, u32[]{:S(2)}, u32[]{:S(2)}) collective-permute-start(bf16[4,72,128]{2,1,0:T(8,128)(2,1)} %get-tuple-element.37), channel_id=1, source_target_pairs={{0,17},{1,16},{16,33},{17,32},{32,49},{33,48},{48,65},{49,64},{64,... | collective-permute-start | bytes 221192 | tf_op jit(solution)/shard_map/ppermute | solution.py:268
  62.7 13.3 %copy-start.11 = (bf16[4,72,128]{2,1,0:T(8,128)(2,1)}, bf16[4,72,128]{2,1,0:T(8,128)(2,1)S(1)}, u32[]{:S(2)}) copy-start(bf16[4,72,128]{2,1,0:T(8,128)(2,1)S(1)} %collective-permute-done.8.from_e_ref) | copy-start | bytes 221188
  62.8 13.3 %copy-start.12 = (bf16[4,72,128]{2,1,0:T(8,128)(2,1)}, bf16[4,72,128]{2,1,0:T(8,128)(2,1)S(1)}, u32[]{:S(2)}) copy-start(bf16[4,72,128]{2,1,0:T(8,128)(2,1)S(1)} %collective-permute-done.9.from_w_ref) | copy-start | bytes 221188
  63.7 12.3 %copy-start.13 = (bf16[4,72,128]{2,1,0:T(8,128)(2,1)}, bf16[4,72,128]{2,1,0:T(8,128)(2,1)S(1)}, u32[]{:S(2)}) copy-start(bf16[4,72,128]{2,1,0:T(8,128)(2,1)S(1)} %collective-permute-done.10.from_e2_ref) | copy-start | bytes 221188
  70.9 51.0 %collective-permute-start.23 = (bf16[576,1024]{1,0:T(8,128)(2,1)}, bf16[576,1024]{1,0:T(8,128)(2,1)S(1)}, u32[]{:S(2)}, u32[]{:S(2)}) collective-permute-start(bf16[576,1024]{1,0:T(8,128)(2,1)} %copy-done), channel_id=1, source_target_pairs={{0,1},{1,0},{2,3},{3,2},{4,5},{5,4},{6,7},{7,6},{8,9},{9,8},{10,11... | collective-permute-start | bytes 3538952 | tf_op jit(solution)/shard_map/ppermute | solution.py:230
  97.5 19.1 %copy-start.7 = (s32[8]{0:T(128)S(1)}, s32[8]{0:T(128)}, u32[]{:S(2)}) copy-start(s32[8]{0:T(128)} %get-tuple-element.62.table_ref) | copy-start | bytes 100
  105.8 11.5 %collective-permute-start.13 = (bf16[8,72,128]{2,1,0:T(8,128)(2,1)}, bf16[8,72,128]{2,1,0:T(8,128)(2,1)S(1)}, u32[]{:S(2)}, u32[]{:S(2)}) collective-permute-start(bf16[8,72,128]{2,1,0:T(8,128)(2,1)} %get-tuple-element.47), channel_id=1, source_target_pairs={{0,16},{16,32},{32,48},{48,64},{64,80},{80,96},{96,112},{112,128},... | collective-permute-start | bytes 442376 | tf_op jit(solution)/shard_map/ppermute | solution.py:230
  111.1 7.6 %collective-permute-start.14 = (bf16[8,72,128]{2,1,0:T(8,128)(2,1)}, bf16[8,72,128]{2,1,0:T(8,128)(2,1)S(1)}, u32[]{:S(2)}, u32[]{:S(2)}) collective-permute-start(bf16[8,72,128]{2,1,0:T(8,128)(2,1)} %get-tuple-element.48), channel_id=1, source_target_pairs={{0,496},{16,0},{32,16},{48,32},{64,48},{80,64},{96,80},{112,96},{1... | collective-permute-start | bytes 442376 | tf_op jit(solution)/shard_map/ppermute | solution.py:230
  122.9 38.9 %copy-start.9 = (bf16[8,72,192]{2,1,0:T(8,128)(2,1)S(1)}, bf16[8,72,192]{2,1,0:T(8,128)(2,1)}, u32[]{:S(2)}) copy-start(bf16[8,72,192]{2,1,0:T(8,128)(2,1)} %get-tuple-element.50) | copy-start | bytes 663556
  126.5 50.6 %copy-start.15 = (s32[8]{0:T(128)S(1)}, s32[8]{0:T(128)}, u32[]{:S(2)}) copy-start(s32[8]{0:T(128)} %constant.40.clone) | copy-start | bytes 100
  156.9 13.1 %all-to-all-start.1 = ((bf16[16,40,128]{2,1,0:T(8,128)(2,1)}), bf16[16,40,128]{2,1,0:T(8,128)(2,1)S(1)}, u32[]{:S(2)}, u32[]{:S(2)}) async-start(bf16[16,40,128]{2,1,0:T(8,128)(2,1)} %get-tuple-element.44), calls=%async_computation.1 | async-start | bytes 327680 | tf_op jit(solution)/shard_map/all_to_all | solution.py:234
  161.8 15.9 %collective-permute-start.15 = (bf16[8,72,192]{2,1,0:T(8,128)(2,1)S(1)}, bf16[8,72,192]{2,1,0:T(8,128)(2,1)S(1)}, u32[]{:S(2)}, u32[]{:S(2)}) collective-permute-start(bf16[8,72,192]{2,1,0:T(8,128)(2,1)S(1)} %copy-done.9), channel_id=1, source_target_pairs={{0,1},{1,0},{2,3},{3,2},{4,5},{5,4},{6,7},{7,6},{8,9},{9,8},{10,11... | collective-permute-start | bytes 663560 | tf_op jit(solution)/shard_map/ppermute | solution.py:230
  170.8 44.2 %all-to-all-start.3 = ((bf16[32,48,128]{2,1,0:T(8,128)(2,1)}), bf16[32,48,128]{2,1,0:T(8,128)(2,1)S(1)}, u32[]{:S(2)}, u32[]{:S(2)}) async-start(bf16[32,48,128]{2,1,0:T(8,128)(2,1)} %broadcast_in_dim.12), calls=%async_computation.3 | async-start | bytes 786432 | tf_op jit(solution)/shard_map/all_to_all | solution.py:234
  181.2 18.2 %collective-permute-start.16 = (bf16[72,1024]{1,0:T(8,128)(2,1)}, bf16[72,1024]{1,0:T(8,128)(2,1)S(1)}, u32[]{:S(2)}, u32[]{:S(2)}) collective-permute-start(bf16[72,1024]{1,0:T(8,128)(2,1)} %get-tuple-element.51), channel_id=1, source_target_pairs={{0,8},{2,10},{4,12},{6,14},{8,0},{10,2},{12,4},{14,6},{1,9},{3,11}... | collective-permute-start | bytes 442376 | tf_op jit(solution)/shard_map/ppermute | solution.py:230
  183.7 22.0 %collective-permute-start.17 = (bf16[72,1024]{1,0:T(8,128)(2,1)}, bf16[72,1024]{1,0:T(8,128)(2,1)S(1)}, u32[]{:S(2)}, u32[]{:S(2)}) collective-permute-start(bf16[72,1024]{1,0:T(8,128)(2,1)} %get-tuple-element.52), channel_id=1, source_target_pairs={{0,6},{2,8},{4,10},{6,12},{8,14},{10,0},{12,2},{14,4},{1,7},{3,9},... | collective-permute-start | bytes 442376 | tf_op jit(solution)/shard_map/ppermute | solution.py:230
  187.8 22.8 %collective-permute-start.18 = (bf16[72,1024]{1,0:T(8,128)(2,1)}, bf16[72,1024]{1,0:T(8,128)(2,1)S(1)}, u32[]{:S(2)}, u32[]{:S(2)}) collective-permute-start(bf16[72,1024]{1,0:T(8,128)(2,1)} %get-tuple-element.53), channel_id=1, source_target_pairs={{0,10},{2,12},{4,14},{6,0},{8,2},{10,4},{12,6},{14,8},{1,11},{3,13... | collective-permute-start | bytes 442376 | tf_op jit(solution)/shard_map/ppermute | solution.py:230
  192.0 18.7 %collective-permute-start.19 = (bf16[72,1024]{1,0:T(8,128)(2,1)}, bf16[72,1024]{1,0:T(8,128)(2,1)S(1)}, u32[]{:S(2)}, u32[]{:S(2)}) collective-permute-start(bf16[72,1024]{1,0:T(8,128)(2,1)} %get-tuple-element.54), channel_id=1, source_target_pairs={{0,4},{2,6},{4,8},{6,10},{8,12},{10,14},{12,0},{14,2},{1,5},{3,7},... | collective-permute-start | bytes 442376 | tf_op jit(solution)/shard_map/ppermute | solution.py:230
  195.7 15.1 %collective-permute-start.20 = (bf16[72,1024]{1,0:T(8,128)(2,1)}, bf16[72,1024]{1,0:T(8,128)(2,1)S(1)}, u32[]{:S(2)}, u32[]{:S(2)}) collective-permute-start(bf16[72,1024]{1,0:T(8,128)(2,1)} %get-tuple-element.55), channel_id=1, source_target_pairs={{0,12},{2,14},{4,0},{6,2},{8,4},{10,6},{12,8},{14,10},{1,13},{3,15... | collective-permute-start | bytes 442376 | tf_op jit(solution)/shard_map/ppermute | solution.py:230
  199.4 14.0 %collective-permute-start.21 = (bf16[72,1024]{1,0:T(8,128)(2,1)}, bf16[72,1024]{1,0:T(8,128)(2,1)S(1)}, u32[]{:S(2)}, u32[]{:S(2)}) collective-permute-start(bf16[72,1024]{1,0:T(8,128)(2,1)} %get-tuple-element.56), channel_id=1, source_target_pairs={{0,2},{2,4},{4,6},{6,8},{8,10},{10,12},{12,14},{14,0},{1,3},{3,5},... | collective-permute-start | bytes 442376 | tf_op jit(solution)/shard_map/ppermute | solution.py:230
  205.7 8.4 %collective-permute-start.22 = (bf16[72,1024]{1,0:T(8,128)(2,1)}, bf16[72,1024]{1,0:T(8,128)(2,1)S(1)}, u32[]{:S(2)}, u32[]{:S(2)}) collective-permute-start(bf16[72,1024]{1,0:T(8,128)(2,1)} %get-tuple-element.57), channel_id=1, source_target_pairs={{0,14},{2,0},{4,2},{6,4},{8,6},{10,8},{12,10},{14,12},{1,15},{3,1}... | collective-permute-start | bytes 442376 | tf_op jit(solution)/shard_map/ppermute | solution.py:230
  (10 other events, 34.1 us)
where the time goes:
time: 218 us; the launch traced here: 216 us
  starting transfers between devices  99.9 us (46%)
  blocking collectives  51.8 us (24%)
  waiting for transfers between devices  26.7 us (12%)
  Pallas kernels  26.7 us (12%)
  local copies, waits for them, and re-layouts  6.65 us (3%)
  other arithmetic  3.45 us (2%)
    ppermute x22, starting transfers between devices, shift(): lax.ppermute(value, axis, [(i, (i + distance) % size) for i in range(size)])  81.4 us
    all_to_all x2, blocking collectives, exchange(): return lax.all_to_all(value, axis, 0, 0, tiled=True)  51.8 us
    ppermute x22, waiting for transfers between devices, shift(): lax.ppermute(value, axis, [(i, (i + distance) % size) for i in range(size)])  13.7 us
    all_to_all x2, starting transfers between devices, exchange(): return lax.all_to_all(value, axis, 0, 0, tiled=True)  11.1 us
    pallas_call x1, Pallas kernels, step(): call(attend_kernel, [((RANKS, 40, 128), BF16), ((RANKS, TOK, HD), F32), (...  8.29 us
    ppermute x1, waiting for transfers between devices, step(): from_w2 = lax.ppermute(to_e2, LON + ('yl',), across(1))  7.13 us
    unnamed x40, local copies, waits for them, and re-layouts  5.6 us
    all_to_all x2, waiting for transfers between devices, exchange(): return lax.all_to_all(value, axis, 0, 0, tiled=True)  4.89 us
  transfers between devices with their start and end apart: 26, of which 8 were waited for; matrix products, arithmetic and copies ran while one was open for 2% of the time, Pallas kernels for 9%

commit v1 on v0

--- a/solution.py
+++ b/solution.py
@@ -267,10 +267,7 @@
     from_e2 = lax.ppermute(to_w2, LON + ("yl",), across(-1))
     from_w2 = lax.ppermute(to_e2, LON + ("yl",), across(1))
     swapped = shift(swap, "yl", 2, 1)
-    late, from_e, from_w, from_e2, from_w2, swapped = lax.optimization_barrier(
-        (tokens, from_e, from_w, from_e2, from_w2, swapped)
-    )
-    tokens2 = shift(late, "yl", 2, 1)
+    tokens2 = shift(tokens, "yl", 2, 1)
     attended, dq, dkv, grad_east, grad_west = call(
         attend_kernel,
         [

time: 218 us -> 221 us (1.014)
  blocking collectives: 51.8 us -> 28.4 us
  waiting for transfers between devices: 26.7 us -> 41.8 us
  starting transfers between devices: 99.9 us -> 112 us
    all_to_all x2 -> x1, blocking collectives: 51.8 us -> 28.4 us  [exchange(): return lax.all_to_all(value, axis, 0, 0, tiled=True)]
    ppermute x22, waiting for transfers between devices: 13.7 us -> 32.5 us  [shift(): lax.ppermute(value, axis, [(i, (i + distance) % size) for i in range(size)])]
    all_to_all x2 -> x3, starting transfers between devices: 11.1 us -> 22.6 us  [exchange(): return lax.all_to_all(value, axis, 0, 0, tiled=True)]
    ppermute x1, waiting for transfers between devices: 7.13 us -> 3.8 us  [step(): from_w2 = lax.ppermute(to_e2, LON + ('yl',), across(1))]
    ppermute x1, starting transfers between devices: 4.61 us -> 1.92 us  [step(): from_e2 = lax.ppermute(to_w2, LON + ('yl',), across(-1))]
    ppermute x1, starting transfers between devices: 2.75 us -> 5.44 us  [step(): from_w2 = lax.ppermute(to_e2, LON + ('yl',), across(1))]
    unnamed x40 -> x46, local copies, waits for them, and re-layouts: 5.6 us -> 5.96 us
    all_to_all x2 -> x3, waiting for transfers between devices: 4.89 us -> 4.9 us  [exchange(): return lax.all_to_all(value, axis, 0, 0, tiled=True)]
  transfers between devices with their start and end apart: 26 -> 27, of which waited for: 8 -> 9; matrix products, arithmetic and copies ran while one was open for 2% -> 2% of each run, Pallas kernels for 9% -> 11%
where the time goes in v1:
time: 221 us; the launch traced here: 220 us
  starting transfers between devices  112 us (51%)
  waiting for transfers between devices  41.8 us (19%)
  blocking collectives  28.4 us (13%)
  Pallas kernels  26.7 us (12%)
  local copies, waits for them, and re-layouts  7.02 us (3%)
  other arithmetic  2.7 us (1%)
    ppermute x22, starting transfers between devices, shift(): lax.ppermute(value, axis, [(i, (i + distance) % size) for i in range(size)])  81.9 us
    ppermute x22, waiting for transfers between devices, shift(): lax.ppermute(value, axis, [(i, (i + distance) % size) for i in range(size)])  32.5 us
    all_to_all x1, blocking collectives, exchange(): return lax.all_to_all(value, axis, 0, 0, tiled=True)  28.4 us
    all_to_all x3, starting transfers between devices, exchange(): return lax.all_to_all(value, axis, 0, 0, tiled=True)  22.6 us
    pallas_call x1, Pallas kernels, step(): call(attend_kernel, [((RANKS, 40, 128), BF16), ((RANKS, TOK, HD), F32), (...  8.29 us
    unnamed x46, local copies, waits for them, and re-layouts  5.96 us
    ppermute x1, starting transfers between devices, step(): from_w2 = lax.ppermute(to_e2, LON + ('yl',), across(1))  5.44 us
    all_to_all x3, waiting for transfers between devices, exchange(): return lax.all_to_all(value, axis, 0, 0, tiled=True)  4.9 us
  transfers between devices with their start and end apart: 27, of which 9 were waited for; matrix products, arithmetic and copies ran while one was open for 2% of the time, Pallas kernels for 11%

profile of v1, /device:TPU:1, one launch (start us, length us, event | category | flops | bytes accessed | tf_op | source)
XLA Modules:
  0.0 219.7 jit_solution(6340940483397373891)
XLA Ops:
  0.6 6.8 %collective-permute-start.2 = (bf16[72,1024]{1,0:T(8,128)(2,1)}, bf16[72,1024]{1,0:T(8,128)(2,1)S(1)}, u32[]{:S(2)}, u32[]{:S(2)}) collective-permute-start(bf16[72,1024]{1,0:T(8,128)(2,1)} %bitcast.32), channel_id=1, source_target_pairs={{0,4},{2,6},{4,8},{6,10},{8,12},{10,14},{12,0},{14,2},{1,5},{3,7},... | collective-permute-start | bytes 442376 | tf_op jit(solution)/shard_map/ppermute | solution.py:230
  7.4 6.8 %collective-permute-start.3 = (bf16[72,1024]{1,0:T(8,128)(2,1)}, bf16[72,1024]{1,0:T(8,128)(2,1)S(1)}, u32[]{:S(2)}, u32[]{:S(2)}) collective-permute-start(bf16[72,1024]{1,0:T(8,128)(2,1)} %bitcast.33), channel_id=1, source_target_pairs={{0,12},{2,14},{4,0},{6,2},{8,4},{10,6},{12,8},{14,10},{1,13},{3,15... | collective-permute-start | bytes 442376 | tf_op jit(solution)/shard_map/ppermute | solution.py:230
  14.2 3.1 %collective-permute-start = (bf16[72,1024]{1,0:T(8,128)(2,1)}, bf16[72,1024]{1,0:T(8,128)(2,1)S(1)}, u32[]{:S(2)}, u32[]{:S(2)}) collective-permute-start(bf16[72,1024]{1,0:T(8,128)(2,1)} %bitcast.34), channel_id=1, source_target_pairs={{0,2},{2,4},{4,6},{6,8},{8,10},{10,12},{12,14},{14,0},{1,3},{3,5},... | collective-permute-start | bytes 442376 | tf_op jit(solution)/shard_map/ppermute | solution.py:230
  17.3 3.4 %collective-permute-start.1 = (bf16[72,1024]{1,0:T(8,128)(2,1)}, bf16[72,1024]{1,0:T(8,128)(2,1)S(1)}, u32[]{:S(2)}, u32[]{:S(2)}) collective-permute-start(bf16[72,1024]{1,0:T(8,128)(2,1)} %bitcast.35), channel_id=1, source_target_pairs={{0,14},{2,0},{4,2},{6,4},{8,6},{10,8},{12,10},{14,12},{1,15},{3,1}... | collective-permute-start | bytes 442376 | tf_op jit(solution)/shard_map/ppermute | solution.py:230
  23.6 3.3 %collective-permute-start.4 = (bf16[72,1024]{1,0:T(8,128)(2,1)S(1)}, bf16[72,1024]{1,0:T(8,128)(2,1)S(1)}, u32[]{:S(2)}, u32[]{:S(2)}) collective-permute-start(bf16[72,1024]{1,0:T(8,128)(2,1)S(1)} %collective-permute-done.2), channel_id=1, source_target_pairs={{0,2},{2,4},{4,6},{6,8},{8,10},{10,12},{12,14},{14,0},{1,3},{3,5},... | collective-permute-start | bytes 442376 | tf_op jit(solution)/shard_map/ppermute | solution.py:230
  26.9 3.2 %collective-permute-start.5 = (bf16[72,1024]{1,0:T(8,128)(2,1)S(1)}, bf16[72,1024]{1,0:T(8,128)(2,1)S(1)}, u32[]{:S(2)}, u32[]{:S(2)}) collective-permute-start(bf16[72,1024]{1,0:T(8,128)(2,1)S(1)} %collective-permute-done.3), channel_id=1, source_target_pairs={{0,14},{2,0},{4,2},{6,4},{8,6},{10,8},{12,10},{14,12},{1,15},{3,1}... | collective-permute-start | bytes 442376 | tf_op jit(solution)/shard_map/ppermute | solution.py:230
  30.2 4.2 %collective-permute-done.4 = bf16[72,1024]{1,0:T(8,128)(2,1)S(1)} collective-permute-done((bf16[72,1024]{1,0:T(8,128)(2,1)S(1)}, bf16[72,1024]{1,0:T(8,128)(2,1)S(1)}, u32[]{:S(2)}, u32[]{:S(2)}) %collective-permute-start.4) | collective-permute-done | bytes 147488 | tf_op jit(solution)/shard_map/ppermute | solution.py:230
  34.5 3.3 %collective-permute-start.23 = (bf16[576,1024]{1,0:T(8,128)(2,1)S(1)}, bf16[576,1024]{1,0:T(8,128)(2,1)S(1)}, u32[]{:S(2)}, u32[]{:S(2)}) collective-permute-start(bf16[576,1024]{1,0:T(8,128)(2,1)S(1)} %constant_dynamic-update-slice_fusion.tokens_ref), channel_id=1, source_target_pairs={{0,1},{1,0},{2,3},{3,2},{4,5},{5,4},{6,7},{7,6},{8,9},{9,8},{10,11... | collective-permute-start | bytes 3538952 | tf_op jit(solution)/shard_map/ppermute | solution.py:230
  39.8 3.3 %shard_map.86 = bf16[16,40,128]{2,1,0:T(8,128)(2,1)} custom-call(bf16[72,1024]{1,0:T(8,128)(2,1)} %bitcast.30, bf16[16,64,1024]{2,1,0:T(8,128)(2,1)} %weight_ref.1), custom_call_target="tpu_custom_call" | custom-call | flops 150994944 | tf_op jit(solution)/shard_map/pallas_call | solution.py:251
  43.1 6.7 %all-to-all-start = ((bf16[16,40,128]{2,1,0:T(8,128)(2,1)}), bf16[16,40,128]{2,1,0:T(8,128)(2,1)S(1)}, u32[]{:S(2)}, u32[]{:S(2)}) async-start(bf16[16,40,128]{2,1,0:T(8,128)(2,1)} %shard_map.86), calls=%async_computation | async-start | bytes 327680 | tf_op jit(solution)/shard_map/all_to_all | solution.py:234
  50.4 19.1 %collective-permute-done.7.other_ref = bf16[192,1024]{1,0:T(8,128)(2,1)S(1)} collective-permute-done((bf16[192,1024]{1,0:T(8,128)(2,1)S(1)}, bf16[192,1024]{1,0:T(8,128)(2,1)S(1)}, u32[]{:S(2)}, u32[]{:S(2)}) %collective-permute-start.7) | collective-permute-done | bytes 393248 | tf_op jit(solution)/shard_map/ppermute | solution.py:230
  70.3 3.1 %shard_map.85 = (bf16[8,72,128]{2,1,0:T(8,128)(2,1)}, bf16[8,72,64]{2,1,0:T(8,128)(2,1)}, bf16[8,72,192]{2,1,0:T(8,128)(2,1)}, bf16[4,72,128]{2,1,0:T(8,128)(2,1...) custom-call(s32[8]{0:T(128)} %get-tuple-element.50.table_ref, ...), custom_call_target="tpu_custom_call" | custom-call | flops 452984832 | tf_op jit(solution)/shard_map/pallas_call | solution.py:256
  73.4 3.4 %collective-permute-start.8 = (bf16[8,72,192]{2,1,0:T(8,128)(2,1)}, bf16[8,72,192]{2,1,0:T(8,128)(2,1)S(1)}, u32[]{:S(2)}, u32[]{:S(2)}) collective-permute-start(bf16[8,72,192]{2,1,0:T(8,128)(2,1)} %get-tuple-element.28), channel_id=1, source_target_pairs={{0,1},{1,0},{2,3},{3,2},{4,5},{5,4},{6,7},{7,6},{8,9},{9,8},{10,11... | collective-permute-start | bytes 663560 | tf_op jit(solution)/shard_map/ppermute | solution.py:230
  76.8 6.6 %collective-permute-start.9 = (bf16[4,72,128]{2,1,0:T(8,128)(2,1)}, bf16[4,72,128]{2,1,0:T(8,128)(2,1)S(1)}, u32[]{:S(2)}, u32[]{:S(2)}) collective-permute-start(bf16[4,72,128]{2,1,0:T(8,128)(2,1)} %get-tuple-element.29), channel_id=1, source_target_pairs={{0,496},{16,0},{32,16},{48,32},{64,48},{80,64},{96,80},{112,96},{1... | collective-permute-start | bytes 221192 | tf_op jit(solution)/shard_map/ppermute | solution.py:230
  83.5 4.1 %collective-permute-start.10 = (bf16[4,72,128]{2,1,0:T(8,128)(2,1)}, bf16[4,72,128]{2,1,0:T(8,128)(2,1)S(1)}, u32[]{:S(2)}, u32[]{:S(2)}) collective-permute-start(bf16[4,72,128]{2,1,0:T(8,128)(2,1)} %get-tuple-element.30), channel_id=1, source_target_pairs={{0,16},{16,32},{32,48},{48,64},{64,80},{80,96},{96,112},{112,128},... | collective-permute-start | bytes 221192 | tf_op jit(solution)/shard_map/ppermute | solution.py:230
  89.6 5.4 %collective-permute-start.12 = (bf16[4,72,128]{2,1,0:T(8,128)(2,1)}, bf16[4,72,128]{2,1,0:T(8,128)(2,1)S(1)}, u32[]{:S(2)}, u32[]{:S(2)}) collective-permute-start(bf16[4,72,128]{2,1,0:T(8,128)(2,1)} %get-tuple-element.32), channel_id=1, source_target_pairs={{0,17},{1,16},{16,33},{17,32},{32,49},{33,48},{48,65},{49,64},{64,... | collective-permute-start | bytes 221192 | tf_op jit(solution)/shard_map/ppermute | solution.py:268
  95.7 3.8 %collective-permute-done.12.from_w2_ref = bf16[4,72,128]{2,1,0:T(8,128)(2,1)S(1)} collective-permute-done((bf16[4,72,128]{2,1,0:T(8,128)(2,1)}, bf16[4,72,128]{2,1,0:T(8,128)(2,1)S(1)}, u32[]{:S(2)}, u32[]{:S(2)}) %collective-permute-start.12) | collective-permute-done | bytes 73760 | tf_op jit(solution)/shard_map/ppermute | solution.py:268
  100.2 8.3 %shard_map.87 = (bf16[16,40,128]{2,1,0:T(8,128)(2,1)}, f32[16,72,64]{2,1,0:T(8,128)}, f32[16,72,128]{2,1,0:T(8,128)}, bf16[8,72,128]{2,1,0:T(8,128)(2,1)}, bf16[8,72,128]{2,1,0:T(8,128)(2,1)}) custom-call(s32[1]{0:T(128)} %bitcast.place_ref, bf16[8,72,128]{2,1,0:T(8,128)(2,1)} %get-tuple-element.26.kv_ref, bf16[8,72,64]{2,1,0:T(8,128)(2,1)} %get-tuple-element.27.q_ref, ...), custom_call_target="tpu_custom_call" | custom-call | flops 1019215872 | tf_op jit(solution)/shard_map/pallas_call | solution.py:271
  110.4 5.8 %collective-permute-start.14 = (bf16[8,72,128]{2,1,0:T(8,128)(2,1)}, bf16[8,72,128]{2,1,0:T(8,128)(2,1)S(1)}, u32[]{:S(2)}, u32[]{:S(2)}) collective-permute-start(bf16[8,72,128]{2,1,0:T(8,128)(2,1)} %get-tuple-element.37), channel_id=1, source_target_pairs={{0,496},{16,0},{32,16},{48,32},{64,48},{80,64},{96,80},{112,96},{1... | collective-permute-start | bytes 442376 | tf_op jit(solution)/shard_map/ppermute | solution.py:230
  123.8 3.6 %shard_map.91 = bf16[32,48,128]{2,1,0:T(8,128)(2,1)} custom-call(s32[16]{0:T(128)} %pad_add_fusion.table_ref, bf16[576,1024]{1,0:T(8,128)(2,1)} %copy-done, bf16[576,1024]{1,0:T(8,128)(2,1)} %copy-done.1, bf16[16,72,192]{2,1,0:T(8,128)(2,1)} %get-tuple-element.48.pg_ref), custom_call_target="tpu_custom_call" | custom-call | flops 452984832 | tf_op jit(solution)/shard_map/pallas_call | solution.py:303
  127.4 28.4 %all_to_all.20 = bf16[32,48,128]{2,1,0:T(8,128)(2,1)S(1)} all-to-all(bf16[32,48,128]{2,1,0:T(8,128)(2,1)} %shard_map.91), channel_id=1, replica_groups=mesh['x'=4,'yh'=4,'core'=2,'z'=8,'yl'=2] {'x','yh','core'}, dimensions={0} | all-to-all | bytes 786432 | tf_op jit(solution)/shard_map/all_to_all | solution.py:234
  155.8 9.2 %all-to-all-start.1 = ((bf16[16,40,128]{2,1,0:T(8,128)(2,1)}), bf16[16,40,128]{2,1,0:T(8,128)(2,1)S(1)}, u32[]{:S(2)}, u32[]{:S(2)}) async-start(bf16[16,40,128]{2,1,0:T(8,128)(2,1)} %get-tuple-element.33), calls=%async_computation.1 | async-start | bytes 327680 | tf_op jit(solution)/shard_map/all_to_all | solution.py:234
  165.0 3.3 %collective-permute-start.15 = (bf16[8,72,192]{2,1,0:T(8,128)(2,1)S(1)}, bf16[8,72,192]{2,1,0:T(8,128)(2,1)S(1)}, u32[]{:S(2)}, u32[]{:S(2)}) collective-permute-start(bf16[8,72,192]{2,1,0:T(8,128)(2,1)S(1)} %copy-done.12), channel_id=1, source_target_pairs={{0,1},{1,0},{2,3},{3,2},{4,5},{5,4},{6,7},{7,6},{8,9},{9,8},{10,11... | collective-permute-start | bytes 663560 | tf_op jit(solution)/shard_map/ppermute | solution.py:230
  168.3 4.9 %all-to-all-done.1.att_ref = bf16[16,40,128]{2,1,0:T(8,128)(2,1)S(1)} async-done(((bf16[16,40,128]{2,1,0:T(8,128)(2,1)}), bf16[16,40,128]{2,1,0:T(8,128)(2,1)S(1)}, u32[]{:S(2)}, u32[]{:S(2)}) %all-to-all-start.1) | async-done | bytes 163872 | tf_op jit(solution)/shard_map/all_to_all | solution.py:234
  174.0 6.7 %all-to-all-start.3 = ((bf16[32,48,128]{2,1,0:T(8,128)(2,1)}), bf16[32,48,128]{2,1,0:T(8,128)(2,1)S(1)}, u32[]{:S(2)}, u32[]{:S(2)}) async-start(bf16[32,48,128]{2,1,0:T(8,128)(2,1)} %broadcast_in_dim.12), calls=%async_computation.3 | async-start | bytes 786432 | tf_op jit(solution)/shard_map/all_to_all | solution.py:234
  187.2 3.8 %collective-permute-start.17 = (bf16[72,1024]{1,0:T(8,128)(2,1)}, bf16[72,1024]{1,0:T(8,128)(2,1)S(1)}, u32[]{:S(2)}, u32[]{:S(2)}) collective-permute-start(bf16[72,1024]{1,0:T(8,128)(2,1)} %get-tuple-element.41), channel_id=1, source_target_pairs={{0,6},{2,8},{4,10},{6,12},{8,14},{10,0},{12,2},{14,4},{1,7},{3,9},... | collective-permute-start | bytes 442376 | tf_op jit(solution)/shard_map/ppermute | solution.py:230
  191.0 4.5 %collective-permute-start.18 = (bf16[72,1024]{1,0:T(8,128)(2,1)}, bf16[72,1024]{1,0:T(8,128)(2,1)S(1)}, u32[]{:S(2)}, u32[]{:S(2)}) collective-permute-start(bf16[72,1024]{1,0:T(8,128)(2,1)} %get-tuple-element.42), channel_id=1, source_target_pairs={{0,10},{2,12},{4,14},{6,0},{8,2},{10,4},{12,6},{14,8},{1,11},{3,13... | collective-permute-start | bytes 442376 | tf_op jit(solution)/shard_map/ppermute | solution.py:230
  195.5 3.9 %collective-permute-start.19 = (bf16[72,1024]{1,0:T(8,128)(2,1)}, bf16[72,1024]{1,0:T(8,128)(2,1)S(1)}, u32[]{:S(2)}, u32[]{:S(2)}) collective-permute-start(bf16[72,1024]{1,0:T(8,128)(2,1)} %get-tuple-element.43), channel_id=1, source_target_pairs={{0,4},{2,6},{4,8},{6,10},{8,12},{10,14},{12,0},{14,2},{1,5},{3,7},... | collective-permute-start | bytes 442376 | tf_op jit(solution)/shard_map/ppermute | solution.py:230
  199.4 3.5 %collective-permute-start.20 = (bf16[72,1024]{1,0:T(8,128)(2,1)}, bf16[72,1024]{1,0:T(8,128)(2,1)S(1)}, u32[]{:S(2)}, u32[]{:S(2)}) collective-permute-start(bf16[72,1024]{1,0:T(8,128)(2,1)} %get-tuple-element.44), channel_id=1, source_target_pairs={{0,12},{2,14},{4,0},{6,2},{8,4},{10,6},{12,8},{14,10},{1,13},{3,15... | collective-permute-start | bytes 442376 | tf_op jit(solution)/shard_map/ppermute | solution.py:230
  202.9 3.1 %collective-permute-start.21 = (bf16[72,1024]{1,0:T(8,128)(2,1)}, bf16[72,1024]{1,0:T(8,128)(2,1)S(1)}, u32[]{:S(2)}, u32[]{:S(2)}) collective-permute-start(bf16[72,1024]{1,0:T(8,128)(2,1)} %get-tuple-element.45), channel_id=1, source_target_pairs={{0,2},{2,4},{4,6},{6,8},{8,10},{10,12},{12,14},{14,0},{1,3},{3,5},... | collective-permute-start | bytes 442376 | tf_op jit(solution)/shard_map/ppermute | solution.py:230
  206.0 3.3 %collective-permute-done.17 = bf16[72,1024]{1,0:T(8,128)(2,1)S(1)} collective-permute-done((bf16[72,1024]{1,0:T(8,128)(2,1)}, bf16[72,1024]{1,0:T(8,128)(2,1)S(1)}, u32[]{:S(2)}, u32[]{:S(2)}) %collective-permute-start.17) | collective-permute-done | bytes 147488 | tf_op jit(solution)/shard_map/ppermute | solution.py:230
  211.3 3.0 %shard_map.88 = bf16[72,1024]{1,0:T(8,128)(2,1)} custom-call(bf16[16,40,128]{2,1,0:T(8,128)(2,1)} %copy-done.2, bf16[1024,1024]{1,0:T(8,128)(2,1)} %bitcast.23), custom_call_target="tpu_custom_call" | custom-call | flops 150994944 | tf_op jit(solution)/shard_map/pallas_call | solution.py:325
  (86 shorter events, 33.7 us)
Async XLA Ops:
  0.6 37.2 %copy-start.3 = (bf16[1,1024,192]{1,2,0:T(8,128)(2,1)S(1)}, bf16[1,1024,192]{1,2,0:T(8,128)(2,1)}, u32[]{:S(2)}) copy-start(bf16[1,1024,192]{1,2,0:T(8,128)(2,1)} %param.8) | copy-start | bytes 1179652
  0.6 21.0 %collective-permute-start.2 = (bf16[72,1024]{1,0:T(8,128)(2,1)}, bf16[72,1024]{1,0:T(8,128)(2,1)S(1)}, u32[]{:S(2)}, u32[]{:S(2)}) collective-permute-start(bf16[72,1024]{1,0:T(8,128)(2,1)} %bitcast.32), channel_id=1, source_target_pairs={{0,4},{2,6},{4,8},{6,10},{8,12},{10,14},{12,0},{14,2},{1,5},{3,7},... | collective-permute-start | bytes 442376 | tf_op jit(solution)/shard_map/ppermute | solution.py:230
  7.4 19.5 %collective-permute-start.3 = (bf16[72,1024]{1,0:T(8,128)(2,1)}, bf16[72,1024]{1,0:T(8,128)(2,1)S(1)}, u32[]{:S(2)}, u32[]{:S(2)}) collective-permute-start(bf16[72,1024]{1,0:T(8,128)(2,1)} %bitcast.33), channel_id=1, source_target_pairs={{0,12},{2,14},{4,0},{6,2},{8,4},{10,6},{12,8},{14,10},{1,13},{3,15... | collective-permute-start | bytes 442376 | tf_op jit(solution)/shard_map/ppermute | solution.py:230
  14.2 15.9 %collective-permute-start = (bf16[72,1024]{1,0:T(8,128)(2,1)}, bf16[72,1024]{1,0:T(8,128)(2,1)S(1)}, u32[]{:S(2)}, u32[]{:S(2)}) collective-permute-start(bf16[72,1024]{1,0:T(8,128)(2,1)} %bitcast.34), channel_id=1, source_target_pairs={{0,2},{2,4},{4,6},{6,8},{8,10},{10,12},{12,14},{14,0},{1,3},{3,5},... | collective-permute-start | bytes 442376 | tf_op jit(solution)/shard_map/ppermute | solution.py:230
  17.3 12.8 %collective-permute-start.1 = (bf16[72,1024]{1,0:T(8,128)(2,1)}, bf16[72,1024]{1,0:T(8,128)(2,1)S(1)}, u32[]{:S(2)}, u32[]{:S(2)}) collective-permute-start(bf16[72,1024]{1,0:T(8,128)(2,1)} %bitcast.35), channel_id=1, source_target_pairs={{0,14},{2,0},{4,2},{6,4},{8,6},{10,8},{12,10},{14,12},{1,15},{3,1}... | collective-permute-start | bytes 442376 | tf_op jit(solution)/shard_map/ppermute | solution.py:230
  21.6 12.8 %collective-permute-start.6 = (bf16[72,1024]{1,0:T(8,128)(2,1)S(1)}, bf16[72,1024]{1,0:T(8,128)(2,1)S(1)}, u32[]{:S(2)}, u32[]{:S(2)}) collective-permute-start(bf16[72,1024]{1,0:T(8,128)(2,1)S(1)} %collective-permute-done.2), channel_id=1, source_target_pairs={{0,4},{2,6},{4,8},{6,10},{8,12},{10,14},{12,0},{14,2},{1,5},{3,7},... | collective-permute-start | bytes 442376 | tf_op jit(solution)/shard_map/ppermute | solution.py:230
  23.6 10.8 %collective-permute-start.4 = (bf16[72,1024]{1,0:T(8,128)(2,1)S(1)}, bf16[72,1024]{1,0:T(8,128)(2,1)S(1)}, u32[]{:S(2)}, u32[]{:S(2)}) collective-permute-start(bf16[72,1024]{1,0:T(8,128)(2,1)S(1)} %collective-permute-done.2), channel_id=1, source_target_pairs={{0,2},{2,4},{4,6},{6,8},{8,10},{10,12},{12,14},{14,0},{1,3},{3,5},... | collective-permute-start | bytes 442376 | tf_op jit(solution)/shard_map/ppermute | solution.py:230
  26.9 7.5 %collective-permute-start.5 = (bf16[72,1024]{1,0:T(8,128)(2,1)S(1)}, bf16[72,1024]{1,0:T(8,128)(2,1)S(1)}, u32[]{:S(2)}, u32[]{:S(2)}) collective-permute-start(bf16[72,1024]{1,0:T(8,128)(2,1)S(1)} %collective-permute-done.3), channel_id=1, source_target_pairs={{0,14},{2,0},{4,2},{6,4},{8,6},{10,8},{12,10},{14,12},{1,15},{3,1}... | collective-permute-start | bytes 442376 | tf_op jit(solution)/shard_map/ppermute | solution.py:230
  34.5 88.3 %collective-permute-start.23 = (bf16[576,1024]{1,0:T(8,128)(2,1)S(1)}, bf16[576,1024]{1,0:T(8,128)(2,1)S(1)}, u32[]{:S(2)}, u32[]{:S(2)}) collective-permute-start(bf16[576,1024]{1,0:T(8,128)(2,1)S(1)} %constant_dynamic-update-slice_fusion.tokens_ref), channel_id=1, source_target_pairs={{0,1},{1,0},{2,3},{3,2},{4,5},{5,4},{6,7},{7,6},{8,9},{9,8},{10,11... | collective-permute-start | bytes 3538952 | tf_op jit(solution)/shard_map/ppermute | solution.py:230
  37.8 31.7 %collective-permute-start.7 = (bf16[192,1024]{1,0:T(8,128)(2,1)S(1)}, bf16[192,1024]{1,0:T(8,128)(2,1)S(1)}, u32[]{:S(2)}, u32[]{:S(2)}) collective-permute-start(bf16[192,1024]{1,0:T(8,128)(2,1)S(1)} %bitcast.29), channel_id=1, source_target_pairs={{0,1},{1,0},{2,3},{3,2},{4,5},{5,4},{6,7},{7,6},{8,9},{9,8},{10,11... | collective-permute-start | bytes 1179656 | tf_op jit(solution)/shard_map/ppermute | solution.py:230
  43.1 52.0 %all-to-all-start = ((bf16[16,40,128]{2,1,0:T(8,128)(2,1)}), bf16[16,40,128]{2,1,0:T(8,128)(2,1)S(1)}, u32[]{:S(2)}, u32[]{:S(2)}) async-start(bf16[16,40,128]{2,1,0:T(8,128)(2,1)} %shard_map.86), calls=%async_computation | async-start | bytes 327680 | tf_op jit(solution)/shard_map/all_to_all | solution.py:234
  73.4 26.0 %collective-permute-start.8 = (bf16[8,72,192]{2,1,0:T(8,128)(2,1)}, bf16[8,72,192]{2,1,0:T(8,128)(2,1)S(1)}, u32[]{:S(2)}, u32[]{:S(2)}) collective-permute-start(bf16[8,72,192]{2,1,0:T(8,128)(2,1)} %get-tuple-element.28), channel_id=1, source_target_pairs={{0,1},{1,0},{2,3},{3,2},{4,5},{5,4},{6,7},{7,6},{8,9},{9,8},{10,11... | collective-permute-start | bytes 663560 | tf_op jit(solution)/shard_map/ppermute | solution.py:230
  76.8 12.7 %collective-permute-start.9 = (bf16[4,72,128]{2,1,0:T(8,128)(2,1)}, bf16[4,72,128]{2,1,0:T(8,128)(2,1)S(1)}, u32[]{:S(2)}, u32[]{:S(2)}) collective-permute-start(bf16[4,72,128]{2,1,0:T(8,128)(2,1)} %get-tuple-element.29), channel_id=1, source_target_pairs={{0,496},{16,0},{32,16},{48,32},{64,48},{80,64},{96,80},{112,96},{1... | collective-permute-start | bytes 221192 | tf_op jit(solution)/shard_map/ppermute | solution.py:230
  83.5 11.5 %collective-permute-start.10 = (bf16[4,72,128]{2,1,0:T(8,128)(2,1)}, bf16[4,72,128]{2,1,0:T(8,128)(2,1)S(1)}, u32[]{:S(2)}, u32[]{:S(2)}) collective-permute-start(bf16[4,72,128]{2,1,0:T(8,128)(2,1)} %get-tuple-element.30), channel_id=1, source_target_pairs={{0,16},{16,32},{32,48},{48,64},{64,80},{80,96},{96,112},{112,128},... | collective-permute-start | bytes 221192 | tf_op jit(solution)/shard_map/ppermute | solution.py:230
  87.6 8.0 %collective-permute-start.11 = (bf16[4,72,128]{2,1,0:T(8,128)(2,1)}, bf16[4,72,128]{2,1,0:T(8,128)(2,1)S(1)}, u32[]{:S(2)}, u32[]{:S(2)}) collective-permute-start(bf16[4,72,128]{2,1,0:T(8,128)(2,1)} %get-tuple-element.31), channel_id=1, source_target_pairs={{0,497},{1,496},{16,1},{17,0},{32,17},{33,16},{48,33},{49,32},{64,... | collective-permute-start | bytes 221192 | tf_op jit(solution)/shard_map/ppermute | solution.py:267
  89.6 9.9 %collective-permute-start.12 = (bf16[4,72,128]{2,1,0:T(8,128)(2,1)}, bf16[4,72,128]{2,1,0:T(8,128)(2,1)S(1)}, u32[]{:S(2)}, u32[]{:S(2)}) collective-permute-start(bf16[4,72,128]{2,1,0:T(8,128)(2,1)} %get-tuple-element.32), channel_id=1, source_target_pairs={{0,17},{1,16},{16,33},{17,32},{32,49},{33,48},{48,65},{49,64},{64,... | collective-permute-start | bytes 221192 | tf_op jit(solution)/shard_map/ppermute | solution.py:268
  100.2 16.0 %copy-start.9 = (s32[8]{0:T(128)S(1)}, s32[8]{0:T(128)}, u32[]{:S(2)}) copy-start(s32[8]{0:T(128)} %get-tuple-element.50.table_ref) | copy-start | bytes 100
  108.5 8.3 %collective-permute-start.13 = (bf16[8,72,128]{2,1,0:T(8,128)(2,1)}, bf16[8,72,128]{2,1,0:T(8,128)(2,1)S(1)}, u32[]{:S(2)}, u32[]{:S(2)}) collective-permute-start(bf16[8,72,128]{2,1,0:T(8,128)(2,1)} %get-tuple-element.36), channel_id=1, source_target_pairs={{0,16},{16,32},{32,48},{48,64},{64,80},{80,96},{96,112},{112,128},... | collective-permute-start | bytes 442376 | tf_op jit(solution)/shard_map/ppermute | solution.py:230
  110.4 9.2 %collective-permute-start.14 = (bf16[8,72,128]{2,1,0:T(8,128)(2,1)}, bf16[8,72,128]{2,1,0:T(8,128)(2,1)S(1)}, u32[]{:S(2)}, u32[]{:S(2)}) collective-permute-start(bf16[8,72,128]{2,1,0:T(8,128)(2,1)} %get-tuple-element.37), channel_id=1, source_target_pairs={{0,496},{16,0},{32,16},{48,32},{64,48},{80,64},{96,80},{112,96},{1... | collective-permute-start | bytes 442376 | tf_op jit(solution)/shard_map/ppermute | solution.py:230
  123.8 41.1 %copy-start.12 = (bf16[8,72,192]{2,1,0:T(8,128)(2,1)S(1)}, bf16[8,72,192]{2,1,0:T(8,128)(2,1)}, u32[]{:S(2)}) copy-start(bf16[8,72,192]{2,1,0:T(8,128)(2,1)} %get-tuple-element.39) | copy-start | bytes 663556
  127.4 53.3 %copy-start.18 = (s32[8]{0:T(128)S(1)}, s32[8]{0:T(128)}, u32[]{:S(2)}) copy-start(s32[8]{0:T(128)} %constant.40.clone) | copy-start | bytes 100
  155.8 17.4 %all-to-all-start.1 = ((bf16[16,40,128]{2,1,0:T(8,128)(2,1)}), bf16[16,40,128]{2,1,0:T(8,128)(2,1)S(1)}, u32[]{:S(2)}, u32[]{:S(2)}) async-start(bf16[16,40,128]{2,1,0:T(8,128)(2,1)} %get-tuple-element.33), calls=%async_computation.1 | async-start | bytes 327680 | tf_op jit(solution)/shard_map/all_to_all | solution.py:234
  165.0 16.3 %collective-permute-start.15 = (bf16[8,72,192]{2,1,0:T(8,128)(2,1)S(1)}, bf16[8,72,192]{2,1,0:T(8,128)(2,1)S(1)}, u32[]{:S(2)}, u32[]{:S(2)}) collective-permute-start(bf16[8,72,192]{2,1,0:T(8,128)(2,1)S(1)} %copy-done.12), channel_id=1, source_target_pairs={{0,1},{1,0},{2,3},{3,2},{4,5},{5,4},{6,7},{7,6},{8,9},{9,8},{10,11... | collective-permute-start | bytes 663560 | tf_op jit(solution)/shard_map/ppermute | solution.py:230
  173.2 11.6 %copy-start.2 = (bf16[16,40,128]{2,1,0:T(8,128)(2,1)}, bf16[16,40,128]{2,1,0:T(8,128)(2,1)S(1)}, u32[]{:S(2)}) copy-start(bf16[16,40,128]{2,1,0:T(8,128)(2,1)S(1)} %all-to-all-done.1.att_ref) | copy-start | bytes 491524
  174.0 44.3 %all-to-all-start.3 = ((bf16[32,48,128]{2,1,0:T(8,128)(2,1)}), bf16[32,48,128]{2,1,0:T(8,128)(2,1)S(1)}, u32[]{:S(2)}, u32[]{:S(2)}) async-start(bf16[32,48,128]{2,1,0:T(8,128)(2,1)} %broadcast_in_dim.12), calls=%async_computation.3 | async-start | bytes 786432 | tf_op jit(solution)/shard_map/all_to_all | solution.py:234
  184.8 18.1 %collective-permute-start.16 = (bf16[72,1024]{1,0:T(8,128)(2,1)}, bf16[72,1024]{1,0:T(8,128)(2,1)S(1)}, u32[]{:S(2)}, u32[]{:S(2)}) collective-permute-start(bf16[72,1024]{1,0:T(8,128)(2,1)} %get-tuple-element.40), channel_id=1, source_target_pairs={{0,8},{2,10},{4,12},{6,14},{8,0},{10,2},{12,4},{14,6},{1,9},{3,11}... | collective-permute-start | bytes 442376 | tf_op jit(solution)/shard_map/ppermute | solution.py:230
  187.2 22.1 %collective-permute-start.17 = (bf16[72,1024]{1,0:T(8,128)(2,1)}, bf16[72,1024]{1,0:T(8,128)(2,1)S(1)}, u32[]{:S(2)}, u32[]{:S(2)}) collective-permute-start(bf16[72,1024]{1,0:T(8,128)(2,1)} %get-tuple-element.41), channel_id=1, source_target_pairs={{0,6},{2,8},{4,10},{6,12},{8,14},{10,0},{12,2},{14,4},{1,7},{3,9},... | collective-permute-start | bytes 442376 | tf_op jit(solution)/shard_map/ppermute | solution.py:230
  191.0 23.3 %collective-permute-start.18 = (bf16[72,1024]{1,0:T(8,128)(2,1)}, bf16[72,1024]{1,0:T(8,128)(2,1)S(1)}, u32[]{:S(2)}, u32[]{:S(2)}) collective-permute-start(bf16[72,1024]{1,0:T(8,128)(2,1)} %get-tuple-element.42), channel_id=1, source_target_pairs={{0,10},{2,12},{4,14},{6,0},{8,2},{10,4},{12,6},{14,8},{1,11},{3,13... | collective-permute-start | bytes 442376 | tf_op jit(solution)/shard_map/ppermute | solution.py:230
  195.5 18.8 %collective-permute-start.19 = (bf16[72,1024]{1,0:T(8,128)(2,1)}, bf16[72,1024]{1,0:T(8,128)(2,1)S(1)}, u32[]{:S(2)}, u32[]{:S(2)}) collective-permute-start(bf16[72,1024]{1,0:T(8,128)(2,1)} %get-tuple-element.43), channel_id=1, source_target_pairs={{0,4},{2,6},{4,8},{6,10},{8,12},{10,14},{12,0},{14,2},{1,5},{3,7},... | collective-permute-start | bytes 442376 | tf_op jit(solution)/shard_map/ppermute | solution.py:230
  199.4 14.9 %collective-permute-start.20 = (bf16[72,1024]{1,0:T(8,128)(2,1)}, bf16[72,1024]{1,0:T(8,128)(2,1)S(1)}, u32[]{:S(2)}, u32[]{:S(2)}) collective-permute-start(bf16[72,1024]{1,0:T(8,128)(2,1)} %get-tuple-element.44), channel_id=1, source_target_pairs={{0,12},{2,14},{4,0},{6,2},{8,4},{10,6},{12,8},{14,10},{1,13},{3,15... | collective-permute-start | bytes 442376 | tf_op jit(solution)/shard_map/ppermute | solution.py:230
  202.9 14.1 %collective-permute-start.21 = (bf16[72,1024]{1,0:T(8,128)(2,1)}, bf16[72,1024]{1,0:T(8,128)(2,1)S(1)}, u32[]{:S(2)}, u32[]{:S(2)}) collective-permute-start(bf16[72,1024]{1,0:T(8,128)(2,1)} %get-tuple-element.45), channel_id=1, source_target_pairs={{0,2},{2,4},{4,6},{6,8},{8,10},{10,12},{12,14},{14,0},{1,3},{3,5},... | collective-permute-start | bytes 442376 | tf_op jit(solution)/shard_map/ppermute | solution.py:230
  209.3 8.1 %collective-permute-start.22 = (bf16[72,1024]{1,0:T(8,128)(2,1)}, bf16[72,1024]{1,0:T(8,128)(2,1)S(1)}, u32[]{:S(2)}, u32[]{:S(2)}) collective-permute-start(bf16[72,1024]{1,0:T(8,128)(2,1)} %get-tuple-element.46), channel_id=1, source_target_pairs={{0,14},{2,0},{4,2},{6,4},{8,6},{10,8},{12,10},{14,12},{1,15},{3,1}... | collective-permute-start | bytes 442376 | tf_op jit(solution)/shard_map/ppermute | solution.py:230
  (14 other events, 54.8 us)

commit v2 on v1

--- a/solution.py
+++ b/solution.py
@@ -88,9 +88,10 @@
 
 def project_kernel(
     table_ref, tokens_ref, own_ref, other_ref,
-    kv_ref, q_ref, swap_ref, west_ref, east_ref, west2_ref, east2_ref,
+    kv_ref, q_ref, swap_ref, far_ref, near_ref, far2_ref, near2_ref,
     kv32, kv32b,
 ):
+    first_core = table_ref[8] == 0
     own, other = turned(own_ref), turned(other_ref)
     for chunk in range(2):
         rows = tokens_ref[chunk * 288 : (chunk + 1) * 288, :]
@@ -106,22 +107,25 @@
             kv32b[row] = piece[:, :128]
             swap_ref[row] = piece.astype(BF16)
     west, east = pack_pair(kv32[...])
-    west_ref[...] = west.astype(BF16)
-    east_ref[...] = east.astype(BF16)
+    far_ref[...] = jnp.where(first_core, west, east).astype(BF16)
+    near_ref[...] = jnp.where(first_core, east, west).astype(BF16)
     west, east = pack_pair(kv32b[...])
-    west2_ref[...] = west.astype(BF16)
-    east2_ref[...] = east.astype(BF16)
+    far2_ref[...] = jnp.where(first_core, west, east).astype(BF16)
+    near2_ref[...] = jnp.where(first_core, east, west).astype(BF16)
 
 
 def attend_kernel(
-    place_ref, kv_ref, q_ref, swapped_ref, grad_ref, from_e_ref, from_w_ref, from_e2_ref, from_w2_ref,
-    out_ref, dq_ref, dkv_ref, to_e_ref, to_w_ref,
+    place_ref, kv_ref, q_ref, swapped_ref, grad_ref, far_ref, near_ref, far2_ref, near2_ref,
+    out_ref, dq_ref, dkv_ref, to_far_ref, to_near_ref,
     keys, queries, halo, dhalo,
 ):
     scale = HD ** (-0.5)
     yl = place_ref[0]
-    side = unpack_pair(from_e_ref[...].astype(F32), from_w_ref[...].astype(F32))
-    side2 = unpack_pair(from_e2_ref[...].astype(F32), from_w2_ref[...].astype(F32))
+    first_core = place_ref[1] == 0
+    far, near = far_ref[...].astype(F32), near_ref[...].astype(F32)
+    side = unpack_pair(jnp.where(first_core, near, far), jnp.where(first_core, far, near))
+    far, near = far2_ref[...].astype(F32), near2_ref[...].astype(F32)
+    side2 = unpack_pair(jnp.where(first_core, near, far), jnp.where(first_core, far, near))
     for row in range(8):
         mine, theirs = 2 * row + yl, 2 * row + 1 - yl
         keys[mine] = kv_ref[row].astype(F32)
@@ -174,15 +178,17 @@
                 dkv_ref[rank] = own[i]
                 dhalo[rank] = side[i]
     to_e, to_w = pack_pair(dhalo[...])
-    to_e_ref[...] = to_e.astype(BF16)
-    to_w_ref[...] = to_w.astype(BF16)
+    to_far_ref[...] = jnp.where(first_core, to_w, to_e).astype(BF16)
+    to_near_ref[...] = jnp.where(first_core, to_e, to_w).astype(BF16)
 
 
 def combine_kernel(
-    place_ref, dq_ref, dkv_ref, got_w_ref, got_e_ref, pg_ref, mine_ref, swap_ref, pg32
+    place_ref, dq_ref, dkv_ref, far_ref, near_ref, pg_ref, mine_ref, swap_ref, pg32
 ):
     yl = place_ref[0]
-    first, second = unpack_pair(got_w_ref[...].astype(F32), got_e_ref[...].astype(F32))
+    first_core = place_ref[1] == 0
+    far, near = far_ref[...].astype(F32), near_ref[...].astype(F32)
+    first, second = unpack_pair(jnp.where(first_core, far, near), jnp.where(first_core, near, far))
     for half, add in ((0, first), (1, second)):
         span = slice(8 * half, 8 * half + 8)
         pg32[span, :, 0:128] = dkv_ref[span] + add
@@ -236,24 +242,29 @@
 
 def step(latents, out_grad, qkv_weight, out_weight):
     width = latents.shape[-1]
-    z, yl = lax.axis_index("z"), lax.axis_index("yl")
+    z, yl, core = (lax.axis_index(a).astype(jnp.int32) for a in ("z", "yl", "core"))
     mine = latents.reshape(TOK, width)
     own = jnp.swapaxes(qkv_weight[0], 0, 1)
     d1, d7, d2, d6 = (shift(mine, "z", 8, d) for d in (1, 7, 2, 6))
     other = shift(own, "yl", 2, 1)
     d3, d5 = shift(d2, "z", 8, 1), shift(d6, "z", 8, -1)
     d4 = shift(d2, "z", 8, 2)
-    tokens = jnp.concatenate([mine, d1, d7, d2, d6, d3, d5, d4], axis=0)
+    close = jnp.concatenate([mine, d1, d7, d2, d6], axis=0)
+    close2 = shift(close, "yl", 2, 1)
+    distant = jnp.concatenate([d3, d5, d4], axis=0)
+    distant2 = shift(distant, "yl", 2, 1)
+    tokens = jnp.concatenate([close, distant], axis=0)
+    tokens2 = jnp.concatenate([close2, distant2], axis=0)
     distance = jnp.array([0, 1, 7, 2, 6, 3, 5, 4], jnp.int32)
     rows = ((z - distance) % 8).astype(jnp.int32)
-    place = yl.astype(jnp.int32).reshape(1)
+    place = jnp.stack([yl, core])
 
     (token_grad,) = call(
         token_grad_kernel, [((RANKS, 40, 128), BF16)], n_in=2, flops=2 * TOK * width * width
     )(out_grad.reshape(TOK, width), out_weight)
     band_grad = exchange(token_grad, HEAD)
 
-    kv, query, swap, to_w, to_e, to_w2, to_e2 = call(
+    kv, query, swap, far, near, far2, near2 = call(
         project_kernel,
         [((8, TOK, 128), BF16), ((8, TOK, HD), BF16), ((8, TOK, 3 * HD), BF16)]
         + [((4, TOK, 128), BF16)] * 4,
@@ -261,14 +272,11 @@
         smem=(0,),
         n_in=4,
         flops=2 * 1152 * 192 * width,
-    )(rows, tokens, own, other)
-    from_e = shift(to_w, LON, 32, -1)
-    from_w = shift(to_e, LON, 32, 1)
-    from_e2 = lax.ppermute(to_w2, LON + ("yl",), across(-1))
-    from_w2 = lax.ppermute(to_e2, LON + ("yl",), across(1))
+    )(jnp.concatenate([rows, core.reshape(1)]), tokens, own, other)
+    far, near = send_far(far), shift(near, "core", 2, 1)
+    far2, near2 = send_far(far2, 1), send_near(near2, 1)
     swapped = shift(swap, "yl", 2, 1)
-    tokens2 = shift(tokens, "yl", 2, 1)
-    attended, dq, dkv, grad_east, grad_west = call(
+    attended, dq, dkv, grad_far, grad_near = call(
         attend_kernel,
         [
             ((RANKS, 40, 128), BF16),
@@ -286,9 +294,8 @@
         smem=(0,),
         n_in=9,
         flops=8 * 6 * 2 * 144 * 576 * 128,
-    )(place, kv, query, swapped, band_grad, from_e, from_w, from_e2, from_w2)
-    got_west = shift(grad_east, LON, 32, 1)
-    got_east = shift(grad_west, LON, 32, -1)
+    )(place, kv, query, swapped, band_grad, far, near, far2, near2)
+    grad_far, grad_near = send_far(grad_far), shift(grad_near, "core", 2, 1)
     token_att = exchange(attended, HEAD)
 
     pg, pg_mine, pg_swap = call(
@@ -298,7 +305,7 @@
         smem=(0,),
         n_in=5,
         flops=1 << 20,
-    )(place, dq, dkv, got_west, got_east)
+    )(place, dq, dkv, grad_far, grad_near)
     pg_got = shift(pg_swap, "yl", 2, 1)
     (pieces,) = call(
         weight_grad_kernel,
@@ -319,7 +326,10 @@
         n_in=5,
         flops=2 * 576 * 384 * width,
     )(((z + jnp.array(reach, jnp.int32)) % 8).astype(jnp.int32), pg_mine, pg_got, own, other)
-    shares = [shift(s, "z", 8, d) if d else s for s, d in zip(shares, reach)]
+    passed = shift(shares[0], "z", 8, -1)
+    shares = list(shares[1:])
+    shares[1] = (shares[1].astype(F32) + passed.astype(F32)).astype(BF16)
+    shares = [shift(s, "z", 8, d) if d else s for s, d in zip(shares, reach[1:])]
     summed = jnp.sum(pieces.astype(F32), axis=0).astype(BF16)
     copies = exchange(jnp.broadcast_to(summed[None], (32, 48, 128)), LON)
     (mixed,) = call(mix_kernel, [((TOK, width), BF16)], n_in=2, flops=2 * TOK * width * width)(
@@ -331,8 +341,18 @@
     return mixed.reshape(latents.shape), latent_grad.reshape(latents.shape), qkv_grad
 
 
-def across(distance):
-    return [(2 * i + j, 2 * ((i + distance) % 32) + 1 - j) for i in range(32) for j in range(2)]
+def send_far(value, turn=0):
+    routes = [
+        (2 * i + j, 2 * ((i + (1 if i % 2 else -1)) % 32) + (j ^ turn))
+        for i in range(32)
+        for j in range(2)
+    ]
+    return lax.ppermute(value, LON + ("yl",), routes)
+
+
+def send_near(value, turn=0):
+    routes = [(2 * i + j, 2 * (i ^ 1) + (j ^ turn)) for i in range(32) for j in range(2)]
+    return lax.ppermute(value, LON + ("yl",), routes)
 
 
 def solution(mesh):

time: 221 us -> 205 us (0.928)
  waiting for transfers between devices: 41.8 us -> 29.8 us
  blocking collectives: 28.4 us -> 21.9 us
    ppermute x2 -> x4, starting transfers between devices: 7.36 us -> 20.7 us  [the longest x3 17.4 us: send_far(): return lax.ppermute(value, LON + ('yl',), routes)]
    ppermute x22 -> x21, waiting for transfers between devices: 32.5 us -> 21.4 us  [shift(): lax.ppermute(value, axis, [(i, (i + distance) % size) for i in range(size)])]
    ppermute x22 -> x21, starting transfers between devices: 81.9 us -> 74 us  [shift(): lax.ppermute(value, axis, [(i, (i + distance) % size) for i in range(size)])]
    all_to_all x1, blocking collectives: 28.4 us -> 21.9 us  [exchange(): return lax.all_to_all(value, axis, 0, 0, tiled=True)]
    all_to_all x3, waiting for transfers between devices: 4.9 us -> 0.01 us  [exchange(): return lax.all_to_all(value, axis, 0, 0, tiled=True)]
    all_to_all x3, starting transfers between devices: 22.6 us -> 17.8 us  [exchange(): return lax.all_to_all(value, axis, 0, 0, tiled=True)]
    ppermute x2 -> x4, waiting for transfers between devices: 4.4 us -> 8.41 us  [the longest x3 8.41 us: send_far(): return lax.ppermute(value, LON + ('yl',), routes)]
    unnamed x46 -> x53, local copies, waits for them, and re-layouts: 5.96 us -> 5.15 us
  transfers between devices with their start and end apart: 27 -> 28, of which waited for: 9 -> 5; matrix products, arithmetic and copies ran while one was open for 2% -> 2% of each run, Pallas kernels for 11% -> 11%
where the time goes in v2:
time: 205 us; the launch traced here: 203 us
  starting transfers between devices  112 us (55%)
  waiting for transfers between devices  29.8 us (15%)
  Pallas kernels  26.8 us (13%)
  blocking collectives  21.9 us (11%)
  local copies, waits for them, and re-layouts  6.23 us (3%)
  other arithmetic  4.42 us (2%)
    ppermute x21, starting transfers between devices, shift(): lax.ppermute(value, axis, [(i, (i + distance) % size) for i in range(size)])  74 us
    all_to_all x1, blocking collectives, exchange(): return lax.all_to_all(value, axis, 0, 0, tiled=True)  21.9 us
    ppermute x21, waiting for transfers between devices, shift(): lax.ppermute(value, axis, [(i, (i + distance) % size) for i in range(size)])  21.4 us
    all_to_all x3, starting transfers between devices, exchange(): return lax.all_to_all(value, axis, 0, 0, tiled=True)  17.8 us
    ppermute x3, starting transfers between devices, send_far(): return lax.ppermute(value, LON + ('yl',), routes)  17.4 us
    ppermute x3, waiting for transfers between devices, send_far(): return lax.ppermute(value, LON + ('yl',), routes)  8.41 us
    pallas_call x1, Pallas kernels, step(): call(attend_kernel, [((RANKS, 40, 128), BF16), ((RANKS, TOK, HD), F32), (...  8.35 us
    unnamed x53, local copies, waits for them, and re-layouts  5.15 us
  transfers between devices with their start and end apart: 28, of which 5 were waited for; matrix products, arithmetic and copies ran while one was open for 2% of the time, Pallas kernels for 11%

profile of v2, /device:TPU:1, one launch (start us, length us, event | category | flops | bytes accessed | tf_op | source)
XLA Modules:
  0.0 203.0 jit_solution(5465529140398577937)
XLA Ops:
  0.6 4.8 %collective-permute-start = (bf16[72,1024]{1,0:T(8,128)(2,1)}, bf16[72,1024]{1,0:T(8,128)(2,1)S(1)}, u32[]{:S(2)}, u32[]{:S(2)}) collective-permute-start(bf16[72,1024]{1,0:T(8,128)(2,1)} %bitcast.34), channel_id=1, source_target_pairs={{0,2},{2,4},{4,6},{6,8},{8,10},{10,12},{12,14},{14,0},{1,3},{3,5},... | collective-permute-start | bytes 442376 | tf_op jit(solution)/shard_map/ppermute | solution.py:236
  5.5 8.6 %collective-permute-start.1 = (bf16[72,1024]{1,0:T(8,128)(2,1)}, bf16[72,1024]{1,0:T(8,128)(2,1)S(1)}, u32[]{:S(2)}, u32[]{:S(2)}) collective-permute-start(bf16[72,1024]{1,0:T(8,128)(2,1)} %bitcast.35), channel_id=1, source_target_pairs={{0,14},{2,0},{4,2},{6,4},{8,6},{10,8},{12,10},{14,12},{1,15},{3,1}... | collective-permute-start | bytes 442376 | tf_op jit(solution)/shard_map/ppermute | solution.py:236
  16.0 5.5 %collective-permute-start.3 = (bf16[72,1024]{1,0:T(8,128)(2,1)}, bf16[72,1024]{1,0:T(8,128)(2,1)S(1)}, u32[]{:S(2)}, u32[]{:S(2)}) collective-permute-start(bf16[72,1024]{1,0:T(8,128)(2,1)} %bitcast.37), channel_id=1, source_target_pairs={{0,12},{2,14},{4,0},{6,2},{8,4},{10,6},{12,8},{14,10},{1,13},{3,15... | collective-permute-start | bytes 442376 | tf_op jit(solution)/shard_map/ppermute | solution.py:236
  21.5 3.2 %collective-permute-start.7 = (bf16[192,1024]{1,0:T(8,128)(2,1)}, bf16[192,1024]{1,0:T(8,128)(2,1)S(1)}, u32[]{:S(2)}, u32[]{:S(2)}) collective-permute-start(bf16[192,1024]{1,0:T(8,128)(2,1)} %bitcast.28), channel_id=1, source_target_pairs={{0,1},{1,0},{2,3},{3,2},{4,5},{5,4},{6,7},{7,6},{8,9},{9,8},{10,11... | collective-permute-start | bytes 1179656 | tf_op jit(solution)/shard_map/ppermute | solution.py:236
  24.7 3.3 %shard_map.86 = bf16[16,40,128]{2,1,0:T(8,128)(2,1)} custom-call(bf16[72,1024]{1,0:T(8,128)(2,1)} %bitcast.31, bf16[16,64,1024]{2,1,0:T(8,128)(2,1)} %weight_ref.1), custom_call_target="tpu_custom_call" | custom-call | flops 150994944 | tf_op jit(solution)/shard_map/pallas_call | solution.py:262
  28.0 4.0 %all-to-all-start = ((bf16[16,40,128]{2,1,0:T(8,128)(2,1)}), bf16[16,40,128]{2,1,0:T(8,128)(2,1)S(1)}, u32[]{:S(2)}, u32[]{:S(2)}) async-start(bf16[16,40,128]{2,1,0:T(8,128)(2,1)} %shard_map.86), calls=%async_computation | async-start | bytes 327680 | tf_op jit(solution)/shard_map/all_to_all | solution.py:240
  32.7 3.3 %collective-permute-start.4 = (bf16[72,1024]{1,0:T(8,128)(2,1)S(1)}, bf16[72,1024]{1,0:T(8,128)(2,1)S(1)}, u32[]{:S(2)}, u32[]{:S(2)}) collective-permute-start(bf16[72,1024]{1,0:T(8,128)(2,1)S(1)} %collective-permute-done.2), channel_id=1, source_target_pairs={{0,2},{2,4},{4,6},{6,8},{8,10},{10,12},{12,14},{14,0},{1,3},{3,5},... | collective-permute-start | bytes 442376 | tf_op jit(solution)/shard_map/ppermute | solution.py:236
  35.9 3.2 %collective-permute-start.5 = (bf16[72,1024]{1,0:T(8,128)(2,1)S(1)}, bf16[72,1024]{1,0:T(8,128)(2,1)S(1)}, u32[]{:S(2)}, u32[]{:S(2)}) collective-permute-start(bf16[72,1024]{1,0:T(8,128)(2,1)S(1)} %collective-permute-done.3), channel_id=1, source_target_pairs={{0,14},{2,0},{4,2},{6,4},{8,6},{10,8},{12,10},{14,12},{1,15},{3,1}... | collective-permute-start | bytes 442376 | tf_op jit(solution)/shard_map/ppermute | solution.py:236
  39.3 3.3 %collective-permute-start.23 = (bf16[360,1024]{1,0:T(8,128)(2,1)S(1)}, bf16[360,1024]{1,0:T(8,128)(2,1)S(1)}, u32[]{:S(2)}, u32[]{:S(2)}) collective-permute-start(bf16[360,1024]{1,0:T(8,128)(2,1)S(1)} %get-tuple-element.51), channel_id=1, source_target_pairs={{0,1},{1,0},{2,3},{3,2},{4,5},{5,4},{6,7},{7,6},{8,9},{9,8},{10,11... | collective-permute-start | bytes 2211848 | tf_op jit(solution)/shard_map/ppermute | solution.py:236
  45.4 6.4 %collective-permute-done.6 = bf16[72,1024]{1,0:T(8,128)(2,1)S(1)} collective-permute-done((bf16[72,1024]{1,0:T(8,128)(2,1)S(1)}, bf16[72,1024]{1,0:T(8,128)(2,1)S(1)}, u32[]{:S(2)}, u32[]{:S(2)}) %collective-permute-start.6) | collective-permute-done | bytes 147488 | tf_op jit(solution)/shard_map/ppermute | solution.py:236
  53.7 3.2 %shard_map.85 = (bf16[8,72,128]{2,1,0:T(8,128)(2,1)}, bf16[8,72,64]{2,1,0:T(8,128)(2,1)}, bf16[8,72,192]{2,1,0:T(8,128)(2,1)}, bf16[4,72,128]{2,1,0:T(8,128)(2,1...) custom-call(s32[9]{0:T(128)} %pad_add_fusion.1.table_ref, ...), custom_call_target="tpu_custom_call" | custom-call | flops 452984832 | tf_op jit(solution)/shard_map/pallas_call | solution.py:267
  59.0 8.5 %collective-permute-start.9 = (bf16[4,72,128]{2,1,0:T(8,128)(2,1)}, bf16[4,72,128]{2,1,0:T(8,128)(2,1)S(1)}, u32[]{:S(2)}, u32[]{:S(2)}) collective-permute-start(bf16[4,72,128]{2,1,0:T(8,128)(2,1)} %get-tuple-element.29), channel_id=1, source_target_pairs={{0,496},{1,497},{16,32},{17,33},{32,16},{33,17},{48,64},{49,65},{6... | collective-permute-start | bytes 221192 | tf_op jit(solution)/shard_map/ppermute | solution.py:350
  69.5 3.2 %collective-permute-start.24 = (bf16[216,1024]{1,0:T(8,128)(2,1)S(1)}, bf16[216,1024]{1,0:T(8,128)(2,1)S(1)}, u32[]{:S(2)}, u32[]{:S(2)}) collective-permute-start(bf16[216,1024]{1,0:T(8,128)(2,1)S(1)} %pad_maximum_fusion.1), channel_id=1, source_target_pairs={{0,1},{1,0},{2,3},{3,2},{4,5},{5,4},{6,7},{7,6},{8,9},{9,8},{10,11... | collective-permute-start | bytes 1327112 | tf_op jit(solution)/shard_map/ppermute | solution.py:236
  72.8 5.8 %collective-permute-start.11 = (bf16[4,72,128]{2,1,0:T(8,128)(2,1)}, bf16[4,72,128]{2,1,0:T(8,128)(2,1)S(1)}, u32[]{:S(2)}, u32[]{:S(2)}) collective-permute-start(bf16[4,72,128]{2,1,0:T(8,128)(2,1)} %get-tuple-element.31), channel_id=1, source_target_pairs={{0,497},{1,496},{16,33},{17,32},{32,17},{33,16},{48,65},{49,64},{6... | collective-permute-start | bytes 221192 | tf_op jit(solution)/shard_map/ppermute | solution.py:350
  78.7 3.3 %collective-permute-start.12 = (bf16[4,72,128]{2,1,0:T(8,128)(2,1)}, bf16[4,72,128]{2,1,0:T(8,128)(2,1)S(1)}, u32[]{:S(2)}, u32[]{:S(2)}) collective-permute-start(bf16[4,72,128]{2,1,0:T(8,128)(2,1)} %get-tuple-element.32), channel_id=1, source_target_pairs={{0,17},{1,16},{16,1},{17,0},{32,49},{33,48},{48,33},{49,32},{64,81... | collective-permute-start | bytes 221192 | tf_op jit(solution)/shard_map/ppermute | solution.py:355
  82.6 5.9 %collective-permute-done.11.far2_ref = bf16[4,72,128]{2,1,0:T(8,128)(2,1)S(1)} collective-permute-done((bf16[4,72,128]{2,1,0:T(8,128)(2,1)}, bf16[4,72,128]{2,1,0:T(8,128)(2,1)S(1)}, u32[]{:S(2)}, u32[]{:S(2)}) %collective-permute-start.11) | collective-permute-done | bytes 73760 | tf_op jit(solution)/shard_map/ppermute | solution.py:350
  89.3 8.3 %shard_map.87 = (bf16[16,40,128]{2,1,0:T(8,128)(2,1)}, f32[16,72,64]{2,1,0:T(8,128)}, f32[16,72,128]{2,1,0:T(8,128)}, bf16[8,72,128]{2,1,0:T(8,128)(2,1)}, bf16[8,72,128]{2,1,0:T(8,128)(2,1)}) custom-call(s32[2]{0:T(128)} %pad_add_fusion.place_ref, bf16[8,72,128]{2,1,0:T(8,128)(2,1)} %get-tuple-element.26.kv_ref, ...), custom_call_target="tpu_custom_call" | custom-call | flops 1019215872 | tf_op jit(solution)/shard_map/pallas_call | solution.py:279
  97.6 3.1 %collective-permute-start.13 = (bf16[8,72,128]{2,1,0:T(8,128)(2,1)}, bf16[8,72,128]{2,1,0:T(8,128)(2,1)S(1)}, u32[]{:S(2)}, u32[]{:S(2)}) collective-permute-start(bf16[8,72,128]{2,1,0:T(8,128)(2,1)} %get-tuple-element.36), channel_id=1, source_target_pairs={{0,496},{1,497},{16,32},{17,33},{32,16},{33,17},{48,64},{49,65},{6... | collective-permute-start | bytes 442376 | tf_op jit(solution)/shard_map/ppermute | solution.py:350
  100.7 3.0 %collective-permute-start.14 = (bf16[8,72,128]{2,1,0:T(8,128)(2,1)}, bf16[8,72,128]{2,1,0:T(8,128)(2,1)S(1)}, u32[]{:S(2)}, u32[]{:S(2)}) collective-permute-start(bf16[8,72,128]{2,1,0:T(8,128)(2,1)} %get-tuple-element.37), channel_id=1, source_target_pairs={{0,16},{16,0},{1,17},{17,1},{2,18},{18,2},{3,19},{19,3},{4,20},{20... | collective-permute-start | bytes 442376 | tf_op jit(solution)/shard_map/ppermute | solution.py:236
  111.3 3.6 %shard_map.91 = bf16[32,48,128]{2,1,0:T(8,128)(2,1)} custom-call(s32[16]{0:T(128)} %pad_add_fusion.2.table_ref, bf16[576,1024]{1,0:T(8,128)(2,1)} %copy-done, bf16[576,1024]{1,0:T(8,128)(2,1)} %pad_maximum_fusion.tokens2_ref, bf16[16,72,192]{2,1,0:T(8,128)(2,1)} %get-tuple-element.48.pg_ref), custom_call_target="tpu_custom_call" | custom-call | flops 452984832 | tf_op jit(solution)/shard_map/pallas_call | solution.py:310
  114.9 21.9 %all_to_all.20 = bf16[32,48,128]{2,1,0:T(8,128)(2,1)S(1)} all-to-all(bf16[32,48,128]{2,1,0:T(8,128)(2,1)} %shard_map.91), channel_id=1, replica_groups=mesh['x'=4,'yh'=4,'core'=2,'z'=8,'yl'=2] {'x','yh','core'}, dimensions={0} | all-to-all | bytes 786432 | tf_op jit(solution)/shard_map/all_to_all | solution.py:240
  136.8 8.2 %all-to-all-start.1 = ((bf16[16,40,128]{2,1,0:T(8,128)(2,1)}), bf16[16,40,128]{2,1,0:T(8,128)(2,1)S(1)}, u32[]{:S(2)}, u32[]{:S(2)}) async-start(bf16[16,40,128]{2,1,0:T(8,128)(2,1)} %get-tuple-element.33), calls=%async_computation.1 | async-start | bytes 327680 | tf_op jit(solution)/shard_map/all_to_all | solution.py:240
  145.0 3.3 %collective-permute-start.15 = (bf16[8,72,192]{2,1,0:T(8,128)(2,1)S(1)}, bf16[8,72,192]{2,1,0:T(8,128)(2,1)S(1)}, u32[]{:S(2)}, u32[]{:S(2)}) collective-permute-start(bf16[8,72,192]{2,1,0:T(8,128)(2,1)S(1)} %copy-done.11), channel_id=1, source_target_pairs={{0,1},{1,0},{2,3},{3,2},{4,5},{5,4},{6,7},{7,6},{8,9},{9,8},{10,11... | collective-permute-start | bytes 663560 | tf_op jit(solution)/shard_map/ppermute | solution.py:236
  148.8 6.3 %collective-permute-done.15.got_ref = bf16[8,72,192]{2,1,0:T(8,128)(2,1)S(1)} collective-permute-done((bf16[8,72,192]{2,1,0:T(8,128)(2,1)S(1)}, bf16[8,72,192]{2,1,0:T(8,128)(2,1)S(1)}, u32[]{:S(2)}, u32[]{:S(2)}) %collective-permute-start.15) | collective-permute-done | bytes 221216 | tf_op jit(solution)/shard_map/ppermute | solution.py:236
  158.7 4.1 %collective-permute-start.17 = (bf16[72,1024]{1,0:T(8,128)(2,1)}, bf16[72,1024]{1,0:T(8,128)(2,1)S(1)}, u32[]{:S(2)}, u32[]{:S(2)}) collective-permute-start(bf16[72,1024]{1,0:T(8,128)(2,1)} %get-tuple-element.42), channel_id=1, source_target_pairs={{0,14},{2,0},{4,2},{6,4},{8,6},{10,8},{12,10},{14,12},{1,15},{3,1}... | collective-permute-start | bytes 442376 | tf_op jit(solution)/shard_map/ppermute | solution.py:236
  163.7 5.5 %all-to-all-start.3 = ((bf16[32,48,128]{2,1,0:T(8,128)(2,1)}), bf16[32,48,128]{2,1,0:T(8,128)(2,1)S(1)}, u32[]{:S(2)}, u32[]{:S(2)}) async-start(bf16[32,48,128]{2,1,0:T(8,128)(2,1)} %broadcast_in_dim.12), calls=%async_computation.3 | async-start | bytes 786432 | tf_op jit(solution)/shard_map/all_to_all | solution.py:240
  169.2 3.1 %collective-permute-start.22 = (bf16[72,1024]{1,0:T(8,128)(2,1)S(1)}, bf16[72,1024]{1,0:T(8,128)(2,1)S(1)}, u32[]{:S(2)}, u32[]{:S(2)}) collective-permute-start(bf16[72,1024]{1,0:T(8,128)(2,1)S(1)} %copy-done.17), channel_id=1, source_target_pairs={{0,14},{2,0},{4,2},{6,4},{8,6},{10,8},{12,10},{14,12},{1,15},{3,1}... | collective-permute-start | bytes 442376 | tf_op jit(solution)/shard_map/ppermute | solution.py:236
  174.6 4.0 %collective-permute-start.20 = (bf16[72,1024]{1,0:T(8,128)(2,1)S(1)}, bf16[72,1024]{1,0:T(8,128)(2,1)S(1)}, u32[]{:S(2)}, u32[]{:S(2)}) collective-permute-start(bf16[72,1024]{1,0:T(8,128)(2,1)S(1)} %copy-done.15), channel_id=1, source_target_pairs={{0,12},{2,14},{4,0},{6,2},{8,4},{10,6},{12,8},{14,10},{1,13},{3,15... | collective-permute-start | bytes 442376 | tf_op jit(solution)/shard_map/ppermute | solution.py:236
  180.8 5.2 %collective-permute-start.16 = (bf16[72,1024]{1,0:T(8,128)(2,1)S(1)}, bf16[72,1024]{1,0:T(8,128)(2,1)S(1)}, u32[]{:S(2)}, u32[]{:S(2)}) collective-permute-start(bf16[72,1024]{1,0:T(8,128)(2,1)S(1)} %copy-done.13), channel_id=1, source_target_pairs={{0,6},{2,8},{4,10},{6,12},{8,14},{10,0},{12,2},{14,4},{1,7},{3,9},... | collective-permute-start | bytes 442376 | tf_op jit(solution)/shard_map/ppermute | solution.py:236
  186.1 3.1 %collective-permute-start.18 = (bf16[72,1024]{1,0:T(8,128)(2,1)S(1)}, bf16[72,1024]{1,0:T(8,128)(2,1)S(1)}, u32[]{:S(2)}, u32[]{:S(2)}) collective-permute-start(bf16[72,1024]{1,0:T(8,128)(2,1)S(1)} %add_convert_fusion.1), channel_id=1, source_target_pairs={{0,10},{2,12},{4,14},{6,0},{8,2},{10,4},{12,6},{14,8},{1,11},{3,13... | collective-permute-start | bytes 442376 | tf_op jit(solution)/shard_map/ppermute | solution.py:236
  189.2 3.0 %shard_map.88 = bf16[72,1024]{1,0:T(8,128)(2,1)} custom-call(bf16[16,40,128]{2,1,0:T(8,128)(2,1)} %copy-done.1, bf16[1024,1024]{1,0:T(8,128)(2,1)} %bitcast.24), custom_call_target="tpu_custom_call" | custom-call | flops 150994944 | tf_op jit(solution)/shard_map/pallas_call | solution.py:335
  192.2 8.6 %collective-permute-done.16 = bf16[72,1024]{1,0:T(8,128)(2,1)S(1)} collective-permute-done((bf16[72,1024]{1,0:T(8,128)(2,1)S(1)}, bf16[72,1024]{1,0:T(8,128)(2,1)S(1)}, u32[]{:S(2)}, u32[]{:S(2)}) %collective-permute-start.16) | collective-permute-done | bytes 147488 | tf_op jit(solution)/shard_map/ppermute | solution.py:236
  (101 shorter events, 31.8 us)
Async XLA Ops:
  0.6 38.5 %collective-permute-start = (bf16[72,1024]{1,0:T(8,128)(2,1)}, bf16[72,1024]{1,0:T(8,128)(2,1)S(1)}, u32[]{:S(2)}, u32[]{:S(2)}) collective-permute-start(bf16[72,1024]{1,0:T(8,128)(2,1)} %bitcast.34), channel_id=1, source_target_pairs={{0,2},{2,4},{4,6},{6,8},{8,10},{10,12},{12,14},{14,0},{1,3},{3,5},... | collective-permute-start | bytes 442376 | tf_op jit(solution)/shard_map/ppermute | solution.py:236
  5.5 33.8 %collective-permute-start.1 = (bf16[72,1024]{1,0:T(8,128)(2,1)}, bf16[72,1024]{1,0:T(8,128)(2,1)S(1)}, u32[]{:S(2)}, u32[]{:S(2)}) collective-permute-start(bf16[72,1024]{1,0:T(8,128)(2,1)} %bitcast.35), channel_id=1, source_target_pairs={{0,14},{2,0},{4,2},{6,4},{8,6},{10,8},{12,10},{14,12},{1,15},{3,1}... | collective-permute-start | bytes 442376 | tf_op jit(solution)/shard_map/ppermute | solution.py:236
  14.1 18.6 %collective-permute-start.2 = (bf16[72,1024]{1,0:T(8,128)(2,1)}, bf16[72,1024]{1,0:T(8,128)(2,1)S(1)}, u32[]{:S(2)}, u32[]{:S(2)}) collective-permute-start(bf16[72,1024]{1,0:T(8,128)(2,1)} %bitcast.36), channel_id=1, source_target_pairs={{0,4},{2,6},{4,8},{6,10},{8,12},{10,14},{12,0},{14,2},{1,5},{3,7},... | collective-permute-start | bytes 442376 | tf_op jit(solution)/shard_map/ppermute | solution.py:236
  16.0 19.9 %collective-permute-start.3 = (bf16[72,1024]{1,0:T(8,128)(2,1)}, bf16[72,1024]{1,0:T(8,128)(2,1)S(1)}, u32[]{:S(2)}, u32[]{:S(2)}) collective-permute-start(bf16[72,1024]{1,0:T(8,128)(2,1)} %bitcast.37), channel_id=1, source_target_pairs={{0,12},{2,14},{4,0},{6,2},{8,4},{10,6},{12,8},{14,10},{1,13},{3,15... | collective-permute-start | bytes 442376 | tf_op jit(solution)/shard_map/ppermute | solution.py:236
  21.5 30.4 %collective-permute-start.7 = (bf16[192,1024]{1,0:T(8,128)(2,1)}, bf16[192,1024]{1,0:T(8,128)(2,1)S(1)}, u32[]{:S(2)}, u32[]{:S(2)}) collective-permute-start(bf16[192,1024]{1,0:T(8,128)(2,1)} %bitcast.28), channel_id=1, source_target_pairs={{0,1},{1,0},{2,3},{3,2},{4,5},{5,4},{6,7},{7,6},{8,9},{9,8},{10,11... | collective-permute-start | bytes 1179656 | tf_op jit(solution)/shard_map/ppermute | solution.py:236
  28.0 54.6 %all-to-all-start = ((bf16[16,40,128]{2,1,0:T(8,128)(2,1)}), bf16[16,40,128]{2,1,0:T(8,128)(2,1)S(1)}, u32[]{:S(2)}, u32[]{:S(2)}) async-start(bf16[16,40,128]{2,1,0:T(8,128)(2,1)} %shard_map.86), calls=%async_computation | async-start | bytes 327680 | tf_op jit(solution)/shard_map/all_to_all | solution.py:240
  32.7 12.7 %collective-permute-start.4 = (bf16[72,1024]{1,0:T(8,128)(2,1)S(1)}, bf16[72,1024]{1,0:T(8,128)(2,1)S(1)}, u32[]{:S(2)}, u32[]{:S(2)}) collective-permute-start(bf16[72,1024]{1,0:T(8,128)(2,1)S(1)} %collective-permute-done.2), channel_id=1, source_target_pairs={{0,2},{2,4},{4,6},{6,8},{8,10},{10,12},{12,14},{14,0},{1,3},{3,5},... | collective-permute-start | bytes 442376 | tf_op jit(solution)/shard_map/ppermute | solution.py:236
  35.9 9.5 %collective-permute-start.5 = (bf16[72,1024]{1,0:T(8,128)(2,1)S(1)}, bf16[72,1024]{1,0:T(8,128)(2,1)S(1)}, u32[]{:S(2)}, u32[]{:S(2)}) collective-permute-start(bf16[72,1024]{1,0:T(8,128)(2,1)S(1)} %collective-permute-done.3), channel_id=1, source_target_pairs={{0,14},{2,0},{4,2},{6,4},{8,6},{10,8},{12,10},{14,12},{1,15},{3,1}... | collective-permute-start | bytes 442376 | tf_op jit(solution)/shard_map/ppermute | solution.py:236
  39.3 70.9 %collective-permute-start.23 = (bf16[360,1024]{1,0:T(8,128)(2,1)S(1)}, bf16[360,1024]{1,0:T(8,128)(2,1)S(1)}, u32[]{:S(2)}, u32[]{:S(2)}) collective-permute-start(bf16[360,1024]{1,0:T(8,128)(2,1)S(1)} %get-tuple-element.51), channel_id=1, source_target_pairs={{0,1},{1,0},{2,3},{3,2},{4,5},{5,4},{6,7},{7,6},{8,9},{9,8},{10,11... | collective-permute-start | bytes 2211848 | tf_op jit(solution)/shard_map/ppermute | solution.py:236
  42.6 9.3 %collective-permute-start.6 = (bf16[72,1024]{1,0:T(8,128)(2,1)S(1)}, bf16[72,1024]{1,0:T(8,128)(2,1)S(1)}, u32[]{:S(2)}, u32[]{:S(2)}) collective-permute-start(bf16[72,1024]{1,0:T(8,128)(2,1)S(1)} %collective-permute-done.2), channel_id=1, source_target_pairs={{0,4},{2,6},{4,8},{6,10},{8,12},{10,14},{12,0},{14,2},{1,5},{3,7},... | collective-permute-start | bytes 442376 | tf_op jit(solution)/shard_map/ppermute | solution.py:236
  56.8 31.6 %collective-permute-start.8 = (bf16[8,72,192]{2,1,0:T(8,128)(2,1)}, bf16[8,72,192]{2,1,0:T(8,128)(2,1)S(1)}, u32[]{:S(2)}, u32[]{:S(2)}) collective-permute-start(bf16[8,72,192]{2,1,0:T(8,128)(2,1)} %get-tuple-element.28), channel_id=1, source_target_pairs={{0,1},{1,0},{2,3},{3,2},{4,5},{5,4},{6,7},{7,6},{8,9},{9,8},{10,11... | collective-permute-start | bytes 663560 | tf_op jit(solution)/shard_map/ppermute | solution.py:236
  59.0 13.7 %collective-permute-start.9 = (bf16[4,72,128]{2,1,0:T(8,128)(2,1)}, bf16[4,72,128]{2,1,0:T(8,128)(2,1)S(1)}, u32[]{:S(2)}, u32[]{:S(2)}) collective-permute-start(bf16[4,72,128]{2,1,0:T(8,128)(2,1)} %get-tuple-element.29), channel_id=1, source_target_pairs={{0,496},{1,497},{16,32},{17,33},{32,16},{33,17},{48,64},{49,65},{6... | collective-permute-start | bytes 221192 | tf_op jit(solution)/shard_map/ppermute | solution.py:350
  67.6 11.1 %collective-permute-start.10 = (bf16[4,72,128]{2,1,0:T(8,128)(2,1)}, bf16[4,72,128]{2,1,0:T(8,128)(2,1)S(1)}, u32[]{:S(2)}, u32[]{:S(2)}) collective-permute-start(bf16[4,72,128]{2,1,0:T(8,128)(2,1)} %get-tuple-element.30), channel_id=1, source_target_pairs={{0,16},{16,0},{1,17},{17,1},{2,18},{18,2},{3,19},{19,3},{4,20},{20... | collective-permute-start | bytes 221192 | tf_op jit(solution)/shard_map/ppermute | solution.py:236
  69.5 40.6 %collective-permute-start.24 = (bf16[216,1024]{1,0:T(8,128)(2,1)S(1)}, bf16[216,1024]{1,0:T(8,128)(2,1)S(1)}, u32[]{:S(2)}, u32[]{:S(2)}) collective-permute-start(bf16[216,1024]{1,0:T(8,128)(2,1)S(1)} %pad_maximum_fusion.1), channel_id=1, source_target_pairs={{0,1},{1,0},{2,3},{3,2},{4,5},{5,4},{6,7},{7,6},{8,9},{9,8},{10,11... | collective-permute-start | bytes 1327112 | tf_op jit(solution)/shard_map/ppermute | solution.py:236
  72.8 15.7 %collective-permute-start.11 = (bf16[4,72,128]{2,1,0:T(8,128)(2,1)}, bf16[4,72,128]{2,1,0:T(8,128)(2,1)S(1)}, u32[]{:S(2)}, u32[]{:S(2)}) collective-permute-start(bf16[4,72,128]{2,1,0:T(8,128)(2,1)} %get-tuple-element.31), channel_id=1, source_target_pairs={{0,497},{1,496},{16,33},{17,32},{32,17},{33,16},{48,65},{49,64},{6... | collective-permute-start | bytes 221192 | tf_op jit(solution)/shard_map/ppermute | solution.py:350
  78.7 9.8 %collective-permute-start.12 = (bf16[4,72,128]{2,1,0:T(8,128)(2,1)}, bf16[4,72,128]{2,1,0:T(8,128)(2,1)S(1)}, u32[]{:S(2)}, u32[]{:S(2)}) collective-permute-start(bf16[4,72,128]{2,1,0:T(8,128)(2,1)} %get-tuple-element.32), channel_id=1, source_target_pairs={{0,17},{1,16},{16,1},{17,0},{32,49},{33,48},{48,33},{49,32},{64,81... | collective-permute-start | bytes 221192 | tf_op jit(solution)/shard_map/ppermute | solution.py:355
  97.6 9.2 %collective-permute-start.13 = (bf16[8,72,128]{2,1,0:T(8,128)(2,1)}, bf16[8,72,128]{2,1,0:T(8,128)(2,1)S(1)}, u32[]{:S(2)}, u32[]{:S(2)}) collective-permute-start(bf16[8,72,128]{2,1,0:T(8,128)(2,1)} %get-tuple-element.36), channel_id=1, source_target_pairs={{0,496},{1,497},{16,32},{17,33},{32,16},{33,17},{48,64},{49,65},{6... | collective-permute-start | bytes 442376 | tf_op jit(solution)/shard_map/ppermute | solution.py:350
  100.7 6.2 %collective-permute-start.14 = (bf16[8,72,128]{2,1,0:T(8,128)(2,1)}, bf16[8,72,128]{2,1,0:T(8,128)(2,1)S(1)}, u32[]{:S(2)}, u32[]{:S(2)}) collective-permute-start(bf16[8,72,128]{2,1,0:T(8,128)(2,1)} %get-tuple-element.37), channel_id=1, source_target_pairs={{0,16},{16,0},{1,17},{17,1},{2,18},{18,2},{3,19},{19,3},{4,20},{20... | collective-permute-start | bytes 442376 | tf_op jit(solution)/shard_map/ppermute | solution.py:236
  111.3 33.7 %copy-start.11 = (bf16[8,72,192]{2,1,0:T(8,128)(2,1)S(1)}, bf16[8,72,192]{2,1,0:T(8,128)(2,1)}, u32[]{:S(2)}) copy-start(bf16[8,72,192]{2,1,0:T(8,128)(2,1)} %get-tuple-element.39) | copy-start | bytes 663556
  111.3 37.0 %copy-start.22 = (s32[8]{0:T(128)S(1)}, s32[8]{0:T(128)}, u32[]{:S(2)}) copy-start(s32[8]{0:T(128)} %constant.44.clone) | copy-start | bytes 100
  136.8 26.1 %all-to-all-start.1 = ((bf16[16,40,128]{2,1,0:T(8,128)(2,1)}), bf16[16,40,128]{2,1,0:T(8,128)(2,1)S(1)}, u32[]{:S(2)}, u32[]{:S(2)}) async-start(bf16[16,40,128]{2,1,0:T(8,128)(2,1)} %get-tuple-element.33), calls=%async_computation.1 | async-start | bytes 327680 | tf_op jit(solution)/shard_map/all_to_all | solution.py:240
  145.0 10.1 %collective-permute-start.15 = (bf16[8,72,192]{2,1,0:T(8,128)(2,1)S(1)}, bf16[8,72,192]{2,1,0:T(8,128)(2,1)S(1)}, u32[]{:S(2)}, u32[]{:S(2)}) collective-permute-start(bf16[8,72,192]{2,1,0:T(8,128)(2,1)S(1)} %copy-done.11), channel_id=1, source_target_pairs={{0,1},{1,0},{2,3},{3,2},{4,5},{5,4},{6,7},{7,6},{8,9},{9,8},{10,11... | collective-permute-start | bytes 663560 | tf_op jit(solution)/shard_map/ppermute | solution.py:236
  158.7 27.3 %copy-start.6 = (bf16[72,1024]{1,0:T(8,128)(2,1)S(1)}, bf16[72,1024]{1,0:T(8,128)(2,1)}, u32[]{:S(2)}) copy-start(bf16[72,1024]{1,0:T(8,128)(2,1)} %get-tuple-element.41) | copy-start | bytes 442372
  158.7 22.1 %collective-permute-start.17 = (bf16[72,1024]{1,0:T(8,128)(2,1)}, bf16[72,1024]{1,0:T(8,128)(2,1)S(1)}, u32[]{:S(2)}, u32[]{:S(2)}) collective-permute-start(bf16[72,1024]{1,0:T(8,128)(2,1)} %get-tuple-element.42), channel_id=1, source_target_pairs={{0,14},{2,0},{4,2},{6,4},{8,6},{10,8},{12,10},{14,12},{1,15},{3,1}... | collective-permute-start | bytes 442376 | tf_op jit(solution)/shard_map/ppermute | solution.py:236
  162.9 26.3 %copy-start.1 = (bf16[16,40,128]{2,1,0:T(8,128)(2,1)}, bf16[16,40,128]{2,1,0:T(8,128)(2,1)S(1)}, u32[]{:S(2)}) copy-start(bf16[16,40,128]{2,1,0:T(8,128)(2,1)S(1)} %all-to-all-done.1.att_ref) | copy-start | bytes 491524
  163.7 38.0 %all-to-all-start.3 = ((bf16[32,48,128]{2,1,0:T(8,128)(2,1)}), bf16[32,48,128]{2,1,0:T(8,128)(2,1)S(1)}, u32[]{:S(2)}, u32[]{:S(2)}) async-start(bf16[32,48,128]{2,1,0:T(8,128)(2,1)} %broadcast_in_dim.12), calls=%async_computation.3 | async-start | bytes 786432 | tf_op jit(solution)/shard_map/all_to_all | solution.py:240
  169.2 16.8 %collective-permute-start.22 = (bf16[72,1024]{1,0:T(8,128)(2,1)S(1)}, bf16[72,1024]{1,0:T(8,128)(2,1)S(1)}, u32[]{:S(2)}, u32[]{:S(2)}) collective-permute-start(bf16[72,1024]{1,0:T(8,128)(2,1)S(1)} %copy-done.17), channel_id=1, source_target_pairs={{0,14},{2,0},{4,2},{6,4},{8,6},{10,8},{12,10},{14,12},{1,15},{3,1}... | collective-permute-start | bytes 442376 | tf_op jit(solution)/shard_map/ppermute | solution.py:236
  172.3 19.9 %collective-permute-start.21 = (bf16[72,1024]{1,0:T(8,128)(2,1)S(1)}, bf16[72,1024]{1,0:T(8,128)(2,1)S(1)}, u32[]{:S(2)}, u32[]{:S(2)}) collective-permute-start(bf16[72,1024]{1,0:T(8,128)(2,1)S(1)} %copy-done.16), channel_id=1, source_target_pairs={{0,2},{2,4},{4,6},{6,8},{8,10},{10,12},{12,14},{14,0},{1,3},{3,5},... | collective-permute-start | bytes 442376 | tf_op jit(solution)/shard_map/ppermute | solution.py:236
  174.6 17.7 %collective-permute-start.20 = (bf16[72,1024]{1,0:T(8,128)(2,1)S(1)}, bf16[72,1024]{1,0:T(8,128)(2,1)S(1)}, u32[]{:S(2)}, u32[]{:S(2)}) collective-permute-start(bf16[72,1024]{1,0:T(8,128)(2,1)S(1)} %copy-done.15), channel_id=1, source_target_pairs={{0,12},{2,14},{4,0},{6,2},{8,4},{10,6},{12,8},{14,10},{1,13},{3,15... | collective-permute-start | bytes 442376 | tf_op jit(solution)/shard_map/ppermute | solution.py:236
  178.6 13.7 %collective-permute-start.19 = (bf16[72,1024]{1,0:T(8,128)(2,1)S(1)}, bf16[72,1024]{1,0:T(8,128)(2,1)S(1)}, u32[]{:S(2)}, u32[]{:S(2)}) collective-permute-start(bf16[72,1024]{1,0:T(8,128)(2,1)S(1)} %copy-done.14), channel_id=1, source_target_pairs={{0,4},{2,6},{4,8},{6,10},{8,12},{10,14},{12,0},{14,2},{1,5},{3,7},... | collective-permute-start | bytes 442376 | tf_op jit(solution)/shard_map/ppermute | solution.py:236
  180.8 20.0 %collective-permute-start.16 = (bf16[72,1024]{1,0:T(8,128)(2,1)S(1)}, bf16[72,1024]{1,0:T(8,128)(2,1)S(1)}, u32[]{:S(2)}, u32[]{:S(2)}) collective-permute-start(bf16[72,1024]{1,0:T(8,128)(2,1)S(1)} %copy-done.13), channel_id=1, source_target_pairs={{0,6},{2,8},{4,10},{6,12},{8,14},{10,0},{12,2},{14,4},{1,7},{3,9},... | collective-permute-start | bytes 442376 | tf_op jit(solution)/shard_map/ppermute | solution.py:236
  186.1 14.7 %collective-permute-start.18 = (bf16[72,1024]{1,0:T(8,128)(2,1)S(1)}, bf16[72,1024]{1,0:T(8,128)(2,1)S(1)}, u32[]{:S(2)}, u32[]{:S(2)}) collective-permute-start(bf16[72,1024]{1,0:T(8,128)(2,1)S(1)} %add_convert_fusion.1), channel_id=1, source_target_pairs={{0,10},{2,12},{4,14},{6,0},{8,2},{10,4},{12,6},{14,8},{1,11},{3,13... | collective-permute-start | bytes 442376 | tf_op jit(solution)/shard_map/ppermute | solution.py:236
  (19 other events, 145.9 us)

commit v3 on v2

--- a/solution.py
+++ b/solution.py
@@ -249,12 +249,8 @@
     other = shift(own, "yl", 2, 1)
     d3, d5 = shift(d2, "z", 8, 1), shift(d6, "z", 8, -1)
     d4 = shift(d2, "z", 8, 2)
-    close = jnp.concatenate([mine, d1, d7, d2, d6], axis=0)
-    close2 = shift(close, "yl", 2, 1)
-    distant = jnp.concatenate([d3, d5, d4], axis=0)
-    distant2 = shift(distant, "yl", 2, 1)
-    tokens = jnp.concatenate([close, distant], axis=0)
-    tokens2 = jnp.concatenate([close2, distant2], axis=0)
+    tokens = jnp.concatenate([mine, d1, d7, d2, d6, d3, d5, d4], axis=0)
+    tokens2 = shift(tokens, "yl", 2, 1)
     distance = jnp.array([0, 1, 7, 2, 6, 3, 5, 4], jnp.int32)
     rows = ((z - distance) % 8).astype(jnp.int32)
     place = jnp.stack([yl, core])

time: 205 us -> 215 us (1.049)
  the two profiles are of different devices: /device:TPU:1 before, /device:TPU:104 now
where the time goes in v3:
time: 215 us; the launch traced here: 214 us
  starting transfers between devices  111 us (52%)
  waiting for transfers between devices  44.5 us (21%)
  Pallas kernels  26.8 us (12%)
  blocking collectives  19.4 us (9%)
  local copies, waits for them, and re-layouts  7.07 us (3%)
  other arithmetic  3.42 us (2%)
    ppermute x20, starting transfers between devices, shift(): lax.ppermute(value, axis, [(i, (i + distance) % size) for i in range(size)])  74.7 us
    ppermute x20, waiting for transfers between devices, shift(): lax.ppermute(value, axis, [(i, (i + distance) % size) for i in range(size)])  37.7 us
    all_to_all x3, starting transfers between devices, exchange(): return lax.all_to_all(value, axis, 0, 0, tiled=True)  24.3 us
    all_to_all x1, blocking collectives, exchange(): return lax.all_to_all(value, axis, 0, 0, tiled=True)  19.4 us
    ppermute x3, starting transfers between devices, send_far(): return lax.ppermute(value, LON + ('yl',), routes)  10.2 us
    pallas_call x1, Pallas kernels, step(): call(attend_kernel, [((RANKS, 40, 128), BF16), ((RANKS, TOK, HD), F32), (...  8.34 us
    unnamed x56, local copies, waits for them, and re-layouts  6 us
    ppermute x3, waiting for transfers between devices, send_far(): return lax.ppermute(value, LON + ('yl',), routes)  4.84 us
  transfers between devices with their start and end apart: 27, of which 8 were waited for; matrix products, arithmetic and copies ran while one was open for 2% of the time, Pallas kernels for 11%

profile of v3, /device:TPU:104, one launch (start us, length us, event | category | flops | bytes accessed | tf_op | source)
XLA Modules:
  0.0 213.7 jit_solution(13134666257901800814)
XLA Ops:
  0.6 6.2 %collective-permute-start.2 = (bf16[72,1024]{1,0:T(8,128)(2,1)}, bf16[72,1024]{1,0:T(8,128)(2,1)S(1)}, u32[]{:S(2)}, u32[]{:S(2)}) collective-permute-start(bf16[72,1024]{1,0:T(8,128)(2,1)} %bitcast.34), channel_id=1, source_target_pairs={{0,4},{2,6},{4,8},{6,10},{8,12},{10,14},{12,0},{14,2},{1,5},{3,7},... | collective-permute-start | bytes 442376 | tf_op jit(solution)/shard_map/ppermute | solution.py:236
  6.9 5.9 %collective-permute-start.3 = (bf16[72,1024]{1,0:T(8,128)(2,1)}, bf16[72,1024]{1,0:T(8,128)(2,1)S(1)}, u32[]{:S(2)}, u32[]{:S(2)}) collective-permute-start(bf16[72,1024]{1,0:T(8,128)(2,1)} %bitcast.35), channel_id=1, source_target_pairs={{0,12},{2,14},{4,0},{6,2},{8,4},{10,6},{12,8},{14,10},{1,13},{3,15... | collective-permute-start | bytes 442376 | tf_op jit(solution)/shard_map/ppermute | solution.py:236
  14.7 3.9 %collective-permute-start.1 = (bf16[72,1024]{1,0:T(8,128)(2,1)}, bf16[72,1024]{1,0:T(8,128)(2,1)S(1)}, u32[]{:S(2)}, u32[]{:S(2)}) collective-permute-start(bf16[72,1024]{1,0:T(8,128)(2,1)} %bitcast.37), channel_id=1, source_target_pairs={{0,14},{2,0},{4,2},{6,4},{8,6},{10,8},{12,10},{14,12},{1,15},{3,1}... | collective-permute-start | bytes 442376 | tf_op jit(solution)/shard_map/ppermute | solution.py:236
  19.5 3.7 %collective-permute-start.6 = (bf16[72,1024]{1,0:T(8,128)(2,1)S(1)}, bf16[72,1024]{1,0:T(8,128)(2,1)S(1)}, u32[]{:S(2)}, u32[]{:S(2)}) collective-permute-start(bf16[72,1024]{1,0:T(8,128)(2,1)S(1)} %collective-permute-done.2), channel_id=1, source_target_pairs={{0,4},{2,6},{4,8},{6,10},{8,12},{10,14},{12,0},{14,2},{1,5},{3,7},... | collective-permute-start | bytes 442376 | tf_op jit(solution)/shard_map/ppermute | solution.py:236
  23.2 5.1 %collective-permute-start.4 = (bf16[72,1024]{1,0:T(8,128)(2,1)S(1)}, bf16[72,1024]{1,0:T(8,128)(2,1)S(1)}, u32[]{:S(2)}, u32[]{:S(2)}) collective-permute-start(bf16[72,1024]{1,0:T(8,128)(2,1)S(1)} %collective-permute-done.2), channel_id=1, source_target_pairs={{0,2},{2,4},{4,6},{6,8},{8,10},{10,12},{12,14},{14,0},{1,3},{3,5},... | collective-permute-start | bytes 442376 | tf_op jit(solution)/shard_map/ppermute | solution.py:236
  32.7 2.7 %collective-permute-done.5 = bf16[72,1024]{1,0:T(8,128)(2,1)S(1)} collective-permute-done((bf16[72,1024]{1,0:T(8,128)(2,1)S(1)}, bf16[72,1024]{1,0:T(8,128)(2,1)S(1)}, u32[]{:S(2)}, u32[]{:S(2)}) %collective-permute-start.5) | collective-permute-done | bytes 147488 | tf_op jit(solution)/shard_map/ppermute | solution.py:236
  35.5 3.3 %collective-permute-start.23 = (bf16[576,1024]{1,0:T(8,128)(2,1)S(1)}, bf16[576,1024]{1,0:T(8,128)(2,1)S(1)}, u32[]{:S(2)}, u32[]{:S(2)}) collective-permute-start(bf16[576,1024]{1,0:T(8,128)(2,1)S(1)} %constant_dynamic-update-slice_fusion.tokens_ref), channel_id=1, source_target_pairs={{0,1},{1,0},{2,3},{3,2},{4,5},{5,4},{6,7},{7,6},{8,9},{9,8},{10,11... | collective-permute-start | bytes 3538952 | tf_op jit(solution)/shard_map/ppermute | solution.py:236
  41.3 3.3 %shard_map.86 = bf16[16,40,128]{2,1,0:T(8,128)(2,1)} custom-call(bf16[72,1024]{1,0:T(8,128)(2,1)} %bitcast.31, bf16[16,64,1024]{2,1,0:T(8,128)(2,1)} %weight_ref.1), custom_call_target="tpu_custom_call" | custom-call | flops 150994944 | tf_op jit(solution)/shard_map/pallas_call | solution.py:258
  44.6 6.0 %all-to-all-start = ((bf16[16,40,128]{2,1,0:T(8,128)(2,1)}), bf16[16,40,128]{2,1,0:T(8,128)(2,1)S(1)}, u32[]{:S(2)}, u32[]{:S(2)}) async-start(bf16[16,40,128]{2,1,0:T(8,128)(2,1)} %shard_map.86), calls=%async_computation | async-start | bytes 327680 | tf_op jit(solution)/shard_map/all_to_all | solution.py:240
  51.2 20.6 %collective-permute-done.7.other_ref = bf16[192,1024]{1,0:T(8,128)(2,1)S(1)} collective-permute-done((bf16[192,1024]{1,0:T(8,128)(2,1)S(1)}, bf16[192,1024]{1,0:T(8,128)(2,1)S(1)}, u32[]{:S(2)}, u32[]{:S(2)}) %collective-permute-start.7) | collective-permute-done | bytes 393248 | tf_op jit(solution)/shard_map/ppermute | solution.py:236
  72.6 3.2 %shard_map.85 = (bf16[8,72,128]{2,1,0:T(8,128)(2,1)}, bf16[8,72,64]{2,1,0:T(8,128)(2,1)}, bf16[8,72,192]{2,1,0:T(8,128)(2,1)}, bf16[4,72,128]{2,1,0:T(8,128)(2,1...) custom-call(s32[9]{0:T(128)} %pad_add_fusion.1.table_ref, ...), custom_call_target="tpu_custom_call" | custom-call | flops 452984832 | tf_op jit(solution)/shard_map/pallas_call | solution.py:263
  75.7 3.2 %collective-permute-start.8 = (bf16[8,72,192]{2,1,0:T(8,128)(2,1)}, bf16[8,72,192]{2,1,0:T(8,128)(2,1)S(1)}, u32[]{:S(2)}, u32[]{:S(2)}) collective-permute-start(bf16[8,72,192]{2,1,0:T(8,128)(2,1)} %get-tuple-element.28), channel_id=1, source_target_pairs={{0,1},{1,0},{2,3},{3,2},{4,5},{5,4},{6,7},{7,6},{8,9},{9,8},{10,11... | collective-permute-start | bytes 663560 | tf_op jit(solution)/shard_map/ppermute | solution.py:236
  80.9 2.8 %collective-permute-start.10 = (bf16[4,72,128]{2,1,0:T(8,128)(2,1)}, bf16[4,72,128]{2,1,0:T(8,128)(2,1)S(1)}, u32[]{:S(2)}, u32[]{:S(2)}) collective-permute-start(bf16[4,72,128]{2,1,0:T(8,128)(2,1)} %get-tuple-element.30), channel_id=1, source_target_pairs={{0,16},{16,0},{1,17},{17,1},{2,18},{18,2},{3,19},{19,3},{4,20},{20... | collective-permute-start | bytes 221192 | tf_op jit(solution)/shard_map/ppermute | solution.py:236
  83.7 5.0 %collective-permute-start.11 = (bf16[4,72,128]{2,1,0:T(8,128)(2,1)}, bf16[4,72,128]{2,1,0:T(8,128)(2,1)S(1)}, u32[]{:S(2)}, u32[]{:S(2)}) collective-permute-start(bf16[4,72,128]{2,1,0:T(8,128)(2,1)} %get-tuple-element.31), channel_id=1, source_target_pairs={{0,497},{1,496},{16,33},{17,32},{32,17},{33,16},{48,65},{49,64},{6... | collective-permute-start | bytes 221192 | tf_op jit(solution)/shard_map/ppermute | solution.py:346
  95.4 8.3 %shard_map.87 = (bf16[16,40,128]{2,1,0:T(8,128)(2,1)}, f32[16,72,64]{2,1,0:T(8,128)}, f32[16,72,128]{2,1,0:T(8,128)}, bf16[8,72,128]{2,1,0:T(8,128)(2,1)}, bf16[8,72,128]{2,1,0:T(8,128)(2,1)}) custom-call(s32[2]{0:T(128)} %pad_add_fusion.place_ref, bf16[8,72,128]{2,1,0:T(8,128)(2,1)} %get-tuple-element.26.kv_ref, ...), custom_call_target="tpu_custom_call" | custom-call | flops 1019215872 | tf_op jit(solution)/shard_map/pallas_call | solution.py:275
  103.7 3.3 %collective-permute-start.13 = (bf16[8,72,128]{2,1,0:T(8,128)(2,1)}, bf16[8,72,128]{2,1,0:T(8,128)(2,1)S(1)}, u32[]{:S(2)}, u32[]{:S(2)}) collective-permute-start(bf16[8,72,128]{2,1,0:T(8,128)(2,1)} %get-tuple-element.36), channel_id=1, source_target_pairs={{0,496},{1,497},{16,32},{17,33},{32,16},{33,17},{48,64},{49,65},{6... | collective-permute-start | bytes 442376 | tf_op jit(solution)/shard_map/ppermute | solution.py:346
  109.5 3.6 %collective-permute-done.13.far_ref = bf16[8,72,128]{2,1,0:T(8,128)(2,1)S(1)} collective-permute-done((bf16[8,72,128]{2,1,0:T(8,128)(2,1)}, bf16[8,72,128]{2,1,0:T(8,128)(2,1)S(1)}, u32[]{:S(2)}, u32[]{:S(2)}) %collective-permute-start.13) | collective-permute-done | bytes 147488 | tf_op jit(solution)/shard_map/ppermute | solution.py:346
  113.8 2.6 %shard_map.89 = (bf16[16,72,192]{2,1,0:T(8,128)(2,1)}, bf16[8,72,192]{2,1,0:T(8,128)(2,1)}, bf16[8,72,192]{2,1,0:T(8,128)(2,1)}) custom-call(s32[2]{0:T(128)} %pad_add_fusion.place_ref, f32[16,72,64]{2,1,0:T(8,128)} %get-tuple-element.34.dq_ref, f32[16,72,128]{2,1,0:T(8,128)} %get-tuple-element.35.dkv_ref, bf16[8,72,128]{2,1,0:T(8,128)(2,1)} %copy-done.8, ...), custom_call_target="tpu_custom_call" | custom-call | flops 1048576 | tf_op jit(solution)/shard_map/pallas_call | solution.py:297
  117.5 3.6 %shard_map.91 = bf16[32,48,128]{2,1,0:T(8,128)(2,1)} custom-call(s32[16]{0:T(128)} %pad_add_fusion.2.table_ref, bf16[576,1024]{1,0:T(8,128)(2,1)} %copy-done, bf16[576,1024]{1,0:T(8,128)(2,1)} %copy-done.1, bf16[16,72,192]{2,1,0:T(8,128)(2,1)} %get-tuple-element.48.pg_ref), custom_call_target="tpu_custom_call" | custom-call | flops 452984832 | tf_op jit(solution)/shard_map/pallas_call | solution.py:306
  121.1 19.4 %all_to_all.20 = bf16[32,48,128]{2,1,0:T(8,128)(2,1)S(1)} all-to-all(bf16[32,48,128]{2,1,0:T(8,128)(2,1)} %shard_map.91), channel_id=1, replica_groups=mesh['x'=4,'yh'=4,'core'=2,'z'=8,'yl'=2] {'x','yh','core'}, dimensions={0} | all-to-all | bytes 786432 | tf_op jit(solution)/shard_map/all_to_all | solution.py:240
  140.5 10.0 %all-to-all-start.1 = ((bf16[16,40,128]{2,1,0:T(8,128)(2,1)}), bf16[16,40,128]{2,1,0:T(8,128)(2,1)S(1)}, u32[]{:S(2)}, u32[]{:S(2)}) async-start(bf16[16,40,128]{2,1,0:T(8,128)(2,1)} %get-tuple-element.33), calls=%async_computation.1 | async-start | bytes 327680 | tf_op jit(solution)/shard_map/all_to_all | solution.py:240
  153.6 7.1 %collective-permute-done.15.got_ref = bf16[8,72,192]{2,1,0:T(8,128)(2,1)S(1)} collective-permute-done((bf16[8,72,192]{2,1,0:T(8,128)(2,1)S(1)}, bf16[8,72,192]{2,1,0:T(8,128)(2,1)S(1)}, u32[]{:S(2)}, u32[]{:S(2)}) %collective-permute-start.15) | collective-permute-done | bytes 221216 | tf_op jit(solution)/shard_map/ppermute | solution.py:236
  161.5 2.8 %shard_map.90 = (bf16[72,1024]{1,0:T(8,128)(2,1)}, bf16[72,1024]{1,0:T(8,128)(2,1)}, bf16[72,1024]{1,0:T(8,128)(2,1)}, bf16[72,1024]{1,0:T(8,128)(2,1)}, bf16[72...) custom-call(s32[8]{0:T(128)} %and_select_fusion.table_ref, ...), custom_call_target="tpu_custom_call" | custom-call | flops 452984832 | tf_op jit(solution)/shard_map/pallas_call | solution.py:318
  164.3 2.6 %collective-permute-start.17 = (bf16[72,1024]{1,0:T(8,128)(2,1)}, bf16[72,1024]{1,0:T(8,128)(2,1)S(1)}, u32[]{:S(2)}, u32[]{:S(2)}) collective-permute-start(bf16[72,1024]{1,0:T(8,128)(2,1)} %get-tuple-element.42), channel_id=1, source_target_pairs={{0,14},{2,0},{4,2},{6,4},{8,6},{10,8},{12,10},{14,12},{1,15},{3,1}... | collective-permute-start | bytes 442376 | tf_op jit(solution)/shard_map/ppermute | solution.py:236
  167.9 8.3 %all-to-all-start.3 = ((bf16[32,48,128]{2,1,0:T(8,128)(2,1)}), bf16[32,48,128]{2,1,0:T(8,128)(2,1)S(1)}, u32[]{:S(2)}, u32[]{:S(2)}) async-start(bf16[32,48,128]{2,1,0:T(8,128)(2,1)} %broadcast_in_dim.12), calls=%async_computation.3 | async-start | bytes 786432 | tf_op jit(solution)/shard_map/all_to_all | solution.py:240
  176.2 6.4 %collective-permute-start.16 = (bf16[72,1024]{1,0:T(8,128)(2,1)S(1)}, bf16[72,1024]{1,0:T(8,128)(2,1)S(1)}, u32[]{:S(2)}, u32[]{:S(2)}) collective-permute-start(bf16[72,1024]{1,0:T(8,128)(2,1)S(1)} %copy-done.18), channel_id=1, source_target_pairs={{0,6},{2,8},{4,10},{6,12},{8,14},{10,0},{12,2},{14,4},{1,7},{3,9},... | collective-permute-start | bytes 442376 | tf_op jit(solution)/shard_map/ppermute | solution.py:236
  182.6 3.4 %collective-permute-start.19 = (bf16[72,1024]{1,0:T(8,128)(2,1)S(1)}, bf16[72,1024]{1,0:T(8,128)(2,1)S(1)}, u32[]{:S(2)}, u32[]{:S(2)}) collective-permute-start(bf16[72,1024]{1,0:T(8,128)(2,1)S(1)} %copy-done.17), channel_id=1, source_target_pairs={{0,4},{2,6},{4,8},{6,10},{8,12},{10,14},{12,0},{14,2},{1,5},{3,7},... | collective-permute-start | bytes 442376 | tf_op jit(solution)/shard_map/ppermute | solution.py:236
  186.0 4.6 %collective-permute-start.20 = (bf16[72,1024]{1,0:T(8,128)(2,1)S(1)}, bf16[72,1024]{1,0:T(8,128)(2,1)S(1)}, u32[]{:S(2)}, u32[]{:S(2)}) collective-permute-start(bf16[72,1024]{1,0:T(8,128)(2,1)S(1)} %copy-done.16), channel_id=1, source_target_pairs={{0,12},{2,14},{4,0},{6,2},{8,4},{10,6},{12,8},{14,10},{1,13},{3,15... | collective-permute-start | bytes 442376 | tf_op jit(solution)/shard_map/ppermute | solution.py:236
  192.7 3.7 %collective-permute-start.22 = (bf16[72,1024]{1,0:T(8,128)(2,1)S(1)}, bf16[72,1024]{1,0:T(8,128)(2,1)S(1)}, u32[]{:S(2)}, u32[]{:S(2)}) collective-permute-start(bf16[72,1024]{1,0:T(8,128)(2,1)S(1)} %copy-done.14), channel_id=1, source_target_pairs={{0,14},{2,0},{4,2},{6,4},{8,6},{10,8},{12,10},{14,12},{1,15},{3,1}... | collective-permute-start | bytes 442376 | tf_op jit(solution)/shard_map/ppermute | solution.py:236
  196.5 7.0 %collective-permute-start.18 = (bf16[72,1024]{1,0:T(8,128)(2,1)S(1)}, bf16[72,1024]{1,0:T(8,128)(2,1)S(1)}, u32[]{:S(2)}, u32[]{:S(2)}) collective-permute-start(bf16[72,1024]{1,0:T(8,128)(2,1)S(1)} %add_convert_fusion.1), channel_id=1, source_target_pairs={{0,10},{2,12},{4,14},{6,0},{8,2},{10,4},{12,6},{14,8},{1,11},{3,13... | collective-permute-start | bytes 442376 | tf_op jit(solution)/shard_map/ppermute | solution.py:236
  203.5 3.0 %shard_map.88 = bf16[72,1024]{1,0:T(8,128)(2,1)} custom-call(bf16[16,40,128]{2,1,0:T(8,128)(2,1)} %copy-done.2, bf16[1024,1024]{1,0:T(8,128)(2,1)} %bitcast.24), custom_call_target="tpu_custom_call" | custom-call | flops 150994944 | tf_op jit(solution)/shard_map/pallas_call | solution.py:331
  206.6 4.9 %collective-permute-done.18 = bf16[72,1024]{1,0:T(8,128)(2,1)S(1)} collective-permute-done((bf16[72,1024]{1,0:T(8,128)(2,1)S(1)}, bf16[72,1024]{1,0:T(8,128)(2,1)S(1)}, u32[]{:S(2)}, u32[]{:S(2)}) %collective-permute-start.18) | collective-permute-done | bytes 147488 | tf_op jit(solution)/shard_map/ppermute | solution.py:236
  (99 shorter events, 32.9 us)
Async XLA Ops:
  0.6 38.1 %copy-start.3 = (bf16[1,1024,192]{1,2,0:T(8,128)(2,1)S(1)}, bf16[1,1024,192]{1,2,0:T(8,128)(2,1)}, u32[]{:S(2)}) copy-start(bf16[1,1024,192]{1,2,0:T(8,128)(2,1)} %param.8) | copy-start | bytes 1179652
  0.6 18.9 %collective-permute-start.2 = (bf16[72,1024]{1,0:T(8,128)(2,1)}, bf16[72,1024]{1,0:T(8,128)(2,1)S(1)}, u32[]{:S(2)}, u32[]{:S(2)}) collective-permute-start(bf16[72,1024]{1,0:T(8,128)(2,1)} %bitcast.34), channel_id=1, source_target_pairs={{0,4},{2,6},{4,8},{6,10},{8,12},{10,14},{12,0},{14,2},{1,5},{3,7},... | collective-permute-start | bytes 442376 | tf_op jit(solution)/shard_map/ppermute | solution.py:236
  6.9 21.5 %collective-permute-start.3 = (bf16[72,1024]{1,0:T(8,128)(2,1)}, bf16[72,1024]{1,0:T(8,128)(2,1)S(1)}, u32[]{:S(2)}, u32[]{:S(2)}) collective-permute-start(bf16[72,1024]{1,0:T(8,128)(2,1)} %bitcast.35), channel_id=1, source_target_pairs={{0,12},{2,14},{4,0},{6,2},{8,4},{10,6},{12,8},{14,10},{1,13},{3,15... | collective-permute-start | bytes 442376 | tf_op jit(solution)/shard_map/ppermute | solution.py:236
  12.7 17.5 %collective-permute-start = (bf16[72,1024]{1,0:T(8,128)(2,1)}, bf16[72,1024]{1,0:T(8,128)(2,1)S(1)}, u32[]{:S(2)}, u32[]{:S(2)}) collective-permute-start(bf16[72,1024]{1,0:T(8,128)(2,1)} %bitcast.36), channel_id=1, source_target_pairs={{0,2},{2,4},{4,6},{6,8},{8,10},{10,12},{12,14},{14,0},{1,3},{3,5},... | collective-permute-start | bytes 442376 | tf_op jit(solution)/shard_map/ppermute | solution.py:236
  14.7 15.6 %collective-permute-start.1 = (bf16[72,1024]{1,0:T(8,128)(2,1)}, bf16[72,1024]{1,0:T(8,128)(2,1)S(1)}, u32[]{:S(2)}, u32[]{:S(2)}) collective-permute-start(bf16[72,1024]{1,0:T(8,128)(2,1)} %bitcast.37), channel_id=1, source_target_pairs={{0,14},{2,0},{4,2},{6,4},{8,6},{10,8},{12,10},{14,12},{1,15},{3,1}... | collective-permute-start | bytes 442376 | tf_op jit(solution)/shard_map/ppermute | solution.py:236
  19.5 15.9 %collective-permute-start.6 = (bf16[72,1024]{1,0:T(8,128)(2,1)S(1)}, bf16[72,1024]{1,0:T(8,128)(2,1)S(1)}, u32[]{:S(2)}, u32[]{:S(2)}) collective-permute-start(bf16[72,1024]{1,0:T(8,128)(2,1)S(1)} %collective-permute-done.2), channel_id=1, source_target_pairs={{0,4},{2,6},{4,8},{6,10},{8,12},{10,14},{12,0},{14,2},{1,5},{3,7},... | collective-permute-start | bytes 442376 | tf_op jit(solution)/shard_map/ppermute | solution.py:236
  23.2 9.4 %collective-permute-start.4 = (bf16[72,1024]{1,0:T(8,128)(2,1)S(1)}, bf16[72,1024]{1,0:T(8,128)(2,1)S(1)}, u32[]{:S(2)}, u32[]{:S(2)}) collective-permute-start(bf16[72,1024]{1,0:T(8,128)(2,1)S(1)} %collective-permute-done.2), channel_id=1, source_target_pairs={{0,2},{2,4},{4,6},{6,8},{8,10},{10,12},{12,14},{14,0},{1,3},{3,5},... | collective-permute-start | bytes 442376 | tf_op jit(solution)/shard_map/ppermute | solution.py:236
  28.4 7.0 %collective-permute-start.5 = (bf16[72,1024]{1,0:T(8,128)(2,1)S(1)}, bf16[72,1024]{1,0:T(8,128)(2,1)S(1)}, u32[]{:S(2)}, u32[]{:S(2)}) collective-permute-start(bf16[72,1024]{1,0:T(8,128)(2,1)S(1)} %collective-permute-done.3), channel_id=1, source_target_pairs={{0,14},{2,0},{4,2},{6,4},{8,6},{10,8},{12,10},{14,12},{1,15},{3,1}... | collective-permute-start | bytes 442376 | tf_op jit(solution)/shard_map/ppermute | solution.py:236
  35.5 81.0 %collective-permute-start.23 = (bf16[576,1024]{1,0:T(8,128)(2,1)S(1)}, bf16[576,1024]{1,0:T(8,128)(2,1)S(1)}, u32[]{:S(2)}, u32[]{:S(2)}) collective-permute-start(bf16[576,1024]{1,0:T(8,128)(2,1)S(1)} %constant_dynamic-update-slice_fusion.tokens_ref), channel_id=1, source_target_pairs={{0,1},{1,0},{2,3},{3,2},{4,5},{5,4},{6,7},{7,6},{8,9},{9,8},{10,11... | collective-permute-start | bytes 3538952 | tf_op jit(solution)/shard_map/ppermute | solution.py:236
  38.7 33.1 %collective-permute-start.7 = (bf16[192,1024]{1,0:T(8,128)(2,1)S(1)}, bf16[192,1024]{1,0:T(8,128)(2,1)S(1)}, u32[]{:S(2)}, u32[]{:S(2)}) collective-permute-start(bf16[192,1024]{1,0:T(8,128)(2,1)S(1)} %bitcast.30), channel_id=1, source_target_pairs={{0,1},{1,0},{2,3},{3,2},{4,5},{5,4},{6,7},{7,6},{8,9},{9,8},{10,11... | collective-permute-start | bytes 1179656 | tf_op jit(solution)/shard_map/ppermute | solution.py:236
  44.6 46.7 %all-to-all-start = ((bf16[16,40,128]{2,1,0:T(8,128)(2,1)}), bf16[16,40,128]{2,1,0:T(8,128)(2,1)S(1)}, u32[]{:S(2)}, u32[]{:S(2)}) async-start(bf16[16,40,128]{2,1,0:T(8,128)(2,1)} %shard_map.86), calls=%async_computation | async-start | bytes 327680 | tf_op jit(solution)/shard_map/all_to_all | solution.py:240
  75.7 18.9 %collective-permute-start.8 = (bf16[8,72,192]{2,1,0:T(8,128)(2,1)}, bf16[8,72,192]{2,1,0:T(8,128)(2,1)S(1)}, u32[]{:S(2)}, u32[]{:S(2)}) collective-permute-start(bf16[8,72,192]{2,1,0:T(8,128)(2,1)} %get-tuple-element.28), channel_id=1, source_target_pairs={{0,1},{1,0},{2,3},{3,2},{4,5},{5,4},{6,7},{7,6},{8,9},{9,8},{10,11... | collective-permute-start | bytes 663560 | tf_op jit(solution)/shard_map/ppermute | solution.py:236
  79.0 9.7 %collective-permute-start.9 = (bf16[4,72,128]{2,1,0:T(8,128)(2,1)}, bf16[4,72,128]{2,1,0:T(8,128)(2,1)S(1)}, u32[]{:S(2)}, u32[]{:S(2)}) collective-permute-start(bf16[4,72,128]{2,1,0:T(8,128)(2,1)} %get-tuple-element.29), channel_id=1, source_target_pairs={{0,496},{1,497},{16,32},{17,33},{32,16},{33,17},{48,64},{49,65},{6... | collective-permute-start | bytes 221192 | tf_op jit(solution)/shard_map/ppermute | solution.py:346
  80.9 10.4 %collective-permute-start.10 = (bf16[4,72,128]{2,1,0:T(8,128)(2,1)}, bf16[4,72,128]{2,1,0:T(8,128)(2,1)S(1)}, u32[]{:S(2)}, u32[]{:S(2)}) collective-permute-start(bf16[4,72,128]{2,1,0:T(8,128)(2,1)} %get-tuple-element.30), channel_id=1, source_target_pairs={{0,16},{16,0},{1,17},{17,1},{2,18},{18,2},{3,19},{19,3},{4,20},{20... | collective-permute-start | bytes 221192 | tf_op jit(solution)/shard_map/ppermute | solution.py:236
  83.7 8.9 %collective-permute-start.11 = (bf16[4,72,128]{2,1,0:T(8,128)(2,1)}, bf16[4,72,128]{2,1,0:T(8,128)(2,1)S(1)}, u32[]{:S(2)}, u32[]{:S(2)}) collective-permute-start(bf16[4,72,128]{2,1,0:T(8,128)(2,1)} %get-tuple-element.31), channel_id=1, source_target_pairs={{0,497},{1,496},{16,33},{17,32},{32,17},{33,16},{48,65},{49,64},{6... | collective-permute-start | bytes 221192 | tf_op jit(solution)/shard_map/ppermute | solution.py:346
  88.7 5.9 %collective-permute-start.12 = (bf16[4,72,128]{2,1,0:T(8,128)(2,1)}, bf16[4,72,128]{2,1,0:T(8,128)(2,1)S(1)}, u32[]{:S(2)}, u32[]{:S(2)}) collective-permute-start(bf16[4,72,128]{2,1,0:T(8,128)(2,1)} %get-tuple-element.32), channel_id=1, source_target_pairs={{0,17},{1,16},{16,1},{17,0},{32,49},{33,48},{48,33},{49,32},{64,81... | collective-permute-start | bytes 221192 | tf_op jit(solution)/shard_map/ppermute | solution.py:351
  103.7 9.4 %collective-permute-start.13 = (bf16[8,72,128]{2,1,0:T(8,128)(2,1)}, bf16[8,72,128]{2,1,0:T(8,128)(2,1)S(1)}, u32[]{:S(2)}, u32[]{:S(2)}) collective-permute-start(bf16[8,72,128]{2,1,0:T(8,128)(2,1)} %get-tuple-element.36), channel_id=1, source_target_pairs={{0,496},{1,497},{16,32},{17,33},{32,16},{33,17},{48,64},{49,65},{6... | collective-permute-start | bytes 442376 | tf_op jit(solution)/shard_map/ppermute | solution.py:346
  107.0 6.1 %collective-permute-start.14 = (bf16[8,72,128]{2,1,0:T(8,128)(2,1)}, bf16[8,72,128]{2,1,0:T(8,128)(2,1)S(1)}, u32[]{:S(2)}, u32[]{:S(2)}) collective-permute-start(bf16[8,72,128]{2,1,0:T(8,128)(2,1)} %get-tuple-element.37), channel_id=1, source_target_pairs={{0,16},{16,0},{1,17},{17,1},{2,18},{18,2},{3,19},{19,3},{4,20},{20... | collective-permute-start | bytes 442376 | tf_op jit(solution)/shard_map/ppermute | solution.py:236
  117.5 33.1 %copy-start.12 = (bf16[8,72,192]{2,1,0:T(8,128)(2,1)S(1)}, bf16[8,72,192]{2,1,0:T(8,128)(2,1)}, u32[]{:S(2)}) copy-start(bf16[8,72,192]{2,1,0:T(8,128)(2,1)} %get-tuple-element.39) | copy-start | bytes 663556
  117.5 35.6 %copy-start.23 = (s32[8]{0:T(128)S(1)}, s32[8]{0:T(128)}, u32[]{:S(2)}) copy-start(s32[8]{0:T(128)} %constant.44.clone) | copy-start | bytes 100
  140.5 26.5 %all-to-all-start.1 = ((bf16[16,40,128]{2,1,0:T(8,128)(2,1)}), bf16[16,40,128]{2,1,0:T(8,128)(2,1)S(1)}, u32[]{:S(2)}, u32[]{:S(2)}) async-start(bf16[16,40,128]{2,1,0:T(8,128)(2,1)} %get-tuple-element.33), calls=%async_computation.1 | async-start | bytes 327680 | tf_op jit(solution)/shard_map/all_to_all | solution.py:240
  150.5 10.2 %collective-permute-start.15 = (bf16[8,72,192]{2,1,0:T(8,128)(2,1)S(1)}, bf16[8,72,192]{2,1,0:T(8,128)(2,1)S(1)}, u32[]{:S(2)}, u32[]{:S(2)}) collective-permute-start(bf16[8,72,192]{2,1,0:T(8,128)(2,1)S(1)} %copy-done.12), channel_id=1, source_target_pairs={{0,1},{1,0},{2,3},{3,2},{4,5},{5,4},{6,7},{7,6},{8,9},{9,8},{10,11... | collective-permute-start | bytes 663560 | tf_op jit(solution)/shard_map/ppermute | solution.py:236
  164.3 32.1 %copy-start.7 = (bf16[72,1024]{1,0:T(8,128)(2,1)S(1)}, bf16[72,1024]{1,0:T(8,128)(2,1)}, u32[]{:S(2)}) copy-start(bf16[72,1024]{1,0:T(8,128)(2,1)} %get-tuple-element.41) | copy-start | bytes 442372
  164.3 28.4 %collective-permute-start.17 = (bf16[72,1024]{1,0:T(8,128)(2,1)}, bf16[72,1024]{1,0:T(8,128)(2,1)S(1)}, u32[]{:S(2)}, u32[]{:S(2)}) collective-permute-start(bf16[72,1024]{1,0:T(8,128)(2,1)} %get-tuple-element.42), channel_id=1, source_target_pairs={{0,14},{2,0},{4,2},{6,4},{8,6},{10,8},{12,10},{14,12},{1,15},{3,1}... | collective-permute-start | bytes 442376 | tf_op jit(solution)/shard_map/ppermute | solution.py:236
  167.0 36.5 %copy-start.2 = (bf16[16,40,128]{2,1,0:T(8,128)(2,1)}, bf16[16,40,128]{2,1,0:T(8,128)(2,1)S(1)}, u32[]{:S(2)}) copy-start(bf16[16,40,128]{2,1,0:T(8,128)(2,1)S(1)} %all-to-all-done.1.att_ref) | copy-start | bytes 491524
  167.9 44.5 %all-to-all-start.3 = ((bf16[32,48,128]{2,1,0:T(8,128)(2,1)}), bf16[32,48,128]{2,1,0:T(8,128)(2,1)S(1)}, u32[]{:S(2)}, u32[]{:S(2)}) async-start(bf16[32,48,128]{2,1,0:T(8,128)(2,1)} %broadcast_in_dim.12), calls=%async_computation.3 | async-start | bytes 786432 | tf_op jit(solution)/shard_map/all_to_all | solution.py:240
  176.2 20.3 %collective-permute-start.16 = (bf16[72,1024]{1,0:T(8,128)(2,1)S(1)}, bf16[72,1024]{1,0:T(8,128)(2,1)S(1)}, u32[]{:S(2)}, u32[]{:S(2)}) collective-permute-start(bf16[72,1024]{1,0:T(8,128)(2,1)S(1)} %copy-done.18), channel_id=1, source_target_pairs={{0,6},{2,8},{4,10},{6,12},{8,14},{10,0},{12,2},{14,4},{1,7},{3,9},... | collective-permute-start | bytes 442376 | tf_op jit(solution)/shard_map/ppermute | solution.py:236
  182.6 24.0 %collective-permute-start.19 = (bf16[72,1024]{1,0:T(8,128)(2,1)S(1)}, bf16[72,1024]{1,0:T(8,128)(2,1)S(1)}, u32[]{:S(2)}, u32[]{:S(2)}) collective-permute-start(bf16[72,1024]{1,0:T(8,128)(2,1)S(1)} %copy-done.17), channel_id=1, source_target_pairs={{0,4},{2,6},{4,8},{6,10},{8,12},{10,14},{12,0},{14,2},{1,5},{3,7},... | collective-permute-start | bytes 442376 | tf_op jit(solution)/shard_map/ppermute | solution.py:236
  186.0 20.6 %collective-permute-start.20 = (bf16[72,1024]{1,0:T(8,128)(2,1)S(1)}, bf16[72,1024]{1,0:T(8,128)(2,1)S(1)}, u32[]{:S(2)}, u32[]{:S(2)}) collective-permute-start(bf16[72,1024]{1,0:T(8,128)(2,1)S(1)} %copy-done.16), channel_id=1, source_target_pairs={{0,12},{2,14},{4,0},{6,2},{8,4},{10,6},{12,8},{14,10},{1,13},{3,15... | collective-permute-start | bytes 442376 | tf_op jit(solution)/shard_map/ppermute | solution.py:236
  190.5 16.0 %collective-permute-start.21 = (bf16[72,1024]{1,0:T(8,128)(2,1)S(1)}, bf16[72,1024]{1,0:T(8,128)(2,1)S(1)}, u32[]{:S(2)}, u32[]{:S(2)}) collective-permute-start(bf16[72,1024]{1,0:T(8,128)(2,1)S(1)} %copy-done.15), channel_id=1, source_target_pairs={{0,2},{2,4},{4,6},{6,8},{8,10},{10,12},{12,14},{14,0},{1,3},{3,5},... | collective-permute-start | bytes 442376 | tf_op jit(solution)/shard_map/ppermute | solution.py:236
  192.7 13.8 %collective-permute-start.22 = (bf16[72,1024]{1,0:T(8,128)(2,1)S(1)}, bf16[72,1024]{1,0:T(8,128)(2,1)S(1)}, u32[]{:S(2)}, u32[]{:S(2)}) collective-permute-start(bf16[72,1024]{1,0:T(8,128)(2,1)S(1)} %copy-done.14), channel_id=1, source_target_pairs={{0,14},{2,0},{4,2},{6,4},{8,6},{10,8},{12,10},{14,12},{1,15},{3,1}... | collective-permute-start | bytes 442376 | tf_op jit(solution)/shard_map/ppermute | solution.py:236
  196.5 15.0 %collective-permute-start.18 = (bf16[72,1024]{1,0:T(8,128)(2,1)S(1)}, bf16[72,1024]{1,0:T(8,128)(2,1)S(1)}, u32[]{:S(2)}, u32[]{:S(2)}) collective-permute-start(bf16[72,1024]{1,0:T(8,128)(2,1)S(1)} %add_convert_fusion.1), channel_id=1, source_target_pairs={{0,10},{2,12},{4,14},{6,0},{8,2},{10,4},{12,6},{14,8},{1,11},{3,13... | collective-permute-start | bytes 442376 | tf_op jit(solution)/shard_map/ppermute | solution.py:236
  (19 other events, 152.6 us)

commit v4 on v3

--- a/solution.py
+++ b/solution.py
@@ -87,14 +87,14 @@
 
 
 def project_kernel(
-    table_ref, tokens_ref, own_ref, other_ref,
+    table_ref, t0_ref, t1_ref, t2_ref, t3_ref, own_ref, other_ref,
     kv_ref, q_ref, swap_ref, far_ref, near_ref, far2_ref, near2_ref,
     kv32, kv32b,
 ):
     first_core = table_ref[8] == 0
     own, other = turned(own_ref), turned(other_ref)
-    for chunk in range(2):
-        rows = tokens_ref[chunk * 288 : (chunk + 1) * 288, :]
+    for chunk, (a_ref, b_ref) in enumerate(((t0_ref, t1_ref), (t2_ref, t3_ref))):
+        rows = jnp.concatenate([a_ref[...], b_ref[...]], axis=0)
         proj = dot_nt(rows, own).astype(BF16).astype(F32)
         proj2 = dot_nt(rows, other).astype(BF16).astype(F32)
         for part in range(4):
@@ -183,7 +183,7 @@
 
 
 def combine_kernel(
-    place_ref, dq_ref, dkv_ref, far_ref, near_ref, pg_ref, mine_ref, swap_ref, pg32
+    place_ref, dq_ref, dkv_ref, far_ref, near_ref, mine_ref, swap_ref, pg32
 ):
     yl = place_ref[0]
     first_core = place_ref[1] == 0
@@ -193,7 +193,6 @@
         span = slice(8 * half, 8 * half + 8)
         pg32[span, :, 0:128] = dkv_ref[span] + add
         pg32[span, :, 128:192] = dq_ref[span]
-    pg_ref[...] = pg32[...].astype(BF16)
     for row in range(8):
         mine_ref[row] = pg32[2 * row + yl].astype(BF16)
         swap_ref[row] = pg32[2 * row + 1 - yl].astype(BF16)
@@ -205,25 +204,36 @@
         picks = [table_ref[4 * chunk + i] for i in range(4)]
         rows = jnp.concatenate([mine_ref[p].astype(F32) for p in picks], axis=0).astype(BF16)
         rows2 = jnp.concatenate([got_ref[p].astype(F32) for p in picks], axis=0).astype(BF16)
-        part = dot_nn(rows, own) + dot_nn(rows2, other)
-        for i in range(4):
-            out_refs[4 * chunk + i][...] = part[i * TOK : (i + 1) * TOK].astype(BF16)
-
-
-def weight_grad_kernel(table_ref, tokens_ref, tokens2_ref, pg_ref, piece_ref):
+        part = (dot_nn(rows, own) + dot_nn(rows2, other)).astype(BF16)
+        if chunk == 0:
+            out_refs[0][...] = part[: 2 * TOK]
+            out_refs[1][...] = part[2 * TOK :]
+        else:
+            for i in range(4):
+                out_refs[2 + i][...] = part[i * TOK : (i + 1) * TOK]
+
+
+def weight_grad_kernel(table_ref, pg_ref, t0_ref, t1_ref, t2_ref, t3_ref, out_ref):
     total = None
-    for chunk in range(4):
+    for chunk, (a_ref, b_ref) in enumerate(((t0_ref, t1_ref), (t2_ref, t3_ref))):
         rows = jnp.concatenate(
             [pg_ref[table_ref[4 * chunk + i]].astype(F32) for i in range(4)], axis=0
         ).astype(BF16)
-        source = tokens_ref if chunk < 2 else tokens2_ref
-        span = slice((chunk % 2) * 288, (chunk % 2) * 288 + 288)
-        part = dot_tn(rows, source[span, :])
+        part = dot_tn(rows, jnp.concatenate([a_ref[...], b_ref[...]], axis=0))
         total = part if total is None else total + part
-    total = jnp.concatenate([total[128:192], total[0:128]], axis=0).astype(BF16)
+    out_ref[...] = total.astype(out_ref.dtype)
+
+
+def piece_kernel(own_ref, got_ref, piece_ref):
     for g in range(4):
-        for j in range(8):
-            piece_ref[8 * g + j] = total[48 * g : 48 * g + 48, 128 * j : 128 * j + 128]
+        for start in range(48 * g, 48 * g + 48, 16):
+            row = (start + 128) % 192
+            span = slice(row, row + 16)
+            both = (own_ref[span] + got_ref[span].astype(F32)).astype(BF16)
+            for j in range(8):
+                piece_ref[8 * g + j, start - 48 * g : start - 48 * g + 16] = both[
+                    :, 128 * j : 128 * j + 128
+                ]
 
 
 def mix_kernel(att_ref, weight_ref, out_ref):
@@ -245,13 +255,14 @@
     z, yl, core = (lax.axis_index(a).astype(jnp.int32) for a in ("z", "yl", "core"))
     mine = latents.reshape(TOK, width)
     own = jnp.swapaxes(qkv_weight[0], 0, 1)
-    d1, d7, d2, d6 = (shift(mine, "z", 8, d) for d in (1, 7, 2, 6))
     other = shift(own, "yl", 2, 1)
-    d3, d5 = shift(d2, "z", 8, 1), shift(d6, "z", 8, -1)
-    d4 = shift(d2, "z", 8, 2)
-    tokens = jnp.concatenate([mine, d1, d7, d2, d6, d3, d5, d4], axis=0)
-    tokens2 = shift(tokens, "yl", 2, 1)
-    distance = jnp.array([0, 1, 7, 2, 6, 3, 5, 4], jnp.int32)
+    d7, d2, d1 = (shift(mine, "z", 8, d) for d in (7, 2, 1))
+    pair0 = jnp.concatenate([mine, d7], axis=0)
+    pair1 = jnp.concatenate([d1, d2], axis=0)
+    pair2 = shift(pair0, "z", 8, -2)
+    pair3 = shift(pair1, "z", 8, 2)
+    tokens = (pair0, pair1, pair2, pair3)
+    distance = jnp.array([0, 7, 1, 2, 6, 5, 3, 4], jnp.int32)
     rows = ((z - distance) % 8).astype(jnp.int32)
     place = jnp.stack([yl, core])
 
@@ -266,9 +277,9 @@
         + [((4, TOK, 128), BF16)] * 4,
         scratch=[pltpu.VMEM((8, TOK, 128), F32)] * 2,
         smem=(0,),
-        n_in=4,
+        n_in=7,
         flops=2 * 1152 * 192 * width,
-    )(jnp.concatenate([rows, core.reshape(1)]), tokens, own, other)
+    )(jnp.concatenate([rows, core.reshape(1)]), *tokens, own, other)
     far, near = send_far(far), shift(near, "core", 2, 1)
     far2, near2 = send_far(far2, 1), send_near(near2, 1)
     swapped = shift(swap, "yl", 2, 1)
@@ -294,38 +305,44 @@
     grad_far, grad_near = send_far(grad_far), shift(grad_near, "core", 2, 1)
     token_att = exchange(attended, HEAD)
 
-    pg, pg_mine, pg_swap = call(
+    pg_mine, pg_swap = call(
         combine_kernel,
-        [((RANKS, TOK, 3 * HD), BF16), ((8, TOK, 3 * HD), BF16), ((8, TOK, 3 * HD), BF16)],
+        [((8, TOK, 3 * HD), BF16), ((8, TOK, 3 * HD), BF16)],
         scratch=[pltpu.VMEM((RANKS, TOK, 3 * HD), F32)],
         smem=(0,),
         n_in=5,
         flops=1 << 20,
     )(place, dq, dkv, grad_far, grad_near)
     pg_got = shift(pg_swap, "yl", 2, 1)
-    (pieces,) = call(
-        weight_grad_kernel,
-        [((32, 48, 128), BF16)],
-        smem=(0,),
-        n_in=4,
-        flops=2 * 1152 * 192 * width,
-    )(
-        jnp.concatenate([2 * rows + yl, 2 * rows + 1 - yl]).astype(jnp.int32),
-        tokens, tokens2, pg,
+    grads = []
+    for pg, dtype in ((pg_mine, F32), (pg_got, BF16)):
+        grads += call(
+            weight_grad_kernel,
+            [((3 * HD, width), dtype)],
+            smem=(0,),
+            n_in=6,
+            flops=2 * 576 * 192 * width,
+        )(rows, pg, *tokens)
+    grad_got = shift(grads[1], "yl", 2, 1)
+    (pieces,) = call(piece_kernel, [((32, 48, 128), BF16)], n_in=2, flops=1 << 20)(
+        grads[0], grad_got
     )
     pieces = exchange(pieces, LON)
-    reach = (4, 3, 5, 2, 6, 1, 7, 0)
+    reach = (5, 4, 3, 2, 6, 7, 1, 0)
     shares = call(
         share_kernel,
-        [((TOK, width), BF16)] * 8,
+        [((2 * TOK, width), BF16)] * 2 + [((TOK, width), BF16)] * 4,
         smem=(0,),
         n_in=5,
         flops=2 * 576 * 384 * width,
     )(((z + jnp.array(reach, jnp.int32)) % 8).astype(jnp.int32), pg_mine, pg_got, own, other)
-    passed = shift(shares[0], "z", 8, -1)
-    shares = list(shares[1:])
-    shares[1] = (shares[1].astype(F32) + passed.astype(F32)).astype(BF16)
-    shares = [shift(s, "z", 8, d) if d else s for s, d in zip(shares, reach[1:])]
+    down, up, s6, s7, s1, s0 = shares
+    down, up = shift(down, "z", 8, -2), shift(up, "z", 8, 2)
+    s7 = (s7.astype(F32) + down[:TOK].astype(F32)).astype(BF16)
+    s6 = (s6.astype(F32) + down[TOK:].astype(F32)).astype(BF16)
+    s1 = (s1.astype(F32) + up[:TOK].astype(F32)).astype(BF16)
+    shares = [shift(s6, "z", 8, -2), shift(s7, "z", 8, -1)]
+    shares = [s0, up[TOK:], shift(s1, "z", 8, 1)] + shares
     summed = jnp.sum(pieces.astype(F32), axis=0).astype(BF16)
     copies = exchange(jnp.broadcast_to(summed[None], (32, 48, 128)), LON)
     (mixed,) = call(mix_kernel, [((TOK, width), BF16)], n_in=2, flops=2 * TOK * width * width)(

time: 215 us -> 199 us (0.926)
  the two profiles are of different devices: /device:TPU:104 before, /device:TPU:1 now
where the time goes in v4:
time: 199 us; the launch traced here: 197 us
  starting transfers between devices  109 us (55%)
  waiting for transfers between devices  47 us (24%)
  Pallas kernels  30.6 us (15%)
  local copies, waits for them, and re-layouts  5.83 us (3%)
  other arithmetic  3.73 us (2%)
    ppermute x16, starting transfers between devices, shift(): lax.ppermute(value, axis, [(i, (i + distance) % size) for i in range(size)])  59.6 us
    all_to_all x4, starting transfers between devices, exchange(): return lax.all_to_all(value, axis, 0, 0, tiled=True)  32.4 us
    ppermute x16, waiting for transfers between devices, shift(): lax.ppermute(value, axis, [(i, (i + distance) % size) for i in range(size)])  27.9 us
    all_to_all x4, waiting for transfers between devices, exchange(): return lax.all_to_all(value, axis, 0, 0, tiled=True)  14.7 us
    ppermute x3, starting transfers between devices, send_far(): return lax.ppermute(value, LON + ('yl',), routes)  14.4 us
    pallas_call x1, Pallas kernels, step(): call(attend_kernel, [((RANKS, 40, 128), BF16), ((RANKS, TOK, HD), F32), (...  8.35 us
    pallas_call x2, Pallas kernels, step(): call(weight_grad_kernel, [((3 * HD, width), dtype)], smem=(0,), n_in=6, f...  5.51 us
    unnamed x50, local copies, waits for them, and re-layouts  4.78 us
  transfers between devices with their start and end apart: 24, of which 11 were waited for; matrix products, arithmetic and copies ran while one was open for 2% of the time, Pallas kernels for 8%

profile of v4, /device:TPU:1, one launch (start us, length us, event | category | flops | bytes accessed | tf_op | source)
XLA Modules:
  0.0 197.4 jit_solution(17632286409586194671)
XLA Ops:
  0.7 11.6 %collective-permute-start = (bf16[72,1024]{1,0:T(8,128)(2,1)}, bf16[72,1024]{1,0:T(8,128)(2,1)S(1)}, u32[]{:S(2)}, u32[]{:S(2)}) collective-permute-start(bf16[72,1024]{1,0:T(8,128)(2,1)} %bitcast.34), channel_id=1, source_target_pairs={{0,14},{2,0},{4,2},{6,4},{8,6},{10,8},{12,10},{14,12},{1,15},{3,1}... | collective-permute-start | bytes 442376 | tf_op jit(solution)/shard_map/ppermute | solution.py:246
  16.1 3.3 %shard_map.86 = bf16[16,40,128]{2,1,0:T(8,128)(2,1)} custom-call(bf16[72,1024]{1,0:T(8,128)(2,1)} %bitcast.31, bf16[16,64,1024]{2,1,0:T(8,128)(2,1)} %weight_ref.1), custom_call_target="tpu_custom_call" | custom-call | flops 150994944 | tf_op jit(solution)/shard_map/pallas_call | solution.py:269
  19.4 7.1 %all-to-all-start = ((bf16[16,40,128]{2,1,0:T(8,128)(2,1)}), bf16[16,40,128]{2,1,0:T(8,128)(2,1)S(1)}, u32[]{:S(2)}, u32[]{:S(2)}) async-start(bf16[16,40,128]{2,1,0:T(8,128)(2,1)} %shard_map.86), calls=%async_computation | async-start | bytes 327680 | tf_op jit(solution)/shard_map/all_to_all | solution.py:250
  26.5 3.3 %collective-permute-start.5 = (bf16[192,1024]{1,0:T(8,128)(2,1)S(1)}, bf16[192,1024]{1,0:T(8,128)(2,1)S(1)}, u32[]{:S(2)}, u32[]{:S(2)}) collective-permute-start(bf16[192,1024]{1,0:T(8,128)(2,1)S(1)} %bitcast.30), channel_id=1, source_target_pairs={{0,1},{1,0},{2,3},{3,2},{4,5},{5,4},{6,7},{7,6},{8,9},{9,8},{10,11... | collective-permute-start | bytes 1179656 | tf_op jit(solution)/shard_map/ppermute | solution.py:246
  29.9 5.2 %collective-permute-start.3 = (bf16[144,1024]{1,0:T(8,128)(2,1)S(1)}, bf16[144,1024]{1,0:T(8,128)(2,1)S(1)}, u32[]{:S(2)}, u32[]{:S(2)}) collective-permute-start(bf16[144,1024]{1,0:T(8,128)(2,1)S(1)} %pad_maximum_fusion.t0_ref), channel_id=1, source_target_pairs={{0,12},{2,14},{4,0},{6,2},{8,4},{10,6},{12,8},{14,10},{1,13},{3,15... | collective-permute-start | bytes 884744 | tf_op jit(solution)/shard_map/ppermute | solution.py:246
  39.1 8.8 %collective-permute-done.3.t2_ref = bf16[144,1024]{1,0:T(8,128)(2,1)S(1)} collective-permute-done((bf16[144,1024]{1,0:T(8,128)(2,1)S(1)}, bf16[144,1024]{1,0:T(8,128)(2,1)S(1)}, u32[]{:S(2)}, u32[]{:S(2)}) %collective-permute-start.3) | collective-permute-done | bytes 294944 | tf_op jit(solution)/shard_map/ppermute | solution.py:246
  49.3 3.2 %shard_map.85 = (bf16[8,72,128]{2,1,0:T(8,128)(2,1)}, bf16[8,72,64]{2,1,0:T(8,128)(2,1)}, bf16[8,72,192]{2,1,0:T(8,128)(2,1)}, bf16[4,72,128]{2,1,0:T(8,128)(2,1...) custom-call(s32[9]{0:T(128)} %pad_add_fusion.1.table_ref, ...), custom_call_target="tpu_custom_call" | custom-call | flops 452984832 | tf_op jit(solution)/shard_map/pallas_call | solution.py:274
  54.6 7.1 %collective-permute-start.7 = (bf16[4,72,128]{2,1,0:T(8,128)(2,1)}, bf16[4,72,128]{2,1,0:T(8,128)(2,1)S(1)}, u32[]{:S(2)}, u32[]{:S(2)}) collective-permute-start(bf16[4,72,128]{2,1,0:T(8,128)(2,1)} %get-tuple-element.26), channel_id=1, source_target_pairs={{0,496},{1,497},{16,32},{17,33},{32,16},{33,17},{48,64},{49,65},{6... | collective-permute-start | bytes 221192 | tf_op jit(solution)/shard_map/ppermute | solution.py:363
  61.7 2.4 %collective-permute-start.8 = (bf16[4,72,128]{2,1,0:T(8,128)(2,1)}, bf16[4,72,128]{2,1,0:T(8,128)(2,1)S(1)}, u32[]{:S(2)}, u32[]{:S(2)}) collective-permute-start(bf16[4,72,128]{2,1,0:T(8,128)(2,1)} %get-tuple-element.27), channel_id=1, source_target_pairs={{0,16},{16,0},{1,17},{17,1},{2,18},{18,2},{3,19},{19,3},{4,20},{20... | collective-permute-start | bytes 221192 | tf_op jit(solution)/shard_map/ppermute | solution.py:246
  64.1 5.4 %collective-permute-start.9 = (bf16[4,72,128]{2,1,0:T(8,128)(2,1)}, bf16[4,72,128]{2,1,0:T(8,128)(2,1)S(1)}, u32[]{:S(2)}, u32[]{:S(2)}) collective-permute-start(bf16[4,72,128]{2,1,0:T(8,128)(2,1)} %get-tuple-element.28), channel_id=1, source_target_pairs={{0,497},{1,496},{16,33},{17,32},{32,17},{33,16},{48,65},{49,64},{6... | collective-permute-start | bytes 221192 | tf_op jit(solution)/shard_map/ppermute | solution.py:363
  69.5 2.8 %collective-permute-start.10 = (bf16[4,72,128]{2,1,0:T(8,128)(2,1)}, bf16[4,72,128]{2,1,0:T(8,128)(2,1)S(1)}, u32[]{:S(2)}, u32[]{:S(2)}) collective-permute-start(bf16[4,72,128]{2,1,0:T(8,128)(2,1)} %get-tuple-element.29), channel_id=1, source_target_pairs={{0,17},{1,16},{16,1},{17,0},{32,49},{33,48},{48,33},{49,32},{64,81... | collective-permute-start | bytes 221192 | tf_op jit(solution)/shard_map/ppermute | solution.py:368
  73.0 2.3 %collective-permute-done.10.near2_ref = bf16[4,72,128]{2,1,0:T(8,128)(2,1)S(1)} collective-permute-done((bf16[4,72,128]{2,1,0:T(8,128)(2,1)}, bf16[4,72,128]{2,1,0:T(8,128)(2,1)S(1)}, u32[]{:S(2)}, u32[]{:S(2)}) %collective-permute-start.10) | collective-permute-done | bytes 73760 | tf_op jit(solution)/shard_map/ppermute | solution.py:368
  76.1 8.3 %shard_map.87 = (bf16[16,40,128]{2,1,0:T(8,128)(2,1)}, f32[16,72,64]{2,1,0:T(8,128)}, f32[16,72,128]{2,1,0:T(8,128)}, bf16[8,72,128]{2,1,0:T(8,128)(2,1)}, bf16[8,72,128]{2,1,0:T(8,128)(2,1)}) custom-call(s32[2]{0:T(128)} %pad_add_fusion.place_ref, bf16[8,72,128]{2,1,0:T(8,128)(2,1)} %get-tuple-element.23.kv_ref, ...), custom_call_target="tpu_custom_call" | custom-call | flops 1019215872 | tf_op jit(solution)/shard_map/pallas_call | solution.py:286
  86.4 5.4 %collective-permute-start.12 = (bf16[8,72,128]{2,1,0:T(8,128)(2,1)}, bf16[8,72,128]{2,1,0:T(8,128)(2,1)S(1)}, u32[]{:S(2)}, u32[]{:S(2)}) collective-permute-start(bf16[8,72,128]{2,1,0:T(8,128)(2,1)} %get-tuple-element.34), channel_id=1, source_target_pairs={{0,16},{16,0},{1,17},{17,1},{2,18},{18,2},{3,19},{19,3},{4,20},{20... | collective-permute-start | bytes 442376 | tf_op jit(solution)/shard_map/ppermute | solution.py:246
  94.6 2.4 %shard_map.89 = (bf16[8,72,192]{2,1,0:T(8,128)(2,1)}, bf16[8,72,192]{2,1,0:T(8,128)(2,1)}) custom-call(s32[2]{0:T(128)} %pad_add_fusion.place_ref, f32[16,72,64]{2,1,0:T(8,128)} %get-tuple-element.31.dq_ref, f32[16,72,128]{2,1,0:T(8,128)} %get-tuple-element.32.dkv_ref, bf16[8,72,128]{2,1,0:T(8,128)(2,1)} %copy-done.14, bf16[8,72,128]{2,1,0:T(8,128)(2,1)} %copy-done.15), custom_call_target="tpu_custom_call" | custom-call | flops 1048576 | tf_op jit(solution)/shard_map/pallas_call | solution.py:308
  98.9 6.1 %collective-permute-done.13.got_ref.pg_ref = bf16[8,72,192]{2,1,0:T(8,128)(2,1)S(1)} collective-permute-done((bf16[8,72,192]{2,1,0:T(8,128)(2,1)}, bf16[8,72,192]{2,1,0:T(8,128)(2,1)S(1)}, u32[]{:S(2)}, u32[]{:S(2)}) %collective-permute-start.13) | collective-permute-done | bytes 221216 | tf_op jit(solution)/shard_map/ppermute | solution.py:246
  105.7 2.7 %shard_map.92 = bf16[192,1024]{1,0:T(8,128)(2,1)} custom-call(s32[8]{0:T(128)} %copy-done.16, bf16[8,72,192]{2,1,0:T(8,128)(2,1)} %copy-done.8, bf16[144,1024]{1,0:T(8,128)(2,1)} %copy-done, bf16[144,1024]{1,0:T(8,128)(2,1)} %copy-done.1, bf16[144,1024]{1,0:T(8,128)(2,1)} %copy-done.2, bf16[144,1024]{1,0:T(8,128)(2,1)} %copy-done.3), custom_call_target="tpu_custom_call" | custom-call | flops 226492416 | tf_op jit(solution)/shard_map/pallas_call | solution.py:319
  110.4 2.8 %shard_map.91.own_ref = f32[192,1024]{1,0:T(8,128)} custom-call(s32[8]{0:T(128)} %copy-done.16, bf16[8,72,192]{2,1,0:T(8,128)(2,1)} %get-tuple-element.35.mine_ref.pg_ref, bf16[144,1024]{1,0:T(8,128)(2,1)} %copy-done, bf16[144,1024]{1,0:T(8,128)(2,1)} %copy-done.1, bf16[144,1024]{1,0:T(8,128)(2,1)} %copy-done.2, bf16[144,1024]{1,0:T(8,128)(2,1)} %copy-done.3), custom_call_target="tpu_custom_call" | custom-call | flops 226492416 | tf_op jit(solution)/shard_map/pallas_call | solution.py:319
  113.2 4.6 %collective-permute-done.19.got_ref = bf16[192,1024]{1,0:T(8,128)(2,1)S(1)} collective-permute-done((bf16[192,1024]{1,0:T(8,128)(2,1)}, bf16[192,1024]{1,0:T(8,128)(2,1)S(1)}, u32[]{:S(2)}, u32[]{:S(2)}) %collective-permute-start.19) | collective-permute-done | bytes 393248 | tf_op jit(solution)/shard_map/ppermute | solution.py:246
  120.6 11.5 %all-to-all-start.2 = ((bf16[32,48,128]{2,1,0:T(8,128)(2,1)}), bf16[32,48,128]{2,1,0:T(8,128)(2,1)S(1)}, u32[]{:S(2)}, u32[]{:S(2)}) async-start(bf16[32,48,128]{2,1,0:T(8,128)(2,1)} %shard_map.93), calls=%async_computation.2 | async-start | bytes 786432 | tf_op jit(solution)/shard_map/all_to_all | solution.py:250
  132.6 14.7 %all-to-all-done.2 = bf16[32,48,128]{2,1,0:T(8,128)(2,1)S(1)} async-done(((bf16[32,48,128]{2,1,0:T(8,128)(2,1)}), bf16[32,48,128]{2,1,0:T(8,128)(2,1)S(1)}, u32[]{:S(2)}, u32[]{:S(2)}) %all-to-all-start.2) | async-done | bytes 393248 | tf_op jit(solution)/shard_map/all_to_all | solution.py:250
  147.3 8.9 %all-to-all-start.1 = ((bf16[16,40,128]{2,1,0:T(8,128)(2,1)}), bf16[16,40,128]{2,1,0:T(8,128)(2,1)S(1)}, u32[]{:S(2)}, u32[]{:S(2)}) async-start(bf16[16,40,128]{2,1,0:T(8,128)(2,1)} %get-tuple-element.30), calls=%async_computation.1 | async-start | bytes 327680 | tf_op jit(solution)/shard_map/all_to_all | solution.py:250
  156.3 2.8 %shard_map.90 = (bf16[144,1024]{1,0:T(8,128)(2,1)}, bf16[144,1024]{1,0:T(8,128)(2,1)}, bf16[72,1024]{1,0:T(8,128)(2,1)}, bf16[72,1024]{1,0:T(8,128)(2,1)}, bf16[...) custom-call(s32[8]{0:T(128)} %and_select_fusion.table_ref, bf16[8,72,192]{2,1,0:T(8,128)(2,1)} %get-tuple-element.35.mine_ref.pg_ref, ...), custom_call_target="tpu_custom_call" | custom-call | flops 452984832 | tf_op jit(solution)/shard_map/pallas_call | solution.py:332
  159.1 4.3 %collective-permute-start.14 = (bf16[144,1024]{1,0:T(8,128)(2,1)}, bf16[144,1024]{1,0:T(8,128)(2,1)S(1)}, u32[]{:S(2)}, u32[]{:S(2)}) collective-permute-start(bf16[144,1024]{1,0:T(8,128)(2,1)} %get-tuple-element.38), channel_id=1, source_target_pairs={{0,4},{2,6},{4,8},{6,10},{8,12},{10,14},{12,0},{14,2},{1,5},{3,7},... | collective-permute-start | bytes 884744 | tf_op jit(solution)/shard_map/ppermute | solution.py:246
  163.4 3.2 %collective-permute-start.16 = (bf16[144,1024]{1,0:T(8,128)(2,1)}, bf16[144,1024]{1,0:T(8,128)(2,1)S(1)}, u32[]{:S(2)}, u32[]{:S(2)}) collective-permute-start(bf16[144,1024]{1,0:T(8,128)(2,1)} %get-tuple-element.41), channel_id=1, source_target_pairs={{0,12},{2,14},{4,0},{6,2},{8,4},{10,6},{12,8},{14,10},{1,13},{3,15... | collective-permute-start | bytes 884744 | tf_op jit(solution)/shard_map/ppermute | solution.py:246
  167.5 4.8 %all-to-all-start.3 = ((bf16[32,48,128]{2,1,0:T(8,128)(2,1)}), bf16[32,48,128]{2,1,0:T(8,128)(2,1)S(1)}, u32[]{:S(2)}, u32[]{:S(2)}) async-start(bf16[32,48,128]{2,1,0:T(8,128)(2,1)} %broadcast_in_dim.12), calls=%async_computation.3 | async-start | bytes 786432 | tf_op jit(solution)/shard_map/all_to_all | solution.py:250
  172.3 2.3 %collective-permute-done.14 = bf16[144,1024]{1,0:T(8,128)(2,1)S(1)} collective-permute-done((bf16[144,1024]{1,0:T(8,128)(2,1)}, bf16[144,1024]{1,0:T(8,128)(2,1)S(1)}, u32[]{:S(2)}, u32[]{:S(2)}) %collective-permute-start.14) | collective-permute-done | bytes 294944 | tf_op jit(solution)/shard_map/ppermute | solution.py:246
  175.6 7.0 %collective-permute-start.15 = (bf16[72,1024]{1,0:T(8,128)(2,1)S(1)}, bf16[72,1024]{1,0:T(8,128)(2,1)S(1)}, u32[]{:S(2)}, u32[]{:S(2)}) collective-permute-start(bf16[72,1024]{1,0:T(8,128)(2,1)S(1)} %add_convert_fusion.3), channel_id=1, source_target_pairs={{0,2},{2,4},{4,6},{6,8},{8,10},{10,12},{12,14},{14,0},{1,3},{3,5},... | collective-permute-start | bytes 442376 | tf_op jit(solution)/shard_map/ppermute | solution.py:246
  182.7 2.5 %collective-permute-start.17 = (bf16[72,1024]{1,0:T(8,128)(2,1)S(1)}, bf16[72,1024]{1,0:T(8,128)(2,1)S(1)}, u32[]{:S(2)}, u32[]{:S(2)}) collective-permute-start(bf16[72,1024]{1,0:T(8,128)(2,1)S(1)} %get-tuple-element.43), channel_id=1, source_target_pairs={{0,12},{2,14},{4,0},{6,2},{8,4},{10,6},{12,8},{14,10},{1,13},{3,15... | collective-permute-start | bytes 442376 | tf_op jit(solution)/shard_map/ppermute | solution.py:246
  185.2 2.9 %collective-permute-start.18 = (bf16[72,1024]{1,0:T(8,128)(2,1)S(1)}, bf16[72,1024]{1,0:T(8,128)(2,1)S(1)}, u32[]{:S(2)}, u32[]{:S(2)}) collective-permute-start(bf16[72,1024]{1,0:T(8,128)(2,1)S(1)} %get-tuple-element.44), channel_id=1, source_target_pairs={{0,14},{2,0},{4,2},{6,4},{8,6},{10,8},{12,10},{14,12},{1,15},{3,1}... | collective-permute-start | bytes 442376 | tf_op jit(solution)/shard_map/ppermute | solution.py:246
  188.2 3.0 %shard_map.88 = bf16[72,1024]{1,0:T(8,128)(2,1)} custom-call(bf16[16,40,128]{2,1,0:T(8,128)(2,1)} %copy-done.4, bf16[1024,1024]{1,0:T(8,128)(2,1)} %bitcast.24), custom_call_target="tpu_custom_call" | custom-call | flops 150994944 | tf_op jit(solution)/shard_map/pallas_call | solution.py:348
  192.2 3.1 %collective-permute-done.18 = bf16[72,1024]{1,0:T(8,128)(2,1)S(1)} collective-permute-done((bf16[72,1024]{1,0:T(8,128)(2,1)S(1)}, bf16[72,1024]{1,0:T(8,128)(2,1)S(1)}, u32[]{:S(2)}, u32[]{:S(2)}) %collective-permute-start.18) | collective-permute-done | bytes 147488 | tf_op jit(solution)/shard_map/ppermute | solution.py:246
  (88 shorter events, 30.4 us)
Async XLA Ops:
  0.6 36.5 %copy-start.23 = (s32[8]{0:T(128)S(1)}, s32[8]{0:T(128)}, u32[]{:S(2)}) copy-start(s32[8]{0:T(128)} %constant.44) | copy-start | bytes 100
  0.6 29.2 %copy-start.13 = (bf16[3,3,8,1024]{3,2,1,0:T(8,128)(2,1)S(1)}, bf16[3,3,8,1024]{3,2,1,0:T(8,128)(2,1)}, u32[]{:S(2)}) copy-start(bf16[3,3,8,1024]{3,2,1,0:T(8,128)(2,1)} %param.6) | copy-start | bytes 442372
  0.7 25.9 %copy-start.5 = (bf16[1,1024,192]{1,2,0:T(8,128)(2,1)S(1)}, bf16[1,1024,192]{1,2,0:T(8,128)(2,1)}, u32[]{:S(2)}) copy-start(bf16[1,1024,192]{1,2,0:T(8,128)(2,1)} %param.8) | copy-start | bytes 1179652
  0.7 29.2 %collective-permute-start = (bf16[72,1024]{1,0:T(8,128)(2,1)}, bf16[72,1024]{1,0:T(8,128)(2,1)S(1)}, u32[]{:S(2)}, u32[]{:S(2)}) collective-permute-start(bf16[72,1024]{1,0:T(8,128)(2,1)} %bitcast.34), channel_id=1, source_target_pairs={{0,14},{2,0},{4,2},{6,4},{8,6},{10,8},{12,10},{14,12},{1,15},{3,1}... | collective-permute-start | bytes 442376 | tf_op jit(solution)/shard_map/ppermute | solution.py:246
  12.3 22.8 %collective-permute-start.1 = (bf16[72,1024]{1,0:T(8,128)(2,1)}, bf16[72,1024]{1,0:T(8,128)(2,1)S(1)}, u32[]{:S(2)}, u32[]{:S(2)}) collective-permute-start(bf16[72,1024]{1,0:T(8,128)(2,1)} %bitcast.35), channel_id=1, source_target_pairs={{0,2},{2,4},{4,6},{6,8},{8,10},{10,12},{12,14},{14,0},{1,3},{3,5},... | collective-permute-start | bytes 442376 | tf_op jit(solution)/shard_map/ppermute | solution.py:246
  14.2 20.9 %collective-permute-start.2 = (bf16[72,1024]{1,0:T(8,128)(2,1)}, bf16[72,1024]{1,0:T(8,128)(2,1)S(1)}, u32[]{:S(2)}, u32[]{:S(2)}) collective-permute-start(bf16[72,1024]{1,0:T(8,128)(2,1)} %bitcast.36), channel_id=1, source_target_pairs={{0,4},{2,6},{4,8},{6,10},{8,12},{10,14},{12,0},{14,2},{1,5},{3,7},... | collective-permute-start | bytes 442376 | tf_op jit(solution)/shard_map/ppermute | solution.py:246
  19.4 53.6 %all-to-all-start = ((bf16[16,40,128]{2,1,0:T(8,128)(2,1)}), bf16[16,40,128]{2,1,0:T(8,128)(2,1)S(1)}, u32[]{:S(2)}, u32[]{:S(2)}) async-start(bf16[16,40,128]{2,1,0:T(8,128)(2,1)} %shard_map.86), calls=%async_computation | async-start | bytes 327680 | tf_op jit(solution)/shard_map/all_to_all | solution.py:250
  26.5 12.5 %collective-permute-start.5 = (bf16[192,1024]{1,0:T(8,128)(2,1)S(1)}, bf16[192,1024]{1,0:T(8,128)(2,1)S(1)}, u32[]{:S(2)}, u32[]{:S(2)}) collective-permute-start(bf16[192,1024]{1,0:T(8,128)(2,1)S(1)} %bitcast.30), channel_id=1, source_target_pairs={{0,1},{1,0},{2,3},{3,2},{4,5},{5,4},{6,7},{7,6},{8,9},{9,8},{10,11... | collective-permute-start | bytes 1179656 | tf_op jit(solution)/shard_map/ppermute | solution.py:246
  29.9 17.9 %collective-permute-start.3 = (bf16[144,1024]{1,0:T(8,128)(2,1)S(1)}, bf16[144,1024]{1,0:T(8,128)(2,1)S(1)}, u32[]{:S(2)}, u32[]{:S(2)}) collective-permute-start(bf16[144,1024]{1,0:T(8,128)(2,1)S(1)} %pad_maximum_fusion.t0_ref), channel_id=1, source_target_pairs={{0,12},{2,14},{4,0},{6,2},{8,4},{10,6},{12,8},{14,10},{1,13},{3,15... | collective-permute-start | bytes 884744 | tf_op jit(solution)/shard_map/ppermute | solution.py:246
  35.2 13.3 %collective-permute-start.4 = (bf16[144,1024]{1,0:T(8,128)(2,1)S(1)}, bf16[144,1024]{1,0:T(8,128)(2,1)S(1)}, u32[]{:S(2)}, u32[]{:S(2)}) collective-permute-start(bf16[144,1024]{1,0:T(8,128)(2,1)S(1)} %constant_dynamic-update-slice_fusion.t1_ref), channel_id=1, source_target_pairs={{0,4},{2,6},{4,8},{6,10},{8,12},{10,14},{12,0},{14,2},{1,5},{3,7},... | collective-permute-start | bytes 884744 | tf_op jit(solution)/shard_map/ppermute | solution.py:246
  37.1 47.3 %copy-start.16 = (s32[8]{0:T(128)}, s32[8]{0:T(128)S(1)}, u32[]{:S(2)}) copy-start(s32[8]{0:T(128)S(1)} %and_select_fusion.1.table_ref) | copy-start | bytes 100
  52.4 22.9 %collective-permute-start.6 = (bf16[8,72,192]{2,1,0:T(8,128)(2,1)}, bf16[8,72,192]{2,1,0:T(8,128)(2,1)S(1)}, u32[]{:S(2)}, u32[]{:S(2)}) collective-permute-start(bf16[8,72,192]{2,1,0:T(8,128)(2,1)} %get-tuple-element.25), channel_id=1, source_target_pairs={{0,1},{1,0},{2,3},{3,2},{4,5},{5,4},{6,7},{7,6},{8,9},{9,8},{10,11... | collective-permute-start | bytes 663560 | tf_op jit(solution)/shard_map/ppermute | solution.py:246
  54.6 18.4 %collective-permute-start.7 = (bf16[4,72,128]{2,1,0:T(8,128)(2,1)}, bf16[4,72,128]{2,1,0:T(8,128)(2,1)S(1)}, u32[]{:S(2)}, u32[]{:S(2)}) collective-permute-start(bf16[4,72,128]{2,1,0:T(8,128)(2,1)} %get-tuple-element.26), channel_id=1, source_target_pairs={{0,496},{1,497},{16,32},{17,33},{32,16},{33,17},{48,64},{49,65},{6... | collective-permute-start | bytes 221192 | tf_op jit(solution)/shard_map/ppermute | solution.py:363
  61.7 11.3 %collective-permute-start.8 = (bf16[4,72,128]{2,1,0:T(8,128)(2,1)}, bf16[4,72,128]{2,1,0:T(8,128)(2,1)S(1)}, u32[]{:S(2)}, u32[]{:S(2)}) collective-permute-start(bf16[4,72,128]{2,1,0:T(8,128)(2,1)} %get-tuple-element.27), channel_id=1, source_target_pairs={{0,16},{16,0},{1,17},{17,1},{2,18},{18,2},{3,19},{19,3},{4,20},{20... | collective-permute-start | bytes 221192 | tf_op jit(solution)/shard_map/ppermute | solution.py:246
  64.1 8.9 %collective-permute-start.9 = (bf16[4,72,128]{2,1,0:T(8,128)(2,1)}, bf16[4,72,128]{2,1,0:T(8,128)(2,1)S(1)}, u32[]{:S(2)}, u32[]{:S(2)}) collective-permute-start(bf16[4,72,128]{2,1,0:T(8,128)(2,1)} %get-tuple-element.28), channel_id=1, source_target_pairs={{0,497},{1,496},{16,33},{17,32},{32,17},{33,16},{48,65},{49,64},{6... | collective-permute-start | bytes 221192 | tf_op jit(solution)/shard_map/ppermute | solution.py:363
  69.5 5.9 %collective-permute-start.10 = (bf16[4,72,128]{2,1,0:T(8,128)(2,1)}, bf16[4,72,128]{2,1,0:T(8,128)(2,1)S(1)}, u32[]{:S(2)}, u32[]{:S(2)}) collective-permute-start(bf16[4,72,128]{2,1,0:T(8,128)(2,1)} %get-tuple-element.29), channel_id=1, source_target_pairs={{0,17},{1,16},{16,1},{17,0},{32,49},{33,48},{48,33},{49,32},{64,81... | collective-permute-start | bytes 221192 | tf_op jit(solution)/shard_map/ppermute | solution.py:368
  84.5 9.4 %collective-permute-start.11 = (bf16[8,72,128]{2,1,0:T(8,128)(2,1)}, bf16[8,72,128]{2,1,0:T(8,128)(2,1)S(1)}, u32[]{:S(2)}, u32[]{:S(2)}) collective-permute-start(bf16[8,72,128]{2,1,0:T(8,128)(2,1)} %get-tuple-element.33), channel_id=1, source_target_pairs={{0,496},{1,497},{16,32},{17,33},{32,16},{33,17},{48,64},{49,65},{6... | collective-permute-start | bytes 442376 | tf_op jit(solution)/shard_map/ppermute | solution.py:363
  86.4 7.5 %collective-permute-start.12 = (bf16[8,72,128]{2,1,0:T(8,128)(2,1)}, bf16[8,72,128]{2,1,0:T(8,128)(2,1)S(1)}, u32[]{:S(2)}, u32[]{:S(2)}) collective-permute-start(bf16[8,72,128]{2,1,0:T(8,128)(2,1)} %get-tuple-element.34), channel_id=1, source_target_pairs={{0,16},{16,0},{1,17},{17,1},{2,18},{18,2},{3,19},{19,3},{4,20},{20... | collective-permute-start | bytes 442376 | tf_op jit(solution)/shard_map/ppermute | solution.py:246
  97.0 8.0 %collective-permute-start.13 = (bf16[8,72,192]{2,1,0:T(8,128)(2,1)}, bf16[8,72,192]{2,1,0:T(8,128)(2,1)S(1)}, u32[]{:S(2)}, u32[]{:S(2)}) collective-permute-start(bf16[8,72,192]{2,1,0:T(8,128)(2,1)} %get-tuple-element.36), channel_id=1, source_target_pairs={{0,1},{1,0},{2,3},{3,2},{4,5},{5,4},{6,7},{7,6},{8,9},{9,8},{10,11... | collective-permute-start | bytes 663560 | tf_op jit(solution)/shard_map/ppermute | solution.py:246
  108.4 9.3 %collective-permute-start.19 = (bf16[192,1024]{1,0:T(8,128)(2,1)}, bf16[192,1024]{1,0:T(8,128)(2,1)S(1)}, u32[]{:S(2)}, u32[]{:S(2)}) collective-permute-start(bf16[192,1024]{1,0:T(8,128)(2,1)} %shard_map.92), channel_id=1, source_target_pairs={{0,1},{1,0},{2,3},{3,2},{4,5},{5,4},{6,7},{7,6},{8,9},{9,8},{10,11... | collective-permute-start | bytes 1179656 | tf_op jit(solution)/shard_map/ppermute | solution.py:246
  110.4 21.7 %copy-start.22 = (s32[8]{0:T(128)S(1)}, s32[8]{0:T(128)}, u32[]{:S(2)}) copy-start(s32[8]{0:T(128)} %constant.40.clone) | copy-start | bytes 100
  120.6 26.8 %all-to-all-start.2 = ((bf16[32,48,128]{2,1,0:T(8,128)(2,1)}), bf16[32,48,128]{2,1,0:T(8,128)(2,1)S(1)}, u32[]{:S(2)}, u32[]{:S(2)}) async-start(bf16[32,48,128]{2,1,0:T(8,128)(2,1)} %shard_map.93), calls=%async_computation.2 | async-start | bytes 786432 | tf_op jit(solution)/shard_map/all_to_all | solution.py:250
  147.3 19.4 %all-to-all-start.1 = ((bf16[16,40,128]{2,1,0:T(8,128)(2,1)}), bf16[16,40,128]{2,1,0:T(8,128)(2,1)S(1)}, u32[]{:S(2)}, u32[]{:S(2)}) async-start(bf16[16,40,128]{2,1,0:T(8,128)(2,1)} %get-tuple-element.30), calls=%async_computation.1 | async-start | bytes 327680 | tf_op jit(solution)/shard_map/all_to_all | solution.py:250
  159.1 23.5 %copy-start.11 = (bf16[72,1024]{1,0:T(8,128)(2,1)S(1)}, bf16[72,1024]{1,0:T(8,128)(2,1)}, u32[]{:S(2)}) copy-start(bf16[72,1024]{1,0:T(8,128)(2,1)} %get-tuple-element.40) | copy-start | bytes 442372
  159.1 23.5 %copy-start.12 = (bf16[72,1024]{1,0:T(8,128)(2,1)S(1)}, bf16[72,1024]{1,0:T(8,128)(2,1)}, u32[]{:S(2)}) copy-start(bf16[72,1024]{1,0:T(8,128)(2,1)} %get-tuple-element.42) | copy-start | bytes 442372
  159.1 15.5 %collective-permute-start.14 = (bf16[144,1024]{1,0:T(8,128)(2,1)}, bf16[144,1024]{1,0:T(8,128)(2,1)S(1)}, u32[]{:S(2)}, u32[]{:S(2)}) collective-permute-start(bf16[144,1024]{1,0:T(8,128)(2,1)} %get-tuple-element.38), channel_id=1, source_target_pairs={{0,4},{2,6},{4,8},{6,10},{8,12},{10,14},{12,0},{14,2},{1,5},{3,7},... | collective-permute-start | bytes 884744 | tf_op jit(solution)/shard_map/ppermute | solution.py:246
  163.4 19.2 %collective-permute-start.16 = (bf16[144,1024]{1,0:T(8,128)(2,1)}, bf16[144,1024]{1,0:T(8,128)(2,1)S(1)}, u32[]{:S(2)}, u32[]{:S(2)}) collective-permute-start(bf16[144,1024]{1,0:T(8,128)(2,1)} %get-tuple-element.41), channel_id=1, source_target_pairs={{0,12},{2,14},{4,0},{6,2},{8,4},{10,6},{12,8},{14,10},{1,13},{3,15... | collective-permute-start | bytes 884744 | tf_op jit(solution)/shard_map/ppermute | solution.py:246
  167.5 27.8 %copy-start.10 = (bf16[72,1024]{1,0:T(8,128)(2,1)S(1)}, bf16[72,1024]{1,0:T(8,128)(2,1)}, u32[]{:S(2)}) copy-start(bf16[72,1024]{1,0:T(8,128)(2,1)} %get-tuple-element.37) | copy-start | bytes 442372
  167.5 28.6 %all-to-all-start.3 = ((bf16[32,48,128]{2,1,0:T(8,128)(2,1)}), bf16[32,48,128]{2,1,0:T(8,128)(2,1)S(1)}, u32[]{:S(2)}, u32[]{:S(2)}) async-start(bf16[32,48,128]{2,1,0:T(8,128)(2,1)} %broadcast_in_dim.12), calls=%async_computation.3 | async-start | bytes 786432 | tf_op jit(solution)/shard_map/all_to_all | solution.py:250
  175.6 15.6 %collective-permute-start.15 = (bf16[72,1024]{1,0:T(8,128)(2,1)S(1)}, bf16[72,1024]{1,0:T(8,128)(2,1)S(1)}, u32[]{:S(2)}, u32[]{:S(2)}) collective-permute-start(bf16[72,1024]{1,0:T(8,128)(2,1)S(1)} %add_convert_fusion.3), channel_id=1, source_target_pairs={{0,2},{2,4},{4,6},{6,8},{8,10},{10,12},{12,14},{14,0},{1,3},{3,5},... | collective-permute-start | bytes 442376 | tf_op jit(solution)/shard_map/ppermute | solution.py:246
  182.7 9.5 %collective-permute-start.17 = (bf16[72,1024]{1,0:T(8,128)(2,1)S(1)}, bf16[72,1024]{1,0:T(8,128)(2,1)S(1)}, u32[]{:S(2)}, u32[]{:S(2)}) collective-permute-start(bf16[72,1024]{1,0:T(8,128)(2,1)S(1)} %get-tuple-element.43), channel_id=1, source_target_pairs={{0,12},{2,14},{4,0},{6,2},{8,4},{10,6},{12,8},{14,10},{1,13},{3,15... | collective-permute-start | bytes 442376 | tf_op jit(solution)/shard_map/ppermute | solution.py:246
  185.2 10.1 %collective-permute-start.18 = (bf16[72,1024]{1,0:T(8,128)(2,1)S(1)}, bf16[72,1024]{1,0:T(8,128)(2,1)S(1)}, u32[]{:S(2)}, u32[]{:S(2)}) collective-permute-start(bf16[72,1024]{1,0:T(8,128)(2,1)S(1)} %get-tuple-element.44), channel_id=1, source_target_pairs={{0,14},{2,0},{4,2},{6,4},{8,6},{10,8},{12,10},{14,12},{1,15},{3,1}... | collective-permute-start | bytes 442376 | tf_op jit(solution)/shard_map/ppermute | solution.py:246
  (16 other events, 78.0 us)

commit v5 on v4

--- a/solution.py
+++ b/solution.py
@@ -183,7 +183,7 @@
 
 
 def combine_kernel(
-    place_ref, dq_ref, dkv_ref, far_ref, near_ref, mine_ref, swap_ref, pg32
+    place_ref, dq_ref, dkv_ref, far_ref, near_ref, pg_ref, mine_ref, swap_ref, pg32
 ):
     yl = place_ref[0]
     first_core = place_ref[1] == 0
@@ -193,6 +193,7 @@
         span = slice(8 * half, 8 * half + 8)
         pg32[span, :, 0:128] = dkv_ref[span] + add
         pg32[span, :, 128:192] = dq_ref[span]
+    pg_ref[...] = pg32[...].astype(BF16)
     for row in range(8):
         mine_ref[row] = pg32[2 * row + yl].astype(BF16)
         swap_ref[row] = pg32[2 * row + 1 - yl].astype(BF16)
@@ -213,27 +214,19 @@
                 out_refs[2 + i][...] = part[i * TOK : (i + 1) * TOK]
 
 
-def weight_grad_kernel(table_ref, pg_ref, t0_ref, t1_ref, t2_ref, t3_ref, out_ref):
-    total = None
-    for chunk, (a_ref, b_ref) in enumerate(((t0_ref, t1_ref), (t2_ref, t3_ref))):
+def weight_grad_kernel(table_ref, pg_ref, *refs):
+    total, piece_ref = None, refs[8]
+    for chunk in range(4):
         rows = jnp.concatenate(
             [pg_ref[table_ref[4 * chunk + i]].astype(F32) for i in range(4)], axis=0
         ).astype(BF16)
-        part = dot_tn(rows, jnp.concatenate([a_ref[...], b_ref[...]], axis=0))
+        source = jnp.concatenate([refs[2 * chunk][...], refs[2 * chunk + 1][...]], axis=0)
+        part = dot_tn(rows, source)
         total = part if total is None else total + part
-    out_ref[...] = total.astype(out_ref.dtype)
-
-
-def piece_kernel(own_ref, got_ref, piece_ref):
+    total = jnp.concatenate([total[128:192], total[0:128]], axis=0).astype(BF16)
     for g in range(4):
-        for start in range(48 * g, 48 * g + 48, 16):
-            row = (start + 128) % 192
-            span = slice(row, row + 16)
-            both = (own_ref[span] + got_ref[span].astype(F32)).astype(BF16)
-            for j in range(8):
-                piece_ref[8 * g + j, start - 48 * g : start - 48 * g + 16] = both[
-                    :, 128 * j : 128 * j + 128
-                ]
+        for j in range(8):
+            piece_ref[8 * g + j] = total[48 * g : 48 * g + 48, 128 * j : 128 * j + 128]
 
 
 def mix_kernel(att_ref, weight_ref, out_ref):
@@ -263,6 +256,8 @@
     pair3 = shift(pair1, "z", 8, 2)
     tokens = (pair0, pair1, pair2, pair3)
     distance = jnp.array([0, 7, 1, 2, 6, 5, 3, 4], jnp.int32)
+    late0, late1 = shift(pair0, "yl", 2, 1), shift(pair1, "yl", 2, 1)
+    late2, late3 = shift(pair2, "yl", 2, 1), shift(late1, "z", 8, 2)
     rows = ((z - distance) % 8).astype(jnp.int32)
     place = jnp.stack([yl, core])
 
@@ -305,27 +300,24 @@
     grad_far, grad_near = send_far(grad_far), shift(grad_near, "core", 2, 1)
     token_att = exchange(attended, HEAD)
 
-    pg_mine, pg_swap = call(
+    pg, pg_mine, pg_swap = call(
         combine_kernel,
-        [((8, TOK, 3 * HD), BF16), ((8, TOK, 3 * HD), BF16)],
+        [((RANKS, TOK, 3 * HD), BF16), ((8, TOK, 3 * HD), BF16), ((8, TOK, 3 * HD), BF16)],
         scratch=[pltpu.VMEM((RANKS, TOK, 3 * HD), F32)],
         smem=(0,),
         n_in=5,
         flops=1 << 20,
     )(place, dq, dkv, grad_far, grad_near)
     pg_got = shift(pg_swap, "yl", 2, 1)
-    grads = []
-    for pg, dtype in ((pg_mine, F32), (pg_got, BF16)):
-        grads += call(
-            weight_grad_kernel,
-            [((3 * HD, width), dtype)],
-            smem=(0,),
-            n_in=6,
-            flops=2 * 576 * 192 * width,
-        )(rows, pg, *tokens)
-    grad_got = shift(grads[1], "yl", 2, 1)
-    (pieces,) = call(piece_kernel, [((32, 48, 128), BF16)], n_in=2, flops=1 << 20)(
-        grads[0], grad_got
+    (pieces,) = call(
+        weight_grad_kernel,
+        [((32, 48, 128), BF16)],
+        smem=(0,),
+        n_in=10,
+        flops=2 * 1152 * 192 * width,
+    )(
+        jnp.concatenate([2 * rows + yl, 2 * rows + 1 - yl]).astype(jnp.int32),
+        pg, *tokens, late0, late1, late2, late3,
     )
     pieces = exchange(pieces, LON)
     reach = (5, 4, 3, 2, 6, 7, 1, 0)

time: 199 us -> 186 us (0.935)
  waiting for transfers between devices: 47 us -> 35.6 us
  Pallas kernels: 30.6 us -> 26.7 us
  starting transfers between devices: 109 us -> 111 us
    ppermute x16 -> x19, starting transfers between devices: 59.6 us -> 72.1 us  [shift(): lax.ppermute(value, axis, [(i, (i + distance) % size) for i in range(size)])]
    all_to_all x4, starting transfers between devices: 32.4 us -> 24 us  [exchange(): return lax.all_to_all(value, axis, 0, 0, tiled=True)]
    ppermute x16 -> x19, waiting for transfers between devices: 27.9 us -> 21.7 us  [shift(): lax.ppermute(value, axis, [(i, (i + distance) % size) for i in range(size)])]
    ppermute x3, starting transfers between devices: 14.4 us -> 10.4 us  [send_far(): return lax.ppermute(value, LON + ('yl',), routes)]
    pallas_call x4 -> x2, Pallas kernels: 9.97 us -> 6.15 us  [the longest x1 3.53 us: step(): call(weight_grad_kernel, [((32, 48, 128), BF16)], smem=(0,), n_in=10, flo...]
    ppermute x1, waiting for transfers between devices: 2.32 us -> 0.01 us  [send_near(): return lax.ppermute(value, LON + ('yl',), routes)]
    unnamed x50 -> x52, local copies, waits for them, and re-layouts: 4.78 us -> 5.58 us
  transfers between devices with their start and end apart: 24 -> 27, of which waited for: 11 -> 5; matrix products, arithmetic and copies ran while one was open for 2% -> 3% of each run, Pallas kernels for 8% -> 13%
where the time goes in v5:
time: 186 us; the launch traced here: 185 us
  starting transfers between devices  111 us (60%)
  waiting for transfers between devices  35.6 us (19%)
  Pallas kernels  26.7 us (14%)
  local copies, waits for them, and re-layouts  6.64 us (4%)
  other arithmetic  4.4 us (2%)
    ppermute x19, starting transfers between devices, shift(): lax.ppermute(value, axis, [(i, (i + distance) % size) for i in range(size)])  72.1 us
    all_to_all x4, starting transfers between devices, exchange(): return lax.all_to_all(value, axis, 0, 0, tiled=True)  24 us
    ppermute x19, waiting for transfers between devices, shift(): lax.ppermute(value, axis, [(i, (i + distance) % size) for i in range(size)])  21.7 us
    all_to_all x4, waiting for transfers between devices, exchange(): return lax.all_to_all(value, axis, 0, 0, tiled=True)  12.8 us
    ppermute x3, starting transfers between devices, send_far(): return lax.ppermute(value, LON + ('yl',), routes)  10.4 us
    pallas_call x1, Pallas kernels, step(): call(attend_kernel, [((RANKS, 40, 128), BF16), ((RANKS, TOK, HD), F32), (...  8.33 us
    unnamed x52, local copies, waits for them, and re-layouts  5.58 us
    ppermute x1, starting transfers between devices, send_near(): return lax.ppermute(value, LON + ('yl',), routes)  4 us
  transfers between devices with their start and end apart: 27, of which 5 were waited for; matrix products, arithmetic and copies ran while one was open for 3% of the time, Pallas kernels for 13%

profile of v5, /device:TPU:1, one launch (start us, length us, event | category | flops | bytes accessed | tf_op | source)
XLA Modules:
  0.0 185.2 jit_solution(2873704325864311150)
XLA Ops:
  0.7 4.9 %collective-permute-start.1 = (bf16[72,1024]{1,0:T(8,128)(2,1)}, bf16[72,1024]{1,0:T(8,128)(2,1)S(1)}, u32[]{:S(2)}, u32[]{:S(2)}) collective-permute-start(bf16[72,1024]{1,0:T(8,128)(2,1)} %bitcast.34), channel_id=1, source_target_pairs={{0,2},{2,4},{4,6},{6,8},{8,10},{10,12},{12,14},{14,0},{1,3},{3,5},... | collective-permute-start | bytes 442376 | tf_op jit(solution)/shard_map/ppermute | solution.py:239
  5.6 5.8 %collective-permute-start.2 = (bf16[72,1024]{1,0:T(8,128)(2,1)}, bf16[72,1024]{1,0:T(8,128)(2,1)S(1)}, u32[]{:S(2)}, u32[]{:S(2)}) collective-permute-start(bf16[72,1024]{1,0:T(8,128)(2,1)} %bitcast.35), channel_id=1, source_target_pairs={{0,4},{2,6},{4,8},{6,10},{8,12},{10,14},{12,0},{14,2},{1,5},{3,7},... | collective-permute-start | bytes 442376 | tf_op jit(solution)/shard_map/ppermute | solution.py:239
  11.4 4.7 %collective-permute-start = (bf16[72,1024]{1,0:T(8,128)(2,1)}, bf16[72,1024]{1,0:T(8,128)(2,1)S(1)}, u32[]{:S(2)}, u32[]{:S(2)}) collective-permute-start(bf16[72,1024]{1,0:T(8,128)(2,1)} %bitcast.36), channel_id=1, source_target_pairs={{0,14},{2,0},{4,2},{6,4},{8,6},{10,8},{12,10},{14,12},{1,15},{3,1}... | collective-permute-start | bytes 442376 | tf_op jit(solution)/shard_map/ppermute | solution.py:239
  16.1 3.2 %collective-permute-start.5 = (bf16[192,1024]{1,0:T(8,128)(2,1)}, bf16[192,1024]{1,0:T(8,128)(2,1)S(1)}, u32[]{:S(2)}, u32[]{:S(2)}) collective-permute-start(bf16[192,1024]{1,0:T(8,128)(2,1)} %bitcast.28), channel_id=1, source_target_pairs={{0,1},{1,0},{2,3},{3,2},{4,5},{5,4},{6,7},{7,6},{8,9},{9,8},{10,11... | collective-permute-start | bytes 1179656 | tf_op jit(solution)/shard_map/ppermute | solution.py:239
  19.3 3.3 %shard_map.86 = bf16[16,40,128]{2,1,0:T(8,128)(2,1)} custom-call(bf16[72,1024]{1,0:T(8,128)(2,1)} %bitcast.31, bf16[16,64,1024]{2,1,0:T(8,128)(2,1)} %weight_ref.1), custom_call_target="tpu_custom_call" | custom-call | flops 150994944 | tf_op jit(solution)/shard_map/pallas_call | solution.py:264
  22.6 6.1 %all-to-all-start = ((bf16[16,40,128]{2,1,0:T(8,128)(2,1)}), bf16[16,40,128]{2,1,0:T(8,128)(2,1)S(1)}, u32[]{:S(2)}, u32[]{:S(2)}) async-start(bf16[16,40,128]{2,1,0:T(8,128)(2,1)} %shard_map.86), calls=%async_computation | async-start | bytes 327680 | tf_op jit(solution)/shard_map/all_to_all | solution.py:243
  28.8 4.2 %collective-permute-start.4 = (bf16[144,1024]{1,0:T(8,128)(2,1)S(1)}, bf16[144,1024]{1,0:T(8,128)(2,1)S(1)}, u32[]{:S(2)}, u32[]{:S(2)}) collective-permute-start(bf16[144,1024]{1,0:T(8,128)(2,1)S(1)} %constant_dynamic-update-slice_fusion.t1_ref.refs_1_), channel_id=1, source_target_pairs={{0,4},{2,6},{4,8},{6,10},{8,12},{10,14},{12,0},{14,2},{1,5},{3,7},... | collective-permute-start | bytes 884744 | tf_op jit(solution)/shard_map/ppermute | solution.py:239
  33.0 3.1 %collective-permute-start.20 = (bf16[144,1024]{1,0:T(8,128)(2,1)S(1)}, bf16[144,1024]{1,0:T(8,128)(2,1)S(1)}, u32[]{:S(2)}, u32[]{:S(2)}) collective-permute-start(bf16[144,1024]{1,0:T(8,128)(2,1)S(1)} %constant_dynamic-update-slice_fusion.t1_ref.refs_1_), channel_id=1, source_target_pairs={{0,1},{1,0},{2,3},{3,2},{4,5},{5,4},{6,7},{7,6},{8,9},{9,8},{10,11... | collective-permute-start | bytes 884744 | tf_op jit(solution)/shard_map/ppermute | solution.py:239
  36.1 3.4 %collective-permute-start.3 = (bf16[144,1024]{1,0:T(8,128)(2,1)S(1)}, bf16[144,1024]{1,0:T(8,128)(2,1)S(1)}, u32[]{:S(2)}, u32[]{:S(2)}) collective-permute-start(bf16[144,1024]{1,0:T(8,128)(2,1)S(1)} %pad_maximum_fusion.t0_ref.refs_0_), channel_id=1, source_target_pairs={{0,12},{2,14},{4,0},{6,2},{8,4},{10,6},{12,8},{14,10},{1,13},{3,15... | collective-permute-start | bytes 884744 | tf_op jit(solution)/shard_map/ppermute | solution.py:239
  40.1 15.0 %collective-permute-done.3.t2_ref.refs_2_ = bf16[144,1024]{1,0:T(8,128)(2,1)S(1)} collective-permute-done((bf16[144,1024]{1,0:T(8,128)(2,1)S(1)}, bf16[144,1024]{1,0:T(8,128)(2,1)S(1)}, u32[]{:S(2)}, u32[]{:S(2)}) %collective-permute-start.3) | collective-permute-done | bytes 294944 | tf_op jit(solution)/shard_map/ppermute | solution.py:239
  56.5 3.2 %shard_map.85 = (bf16[8,72,128]{2,1,0:T(8,128)(2,1)}, bf16[8,72,64]{2,1,0:T(8,128)(2,1)}, bf16[8,72,192]{2,1,0:T(8,128)(2,1)}, bf16[4,72,128]{2,1,0:T(8,128)(2,1...) custom-call(s32[9]{0:T(128)} %pad_add_fusion.1.table_ref, ...), custom_call_target="tpu_custom_call" | custom-call | flops 452984832 | tf_op jit(solution)/shard_map/pallas_call | solution.py:269
  61.9 4.9 %collective-permute-start.7 = (bf16[4,72,128]{2,1,0:T(8,128)(2,1)}, bf16[4,72,128]{2,1,0:T(8,128)(2,1)S(1)}, u32[]{:S(2)}, u32[]{:S(2)}) collective-permute-start(bf16[4,72,128]{2,1,0:T(8,128)(2,1)} %get-tuple-element.27), channel_id=1, source_target_pairs={{0,496},{1,497},{16,32},{17,33},{32,16},{33,17},{48,64},{49,65},{6... | collective-permute-start | bytes 221192 | tf_op jit(solution)/shard_map/ppermute | solution.py:355
  66.8 5.4 %collective-permute-start.8 = (bf16[4,72,128]{2,1,0:T(8,128)(2,1)}, bf16[4,72,128]{2,1,0:T(8,128)(2,1)S(1)}, u32[]{:S(2)}, u32[]{:S(2)}) collective-permute-start(bf16[4,72,128]{2,1,0:T(8,128)(2,1)} %get-tuple-element.28), channel_id=1, source_target_pairs={{0,16},{16,0},{1,17},{17,1},{2,18},{18,2},{3,19},{19,3},{4,20},{20... | collective-permute-start | bytes 221192 | tf_op jit(solution)/shard_map/ppermute | solution.py:239
  72.2 3.1 %collective-permute-start.9 = (bf16[4,72,128]{2,1,0:T(8,128)(2,1)}, bf16[4,72,128]{2,1,0:T(8,128)(2,1)S(1)}, u32[]{:S(2)}, u32[]{:S(2)}) collective-permute-start(bf16[4,72,128]{2,1,0:T(8,128)(2,1)} %get-tuple-element.29), channel_id=1, source_target_pairs={{0,497},{1,496},{16,33},{17,32},{32,17},{33,16},{48,65},{49,64},{6... | collective-permute-start | bytes 221192 | tf_op jit(solution)/shard_map/ppermute | solution.py:355
  75.3 4.0 %collective-permute-start.10 = (bf16[4,72,128]{2,1,0:T(8,128)(2,1)}, bf16[4,72,128]{2,1,0:T(8,128)(2,1)S(1)}, u32[]{:S(2)}, u32[]{:S(2)}) collective-permute-start(bf16[4,72,128]{2,1,0:T(8,128)(2,1)} %get-tuple-element.30), channel_id=1, source_target_pairs={{0,17},{1,16},{16,1},{17,0},{32,49},{33,48},{48,33},{49,32},{64,81... | collective-permute-start | bytes 221192 | tf_op jit(solution)/shard_map/ppermute | solution.py:360
  82.2 3.1 %collective-permute-start.21 = (bf16[144,1024]{1,0:T(8,128)(2,1)}, bf16[144,1024]{1,0:T(8,128)(2,1)S(1)}, u32[]{:S(2)}, u32[]{:S(2)}) collective-permute-start(bf16[144,1024]{1,0:T(8,128)(2,1)} %copy-done.3), channel_id=1, source_target_pairs={{0,1},{1,0},{2,3},{3,2},{4,5},{5,4},{6,7},{7,6},{8,9},{9,8},{10,11... | collective-permute-start | bytes 884744 | tf_op jit(solution)/shard_map/ppermute | solution.py:239
  85.3 3.2 %collective-permute-start.22 = (bf16[144,1024]{1,0:T(8,128)(2,1)S(1)}, bf16[144,1024]{1,0:T(8,128)(2,1)S(1)}, u32[]{:S(2)}, u32[]{:S(2)}) collective-permute-start(bf16[144,1024]{1,0:T(8,128)(2,1)S(1)} %collective-permute-done.20.refs_5_), channel_id=1, source_target_pairs={{0,4},{2,6},{4,8},{6,10},{8,12},{10,14},{12,0},{14,2},{1,5},{3,7},... | collective-permute-start | bytes 884744 | tf_op jit(solution)/shard_map/ppermute | solution.py:239
  89.4 8.3 %shard_map.87 = (bf16[16,40,128]{2,1,0:T(8,128)(2,1)}, f32[16,72,64]{2,1,0:T(8,128)}, f32[16,72,128]{2,1,0:T(8,128)}, bf16[8,72,128]{2,1,0:T(8,128)(2,1)}, bf16[8,72,128]{2,1,0:T(8,128)(2,1)}) custom-call(s32[2]{0:T(128)} %pad_add_fusion.place_ref, bf16[8,72,128]{2,1,0:T(8,128)(2,1)} %get-tuple-element.24.kv_ref, ...), custom_call_target="tpu_custom_call" | custom-call | flops 1019215872 | tf_op jit(solution)/shard_map/pallas_call | solution.py:281
  100.1 5.2 %collective-permute-start.12 = (bf16[8,72,128]{2,1,0:T(8,128)(2,1)}, bf16[8,72,128]{2,1,0:T(8,128)(2,1)S(1)}, u32[]{:S(2)}, u32[]{:S(2)}) collective-permute-start(bf16[8,72,128]{2,1,0:T(8,128)(2,1)} %get-tuple-element.35), channel_id=1, source_target_pairs={{0,16},{16,0},{1,17},{17,1},{2,18},{18,2},{3,19},{19,3},{4,20},{20... | collective-permute-start | bytes 442376 | tf_op jit(solution)/shard_map/ppermute | solution.py:239
  107.8 2.6 %shard_map.89 = (bf16[16,72,192]{2,1,0:T(8,128)(2,1)}, bf16[8,72,192]{2,1,0:T(8,128)(2,1)}, bf16[8,72,192]{2,1,0:T(8,128)(2,1)}) custom-call(s32[2]{0:T(128)} %pad_add_fusion.place_ref, f32[16,72,64]{2,1,0:T(8,128)} %get-tuple-element.32.dq_ref, f32[16,72,128]{2,1,0:T(8,128)} %get-tuple-element.33.dkv_ref, bf16[8,72,128]{2,1,0:T(8,128)(2,1)} %copy-done.14, ...), custom_call_target="tpu_custom_call" | custom-call | flops 1048576 | tf_op jit(solution)/shard_map/pallas_call | solution.py:303
  111.5 3.5 %shard_map.91 = bf16[32,48,128]{2,1,0:T(8,128)(2,1)} custom-call(s32[16]{0:T(128)} %pad_add_fusion.2.table_ref, bf16[16,72,192]{2,1,0:T(8,128)(2,1)} %get-tuple-element.44.pg_ref, bf16[144,1024]{1,0:T(8,128)(2,1)} %copy-done, bf16[144,1024]{1,0:T(8,128)(2,1)} %copy-done.1, bf16[144,1024]{1,0:T(8,128)(2,1)} %copy-done.3, bf16[144,1024]{1,0:T(8,128)(2,1)} %copy-done.2, ...), custom_call_target="tpu_custom_call" | custom-call | flops 452984832 | tf_op jit(solution)/shard_map/pallas_call | solution.py:312
  115.0 8.0 %all-to-all-start.2 = ((bf16[32,48,128]{2,1,0:T(8,128)(2,1)}), bf16[32,48,128]{2,1,0:T(8,128)(2,1)S(1)}, u32[]{:S(2)}, u32[]{:S(2)}) async-start(bf16[32,48,128]{2,1,0:T(8,128)(2,1)} %shard_map.91), calls=%async_computation.2 | async-start | bytes 786432 | tf_op jit(solution)/shard_map/all_to_all | solution.py:243
  126.2 12.7 %all-to-all-done.2 = bf16[32,48,128]{2,1,0:T(8,128)(2,1)S(1)} async-done(((bf16[32,48,128]{2,1,0:T(8,128)(2,1)}), bf16[32,48,128]{2,1,0:T(8,128)(2,1)S(1)}, u32[]{:S(2)}, u32[]{:S(2)}) %all-to-all-start.2) | async-done | bytes 393248 | tf_op jit(solution)/shard_map/all_to_all | solution.py:243
  138.9 4.6 %all-to-all-start.1 = ((bf16[16,40,128]{2,1,0:T(8,128)(2,1)}), bf16[16,40,128]{2,1,0:T(8,128)(2,1)S(1)}, u32[]{:S(2)}, u32[]{:S(2)}) async-start(bf16[16,40,128]{2,1,0:T(8,128)(2,1)} %get-tuple-element.31), calls=%async_computation.1 | async-start | bytes 327680 | tf_op jit(solution)/shard_map/all_to_all | solution.py:243
  144.3 2.8 %shard_map.90 = (bf16[144,1024]{1,0:T(8,128)(2,1)}, bf16[144,1024]{1,0:T(8,128)(2,1)}, bf16[72,1024]{1,0:T(8,128)(2,1)}, bf16[72,1024]{1,0:T(8,128)(2,1)}, bf16[...) custom-call(s32[8]{0:T(128)} %and_select_fusion.table_ref, bf16[8,72,192]{2,1,0:T(8,128)(2,1)} %get-tuple-element.36.mine_ref, ...), custom_call_target="tpu_custom_call" | custom-call | flops 452984832 | tf_op jit(solution)/shard_map/pallas_call | solution.py:324
  147.1 5.5 %collective-permute-start.16 = (bf16[144,1024]{1,0:T(8,128)(2,1)}, bf16[144,1024]{1,0:T(8,128)(2,1)S(1)}, u32[]{:S(2)}, u32[]{:S(2)}) collective-permute-start(bf16[144,1024]{1,0:T(8,128)(2,1)} %get-tuple-element.42), channel_id=1, source_target_pairs={{0,12},{2,14},{4,0},{6,2},{8,4},{10,6},{12,8},{14,10},{1,13},{3,15... | collective-permute-start | bytes 884744 | tf_op jit(solution)/shard_map/ppermute | solution.py:239
  155.4 5.2 %all-to-all-start.3 = ((bf16[32,48,128]{2,1,0:T(8,128)(2,1)}), bf16[32,48,128]{2,1,0:T(8,128)(2,1)S(1)}, u32[]{:S(2)}, u32[]{:S(2)}) async-start(bf16[32,48,128]{2,1,0:T(8,128)(2,1)} %broadcast_in_dim.12), calls=%async_computation.3 | async-start | bytes 786432 | tf_op jit(solution)/shard_map/all_to_all | solution.py:243
  160.6 5.3 %collective-permute-done.16 = bf16[144,1024]{1,0:T(8,128)(2,1)S(1)} collective-permute-done((bf16[144,1024]{1,0:T(8,128)(2,1)}, bf16[144,1024]{1,0:T(8,128)(2,1)S(1)}, u32[]{:S(2)}, u32[]{:S(2)}) %collective-permute-start.16) | collective-permute-done | bytes 294944 | tf_op jit(solution)/shard_map/ppermute | solution.py:239
  167.0 4.0 %collective-permute-start.18 = (bf16[72,1024]{1,0:T(8,128)(2,1)S(1)}, bf16[72,1024]{1,0:T(8,128)(2,1)S(1)}, u32[]{:S(2)}, u32[]{:S(2)}) collective-permute-start(bf16[72,1024]{1,0:T(8,128)(2,1)S(1)} %get-tuple-element.48), channel_id=1, source_target_pairs={{0,14},{2,0},{4,2},{6,4},{8,6},{10,8},{12,10},{14,12},{1,15},{3,1}... | collective-permute-start | bytes 442376 | tf_op jit(solution)/shard_map/ppermute | solution.py:239
  171.0 4.2 %collective-permute-start.17 = (bf16[72,1024]{1,0:T(8,128)(2,1)S(1)}, bf16[72,1024]{1,0:T(8,128)(2,1)S(1)}, u32[]{:S(2)}, u32[]{:S(2)}) collective-permute-start(bf16[72,1024]{1,0:T(8,128)(2,1)S(1)} %get-tuple-element.47), channel_id=1, source_target_pairs={{0,12},{2,14},{4,0},{6,2},{8,4},{10,6},{12,8},{14,10},{1,13},{3,15... | collective-permute-start | bytes 442376 | tf_op jit(solution)/shard_map/ppermute | solution.py:239
  175.2 3.4 %collective-permute-start.15 = (bf16[72,1024]{1,0:T(8,128)(2,1)S(1)}, bf16[72,1024]{1,0:T(8,128)(2,1)S(1)}, u32[]{:S(2)}, u32[]{:S(2)}) collective-permute-start(bf16[72,1024]{1,0:T(8,128)(2,1)S(1)} %add_convert_fusion.3), channel_id=1, source_target_pairs={{0,2},{2,4},{4,6},{6,8},{8,10},{10,12},{12,14},{14,0},{1,3},{3,5},... | collective-permute-start | bytes 442376 | tf_op jit(solution)/shard_map/ppermute | solution.py:239
  178.6 3.0 %shard_map.88 = bf16[72,1024]{1,0:T(8,128)(2,1)} custom-call(bf16[16,40,128]{2,1,0:T(8,128)(2,1)} %copy-done.4, bf16[1024,1024]{1,0:T(8,128)(2,1)} %bitcast.24), custom_call_target="tpu_custom_call" | custom-call | flops 150994944 | tf_op jit(solution)/shard_map/pallas_call | solution.py:340
  (96 shorter events, 24.9 us)
Async XLA Ops:
  0.6 38.9 %copy-start.16 = (s32[8]{0:T(128)S(1)}, s32[8]{0:T(128)}, u32[]{:S(2)}) copy-start(s32[8]{0:T(128)} %constant.48) | copy-start | bytes 100
  0.6 35.4 %copy-start.13 = (bf16[3,3,8,1024]{3,2,1,0:T(8,128)(2,1)S(1)}, bf16[3,3,8,1024]{3,2,1,0:T(8,128)(2,1)}, u32[]{:S(2)}) copy-start(bf16[3,3,8,1024]{3,2,1,0:T(8,128)(2,1)} %param.6) | copy-start | bytes 442372
  0.7 28.1 %collective-permute-start.1 = (bf16[72,1024]{1,0:T(8,128)(2,1)}, bf16[72,1024]{1,0:T(8,128)(2,1)S(1)}, u32[]{:S(2)}, u32[]{:S(2)}) collective-permute-start(bf16[72,1024]{1,0:T(8,128)(2,1)} %bitcast.34), channel_id=1, source_target_pairs={{0,2},{2,4},{4,6},{6,8},{8,10},{10,12},{12,14},{14,0},{1,3},{3,5},... | collective-permute-start | bytes 442376 | tf_op jit(solution)/shard_map/ppermute | solution.py:239
  5.6 23.2 %collective-permute-start.2 = (bf16[72,1024]{1,0:T(8,128)(2,1)}, bf16[72,1024]{1,0:T(8,128)(2,1)S(1)}, u32[]{:S(2)}, u32[]{:S(2)}) collective-permute-start(bf16[72,1024]{1,0:T(8,128)(2,1)} %bitcast.35), channel_id=1, source_target_pairs={{0,4},{2,6},{4,8},{6,10},{8,12},{10,14},{12,0},{14,2},{1,5},{3,7},... | collective-permute-start | bytes 442376 | tf_op jit(solution)/shard_map/ppermute | solution.py:239
  11.4 24.6 %collective-permute-start = (bf16[72,1024]{1,0:T(8,128)(2,1)}, bf16[72,1024]{1,0:T(8,128)(2,1)S(1)}, u32[]{:S(2)}, u32[]{:S(2)}) collective-permute-start(bf16[72,1024]{1,0:T(8,128)(2,1)} %bitcast.36), channel_id=1, source_target_pairs={{0,14},{2,0},{4,2},{6,4},{8,6},{10,8},{12,10},{14,12},{1,15},{3,1}... | collective-permute-start | bytes 442376 | tf_op jit(solution)/shard_map/ppermute | solution.py:239
  16.1 24.0 %collective-permute-start.5 = (bf16[192,1024]{1,0:T(8,128)(2,1)}, bf16[192,1024]{1,0:T(8,128)(2,1)S(1)}, u32[]{:S(2)}, u32[]{:S(2)}) collective-permute-start(bf16[192,1024]{1,0:T(8,128)(2,1)} %bitcast.28), channel_id=1, source_target_pairs={{0,1},{1,0},{2,3},{3,2},{4,5},{5,4},{6,7},{7,6},{8,9},{9,8},{10,11... | collective-permute-start | bytes 1179656 | tf_op jit(solution)/shard_map/ppermute | solution.py:239
  22.6 65.9 %all-to-all-start = ((bf16[16,40,128]{2,1,0:T(8,128)(2,1)}), bf16[16,40,128]{2,1,0:T(8,128)(2,1)S(1)}, u32[]{:S(2)}, u32[]{:S(2)}) async-start(bf16[16,40,128]{2,1,0:T(8,128)(2,1)} %shard_map.86), calls=%async_computation | async-start | bytes 327680 | tf_op jit(solution)/shard_map/all_to_all | solution.py:243
  28.8 26.3 %collective-permute-start.4 = (bf16[144,1024]{1,0:T(8,128)(2,1)S(1)}, bf16[144,1024]{1,0:T(8,128)(2,1)S(1)}, u32[]{:S(2)}, u32[]{:S(2)}) collective-permute-start(bf16[144,1024]{1,0:T(8,128)(2,1)S(1)} %constant_dynamic-update-slice_fusion.t1_ref.refs_1_), channel_id=1, source_target_pairs={{0,4},{2,6},{4,8},{6,10},{8,12},{10,14},{12,0},{14,2},{1,5},{3,7},... | collective-permute-start | bytes 884744 | tf_op jit(solution)/shard_map/ppermute | solution.py:239
  33.0 42.4 %collective-permute-start.20 = (bf16[144,1024]{1,0:T(8,128)(2,1)S(1)}, bf16[144,1024]{1,0:T(8,128)(2,1)S(1)}, u32[]{:S(2)}, u32[]{:S(2)}) collective-permute-start(bf16[144,1024]{1,0:T(8,128)(2,1)S(1)} %constant_dynamic-update-slice_fusion.t1_ref.refs_1_), channel_id=1, source_target_pairs={{0,1},{1,0},{2,3},{3,2},{4,5},{5,4},{6,7},{7,6},{8,9},{9,8},{10,11... | collective-permute-start | bytes 884744 | tf_op jit(solution)/shard_map/ppermute | solution.py:239
  36.1 19.0 %collective-permute-start.3 = (bf16[144,1024]{1,0:T(8,128)(2,1)S(1)}, bf16[144,1024]{1,0:T(8,128)(2,1)S(1)}, u32[]{:S(2)}, u32[]{:S(2)}) collective-permute-start(bf16[144,1024]{1,0:T(8,128)(2,1)S(1)} %pad_maximum_fusion.t0_ref.refs_0_), channel_id=1, source_target_pairs={{0,12},{2,14},{4,0},{6,2},{8,4},{10,6},{12,8},{14,10},{1,13},{3,15... | collective-permute-start | bytes 884744 | tf_op jit(solution)/shard_map/ppermute | solution.py:239
  59.7 28.9 %collective-permute-start.6 = (bf16[8,72,192]{2,1,0:T(8,128)(2,1)}, bf16[8,72,192]{2,1,0:T(8,128)(2,1)S(1)}, u32[]{:S(2)}, u32[]{:S(2)}) collective-permute-start(bf16[8,72,192]{2,1,0:T(8,128)(2,1)} %get-tuple-element.26), channel_id=1, source_target_pairs={{0,1},{1,0},{2,3},{3,2},{4,5},{5,4},{6,7},{7,6},{8,9},{9,8},{10,11... | collective-permute-start | bytes 663560 | tf_op jit(solution)/shard_map/ppermute | solution.py:239
  61.9 18.0 %collective-permute-start.7 = (bf16[4,72,128]{2,1,0:T(8,128)(2,1)}, bf16[4,72,128]{2,1,0:T(8,128)(2,1)S(1)}, u32[]{:S(2)}, u32[]{:S(2)}) collective-permute-start(bf16[4,72,128]{2,1,0:T(8,128)(2,1)} %get-tuple-element.27), channel_id=1, source_target_pairs={{0,496},{1,497},{16,32},{17,33},{32,16},{33,17},{48,64},{49,65},{6... | collective-permute-start | bytes 221192 | tf_op jit(solution)/shard_map/ppermute | solution.py:355
  66.8 15.4 %collective-permute-start.8 = (bf16[4,72,128]{2,1,0:T(8,128)(2,1)}, bf16[4,72,128]{2,1,0:T(8,128)(2,1)S(1)}, u32[]{:S(2)}, u32[]{:S(2)}) collective-permute-start(bf16[4,72,128]{2,1,0:T(8,128)(2,1)} %get-tuple-element.28), channel_id=1, source_target_pairs={{0,16},{16,0},{1,17},{17,1},{2,18},{18,2},{3,19},{19,3},{4,20},{20... | collective-permute-start | bytes 221192 | tf_op jit(solution)/shard_map/ppermute | solution.py:239
  72.2 13.1 %collective-permute-start.9 = (bf16[4,72,128]{2,1,0:T(8,128)(2,1)}, bf16[4,72,128]{2,1,0:T(8,128)(2,1)S(1)}, u32[]{:S(2)}, u32[]{:S(2)}) collective-permute-start(bf16[4,72,128]{2,1,0:T(8,128)(2,1)} %get-tuple-element.29), channel_id=1, source_target_pairs={{0,497},{1,496},{16,33},{17,32},{32,17},{33,16},{48,65},{49,64},{6... | collective-permute-start | bytes 221192 | tf_op jit(solution)/shard_map/ppermute | solution.py:355
  75.3 35.1 %copy-start.6 = (bf16[144,1024]{1,0:T(8,128)(2,1)}, bf16[144,1024]{1,0:T(8,128)(2,1)S(1)}, u32[]{:S(2)}) copy-start(bf16[144,1024]{1,0:T(8,128)(2,1)S(1)} %collective-permute-done.20.refs_5_) | copy-start | bytes 884740
  75.3 13.2 %collective-permute-start.10 = (bf16[4,72,128]{2,1,0:T(8,128)(2,1)}, bf16[4,72,128]{2,1,0:T(8,128)(2,1)S(1)}, u32[]{:S(2)}, u32[]{:S(2)}) collective-permute-start(bf16[4,72,128]{2,1,0:T(8,128)(2,1)} %get-tuple-element.30), channel_id=1, source_target_pairs={{0,17},{1,16},{16,1},{17,0},{32,49},{33,48},{48,33},{49,32},{64,81... | collective-permute-start | bytes 221192 | tf_op jit(solution)/shard_map/ppermute | solution.py:360
  79.9 30.5 %collective-permute-start.19 = (bf16[144,1024]{1,0:T(8,128)(2,1)}, bf16[144,1024]{1,0:T(8,128)(2,1)S(1)}, u32[]{:S(2)}, u32[]{:S(2)}) collective-permute-start(bf16[144,1024]{1,0:T(8,128)(2,1)} %copy-done), channel_id=1, source_target_pairs={{0,1},{1,0},{2,3},{3,2},{4,5},{5,4},{6,7},{7,6},{8,9},{9,8},{10,11... | collective-permute-start | bytes 884744 | tf_op jit(solution)/shard_map/ppermute | solution.py:239
  82.2 28.3 %collective-permute-start.21 = (bf16[144,1024]{1,0:T(8,128)(2,1)}, bf16[144,1024]{1,0:T(8,128)(2,1)S(1)}, u32[]{:S(2)}, u32[]{:S(2)}) collective-permute-start(bf16[144,1024]{1,0:T(8,128)(2,1)} %copy-done.3), channel_id=1, source_target_pairs={{0,1},{1,0},{2,3},{3,2},{4,5},{5,4},{6,7},{7,6},{8,9},{9,8},{10,11... | collective-permute-start | bytes 884744 | tf_op jit(solution)/shard_map/ppermute | solution.py:239
  85.3 25.2 %collective-permute-start.22 = (bf16[144,1024]{1,0:T(8,128)(2,1)S(1)}, bf16[144,1024]{1,0:T(8,128)(2,1)S(1)}, u32[]{:S(2)}, u32[]{:S(2)}) collective-permute-start(bf16[144,1024]{1,0:T(8,128)(2,1)S(1)} %collective-permute-done.20.refs_5_), channel_id=1, source_target_pairs={{0,4},{2,6},{4,8},{6,10},{8,12},{10,14},{12,0},{14,2},{1,5},{3,7},... | collective-permute-start | bytes 884744 | tf_op jit(solution)/shard_map/ppermute | solution.py:239
  97.7 9.4 %collective-permute-start.11 = (bf16[8,72,128]{2,1,0:T(8,128)(2,1)}, bf16[8,72,128]{2,1,0:T(8,128)(2,1)S(1)}, u32[]{:S(2)}, u32[]{:S(2)}) collective-permute-start(bf16[8,72,128]{2,1,0:T(8,128)(2,1)} %get-tuple-element.34), channel_id=1, source_target_pairs={{0,496},{1,497},{16,32},{17,33},{32,16},{33,17},{48,64},{49,65},{6... | collective-permute-start | bytes 442376 | tf_op jit(solution)/shard_map/ppermute | solution.py:355
  100.1 7.0 %collective-permute-start.12 = (bf16[8,72,128]{2,1,0:T(8,128)(2,1)}, bf16[8,72,128]{2,1,0:T(8,128)(2,1)S(1)}, u32[]{:S(2)}, u32[]{:S(2)}) collective-permute-start(bf16[8,72,128]{2,1,0:T(8,128)(2,1)} %get-tuple-element.35), channel_id=1, source_target_pairs={{0,16},{16,0},{1,17},{17,1},{2,18},{18,2},{3,19},{19,3},{4,20},{20... | collective-permute-start | bytes 442376 | tf_op jit(solution)/shard_map/ppermute | solution.py:239
  115.0 23.9 %all-to-all-start.2 = ((bf16[32,48,128]{2,1,0:T(8,128)(2,1)}), bf16[32,48,128]{2,1,0:T(8,128)(2,1)S(1)}, u32[]{:S(2)}, u32[]{:S(2)}) async-start(bf16[32,48,128]{2,1,0:T(8,128)(2,1)} %shard_map.91), calls=%async_computation.2 | async-start | bytes 786432 | tf_op jit(solution)/shard_map/all_to_all | solution.py:243
  123.0 20.5 %collective-permute-start.13 = (bf16[8,72,192]{2,1,0:T(8,128)(2,1)S(1)}, bf16[8,72,192]{2,1,0:T(8,128)(2,1)S(1)}, u32[]{:S(2)}, u32[]{:S(2)}) collective-permute-start(bf16[8,72,192]{2,1,0:T(8,128)(2,1)S(1)} %copy-done.18), channel_id=1, source_target_pairs={{0,1},{1,0},{2,3},{3,2},{4,5},{5,4},{6,7},{7,6},{8,9},{9,8},{10,11... | collective-permute-start | bytes 663560 | tf_op jit(solution)/shard_map/ppermute | solution.py:239
  138.9 15.7 %all-to-all-start.1 = ((bf16[16,40,128]{2,1,0:T(8,128)(2,1)}), bf16[16,40,128]{2,1,0:T(8,128)(2,1)S(1)}, u32[]{:S(2)}, u32[]{:S(2)}) async-start(bf16[16,40,128]{2,1,0:T(8,128)(2,1)} %get-tuple-element.31), calls=%async_computation.1 | async-start | bytes 327680 | tf_op jit(solution)/shard_map/all_to_all | solution.py:243
  147.1 28.1 %copy-start.12 = (bf16[72,1024]{1,0:T(8,128)(2,1)S(1)}, bf16[72,1024]{1,0:T(8,128)(2,1)}, u32[]{:S(2)}) copy-start(bf16[72,1024]{1,0:T(8,128)(2,1)} %get-tuple-element.40) | copy-start | bytes 442372
  147.1 18.8 %collective-permute-start.16 = (bf16[144,1024]{1,0:T(8,128)(2,1)}, bf16[144,1024]{1,0:T(8,128)(2,1)S(1)}, u32[]{:S(2)}, u32[]{:S(2)}) collective-permute-start(bf16[144,1024]{1,0:T(8,128)(2,1)} %get-tuple-element.42), channel_id=1, source_target_pairs={{0,12},{2,14},{4,0},{6,2},{8,4},{10,6},{12,8},{14,10},{1,13},{3,15... | collective-permute-start | bytes 884744 | tf_op jit(solution)/shard_map/ppermute | solution.py:239
  152.6 22.5 %collective-permute-start.14 = (bf16[144,1024]{1,0:T(8,128)(2,1)}, bf16[144,1024]{1,0:T(8,128)(2,1)S(1)}, u32[]{:S(2)}, u32[]{:S(2)}) collective-permute-start(bf16[144,1024]{1,0:T(8,128)(2,1)} %get-tuple-element.39), channel_id=1, source_target_pairs={{0,4},{2,6},{4,8},{6,10},{8,12},{10,14},{12,0},{14,2},{1,5},{3,7},... | collective-permute-start | bytes 884744 | tf_op jit(solution)/shard_map/ppermute | solution.py:239
  155.4 27.6 %copy-start.11 = (bf16[72,1024]{1,0:T(8,128)(2,1)S(1)}, bf16[72,1024]{1,0:T(8,128)(2,1)}, u32[]{:S(2)}) copy-start(bf16[72,1024]{1,0:T(8,128)(2,1)} %get-tuple-element.38) | copy-start | bytes 442372
  155.4 28.4 %all-to-all-start.3 = ((bf16[32,48,128]{2,1,0:T(8,128)(2,1)}), bf16[32,48,128]{2,1,0:T(8,128)(2,1)S(1)}, u32[]{:S(2)}, u32[]{:S(2)}) async-start(bf16[32,48,128]{2,1,0:T(8,128)(2,1)} %broadcast_in_dim.12), calls=%async_computation.3 | async-start | bytes 786432 | tf_op jit(solution)/shard_map/all_to_all | solution.py:243
  167.0 14.6 %collective-permute-start.18 = (bf16[72,1024]{1,0:T(8,128)(2,1)S(1)}, bf16[72,1024]{1,0:T(8,128)(2,1)S(1)}, u32[]{:S(2)}, u32[]{:S(2)}) collective-permute-start(bf16[72,1024]{1,0:T(8,128)(2,1)S(1)} %get-tuple-element.48), channel_id=1, source_target_pairs={{0,14},{2,0},{4,2},{6,4},{8,6},{10,8},{12,10},{14,12},{1,15},{3,1}... | collective-permute-start | bytes 442376 | tf_op jit(solution)/shard_map/ppermute | solution.py:239
  171.0 10.7 %collective-permute-start.17 = (bf16[72,1024]{1,0:T(8,128)(2,1)S(1)}, bf16[72,1024]{1,0:T(8,128)(2,1)S(1)}, u32[]{:S(2)}, u32[]{:S(2)}) collective-permute-start(bf16[72,1024]{1,0:T(8,128)(2,1)S(1)} %get-tuple-element.47), channel_id=1, source_target_pairs={{0,12},{2,14},{4,0},{6,2},{8,4},{10,6},{12,8},{14,10},{1,13},{3,15... | collective-permute-start | bytes 442376 | tf_op jit(solution)/shard_map/ppermute | solution.py:239
  175.2 7.8 %collective-permute-start.15 = (bf16[72,1024]{1,0:T(8,128)(2,1)S(1)}, bf16[72,1024]{1,0:T(8,128)(2,1)S(1)}, u32[]{:S(2)}, u32[]{:S(2)}) collective-permute-start(bf16[72,1024]{1,0:T(8,128)(2,1)S(1)} %add_convert_fusion.3), channel_id=1, source_target_pairs={{0,2},{2,4},{4,6},{6,8},{8,10},{10,12},{12,14},{14,0},{1,3},{3,5},... | collective-permute-start | bytes 442376 | tf_op jit(solution)/shard_map/ppermute | solution.py:239
  (20 other events, 138.5 us)

commit v6 on v5

--- a/solution.py
+++ b/solution.py
@@ -12,6 +12,9 @@
 LON = ("x", "yh", "core")
 F32 = jnp.float32
 BF16 = jnp.bfloat16
+
+
+DISTANCE = (0, 7, 1, 2, 6, 5, 3, 4)
 
 
 def dot_nt(a, b):
@@ -37,7 +40,7 @@
         out_specs=[pl.BlockSpec(memory_space=pltpu.VMEM) for _ in outs],
         scratch_shapes=list(scratch),
         cost_estimate=pl.CostEstimate(flops=flops, bytes_accessed=moved, transcendentals=0),
-        compiler_params=pltpu.CompilerParams(vmem_limit_bytes=56 << 20),
+        compiler_params=pltpu.CompilerParams(vmem_limit_bytes=12 << 20),
     )
 
 
@@ -87,18 +90,18 @@
 
 
 def project_kernel(
-    table_ref, t0_ref, t1_ref, t2_ref, t3_ref, own_ref, other_ref,
+    place_ref, t0_ref, t1_ref, t2_ref, t3_ref, own_ref, other_ref,
     kv_ref, q_ref, swap_ref, far_ref, near_ref, far2_ref, near2_ref,
     kv32, kv32b,
 ):
-    first_core = table_ref[8] == 0
+    first_core = place_ref[2] == 0
     own, other = turned(own_ref), turned(other_ref)
     for chunk, (a_ref, b_ref) in enumerate(((t0_ref, t1_ref), (t2_ref, t3_ref))):
         rows = jnp.concatenate([a_ref[...], b_ref[...]], axis=0)
         proj = dot_nt(rows, own).astype(BF16).astype(F32)
         proj2 = dot_nt(rows, other).astype(BF16).astype(F32)
         for part in range(4):
-            row = table_ref[chunk * 4 + part]
+            row = lax.rem(place_ref[0] + 8 - DISTANCE[chunk * 4 + part], 8)
             piece = proj[part * TOK : (part + 1) * TOK]
             kv32[row] = piece[:, :128]
             kv_ref[row] = piece[:, :128].astype(BF16)
@@ -120,8 +123,8 @@
     keys, queries, halo, dhalo,
 ):
     scale = HD ** (-0.5)
-    yl = place_ref[0]
-    first_core = place_ref[1] == 0
+    yl = place_ref[1]
+    first_core = place_ref[2] == 0
     far, near = far_ref[...].astype(F32), near_ref[...].astype(F32)
     side = unpack_pair(jnp.where(first_core, near, far), jnp.where(first_core, far, near))
     far, near = far2_ref[...].astype(F32), near2_ref[...].astype(F32)
@@ -185,8 +188,8 @@
 def combine_kernel(
     place_ref, dq_ref, dkv_ref, far_ref, near_ref, pg_ref, mine_ref, swap_ref, pg32
 ):
-    yl = place_ref[0]
-    first_core = place_ref[1] == 0
+    yl = place_ref[1]
+    first_core = place_ref[2] == 0
     far, near = far_ref[...].astype(F32), near_ref[...].astype(F32)
     first, second = unpack_pair(jnp.where(first_core, far, near), jnp.where(first_core, near, far))
     for half, add in ((0, first), (1, second)):
@@ -199,10 +202,11 @@
         swap_ref[row] = pg32[2 * row + 1 - yl].astype(BF16)
 
 
-def share_kernel(table_ref, mine_ref, got_ref, own_ref, other_ref, *out_refs):
+def share_kernel(place_ref, mine_ref, got_ref, own_ref, other_ref, *out_refs):
     own, other = turned(own_ref), turned(other_ref)
     for chunk in range(2):
-        picks = [table_ref[4 * chunk + i] for i in range(4)]
+        reach = (6, 7, 1, 0) if chunk else (5, 4, 3, 2)
+        picks = [lax.rem(place_ref[0] + r, 8) for r in reach]
         rows = jnp.concatenate([mine_ref[p].astype(F32) for p in picks], axis=0).astype(BF16)
         rows2 = jnp.concatenate([got_ref[p].astype(F32) for p in picks], axis=0).astype(BF16)
         part = (dot_nn(rows, own) + dot_nn(rows2, other)).astype(BF16)
@@ -214,12 +218,14 @@
                 out_refs[2 + i][...] = part[i * TOK : (i + 1) * TOK]
 
 
-def weight_grad_kernel(table_ref, pg_ref, *refs):
+def weight_grad_kernel(place_ref, pg_ref, *refs):
     total, piece_ref = None, refs[8]
+    yl = place_ref[1]
     for chunk in range(4):
-        rows = jnp.concatenate(
-            [pg_ref[table_ref[4 * chunk + i]].astype(F32) for i in range(4)], axis=0
-        ).astype(BF16)
+        parity = yl if chunk < 2 else 1 - yl
+        near = DISTANCE[4 * (chunk % 2) : 4 * (chunk % 2) + 4]
+        ranks = [2 * lax.rem(place_ref[0] + 8 - d, 8) + parity for d in near]
+        rows = jnp.concatenate([pg_ref[r].astype(F32) for r in ranks], axis=0).astype(BF16)
         source = jnp.concatenate([refs[2 * chunk][...], refs[2 * chunk + 1][...]], axis=0)
         part = dot_tn(rows, source)
         total = part if total is None else total + part
@@ -255,11 +261,9 @@
     pair2 = shift(pair0, "z", 8, -2)
     pair3 = shift(pair1, "z", 8, 2)
     tokens = (pair0, pair1, pair2, pair3)
-    distance = jnp.array([0, 7, 1, 2, 6, 5, 3, 4], jnp.int32)
     late0, late1 = shift(pair0, "yl", 2, 1), shift(pair1, "yl", 2, 1)
     late2, late3 = shift(pair2, "yl", 2, 1), shift(late1, "z", 8, 2)
-    rows = ((z - distance) % 8).astype(jnp.int32)
-    place = jnp.stack([yl, core])
+    place = jnp.stack([z, yl, core])
 
     (token_grad,) = call(
         token_grad_kernel, [((RANKS, 40, 128), BF16)], n_in=2, flops=2 * TOK * width * width
@@ -274,7 +278,7 @@
         smem=(0,),
         n_in=7,
         flops=2 * 1152 * 192 * width,
-    )(jnp.concatenate([rows, core.reshape(1)]), *tokens, own, other)
+    )(place, *tokens, own, other)
     far, near = send_far(far), shift(near, "core", 2, 1)
     far2, near2 = send_far(far2, 1), send_near(near2, 1)
     swapped = shift(swap, "yl", 2, 1)
@@ -315,19 +319,15 @@
         smem=(0,),
         n_in=10,
         flops=2 * 1152 * 192 * width,
-    )(
-        jnp.concatenate([2 * rows + yl, 2 * rows + 1 - yl]).astype(jnp.int32),
-        pg, *tokens, late0, late1, late2, late3,
-    )
+    )(place, pg, *tokens, late0, late1, late2, late3)
     pieces = exchange(pieces, LON)
-    reach = (5, 4, 3, 2, 6, 7, 1, 0)
     shares = call(
         share_kernel,
         [((2 * TOK, width), BF16)] * 2 + [((TOK, width), BF16)] * 4,
         smem=(0,),
         n_in=5,
         flops=2 * 576 * 384 * width,
-    )(((z + jnp.array(reach, jnp.int32)) % 8).astype(jnp.int32), pg_mine, pg_got, own, other)
+    )(place, pg_mine, pg_got, own, other)
     down, up, s6, s7, s1, s0 = shares
     down, up = shift(down, "z", 8, -2), shift(up, "z", 8, 2)
     s7 = (s7.astype(F32) + down[:TOK].astype(F32)).astype(BF16)

time: 186 us -> 178 us (0.957)
  waiting for transfers between devices: 35.6 us -> 23.2 us
  Pallas kernels: 26.7 us -> 17.7 us
  local copies, waits for them, and re-layouts: 6.64 us -> 15.4 us
  starting transfers between devices: 111 us -> 115 us
    ppermute x19, waiting for transfers between devices: 21.7 us -> 8.05 us  [shift(): lax.ppermute(value, axis, [(i, (i + distance) % size) for i in range(size)])]
    unnamed x52 -> x38, local copies, waits for them, and re-layouts: 5.58 us -> 14.3 us
    ppermute x3, starting transfers between devices: 10.4 us -> 18.1 us  [send_far(): return lax.ppermute(value, LON + ('yl',), routes)]
    ppermute x19, starting transfers between devices: 72.1 us -> 66.8 us  [shift(): lax.ppermute(value, axis, [(i, (i + distance) % size) for i in range(size)])]
    all_to_all x4, starting transfers between devices: 24 us -> 26.2 us  [exchange(): return lax.all_to_all(value, axis, 0, 0, tiled=True)]
  transfers between devices with their start and end apart: 27 -> 27, of which waited for: 5 -> 4; matrix products, arithmetic and copies ran while one was open for 3% -> 3% of each run, Pallas kernels for 13% -> 9%
where the time goes in v6:
time: 178 us; the launch traced here: 176 us
  starting transfers between devices  115 us (65%)
  waiting for transfers between devices  23.2 us (13%)
  Pallas kernels  17.7 us (10%)
  local copies, waits for them, and re-layouts  15.4 us (9%)
  other arithmetic  4.06 us (2%)
    ppermute x19, starting transfers between devices, shift(): lax.ppermute(value, axis, [(i, (i + distance) % size) for i in range(size)])  66.8 us
    all_to_all x4, starting transfers between devices, exchange(): return lax.all_to_all(value, axis, 0, 0, tiled=True)  26.2 us
    ppermute x3, starting transfers between devices, send_far(): return lax.ppermute(value, LON + ('yl',), routes)  18.1 us
    unnamed x38, local copies, waits for them, and re-layouts  14.3 us
    all_to_all x4, waiting for transfers between devices, exchange(): return lax.all_to_all(value, axis, 0, 0, tiled=True)  12.6 us
    ppermute x19, waiting for transfers between devices, shift(): lax.ppermute(value, axis, [(i, (i + distance) % size) for i in range(size)])  8.05 us
    pallas_call x1, Pallas kernels, step(): call(attend_kernel, [((RANKS, 40, 128), BF16), ((RANKS, TOK, HD), F32), (...  7.67 us
  transfers between devices with their start and end apart: 27, of which 4 were waited for; matrix products, arithmetic and copies ran while one was open for 3% of the time, Pallas kernels for 9%

profile of v6, /device:TPU:1, one launch (start us, length us, event | category | flops | bytes accessed | tf_op | source)
XLA Modules:
  0.0 176.1 jit_solution(273434233529623032)
XLA Ops:
  0.6 11.6 %collective-permute-start = (bf16[72,1024]{1,0:T(8,128)(2,1)}, bf16[72,1024]{1,0:T(8,128)(2,1)S(1)}, u32[]{:S(2)}, u32[]{:S(2)}) collective-permute-start(bf16[72,1024]{1,0:T(8,128)(2,1)} %bitcast.35), channel_id=1, source_target_pairs={{0,14},{2,0},{4,2},{6,4},{8,6},{10,8},{12,10},{14,12},{1,15},{3,1}... | collective-permute-start | bytes 442376 | tf_op jit(solution)/shard_map/ppermute | solution.py:245
  12.3 1.9 %collective-permute-start.1 = (bf16[72,1024]{1,0:T(8,128)(2,1)}, bf16[72,1024]{1,0:T(8,128)(2,1)S(1)}, u32[]{:S(2)}, u32[]{:S(2)}) collective-permute-start(bf16[72,1024]{1,0:T(8,128)(2,1)} %bitcast.36), channel_id=1, source_target_pairs={{0,2},{2,4},{4,6},{6,8},{8,10},{10,12},{12,14},{14,0},{1,3},{3,5},... | collective-permute-start | bytes 442376 | tf_op jit(solution)/shard_map/ppermute | solution.py:245
  14.2 1.9 %collective-permute-start.2 = (bf16[72,1024]{1,0:T(8,128)(2,1)}, bf16[72,1024]{1,0:T(8,128)(2,1)S(1)}, u32[]{:S(2)}, u32[]{:S(2)}) collective-permute-start(bf16[72,1024]{1,0:T(8,128)(2,1)} %bitcast.37), channel_id=1, source_target_pairs={{0,4},{2,6},{4,8},{6,10},{8,12},{10,14},{12,0},{14,2},{1,5},{3,7},... | collective-permute-start | bytes 442376 | tf_op jit(solution)/shard_map/ppermute | solution.py:245
  16.1 3.2 %collective-permute-start.5 = (bf16[192,1024]{1,0:T(8,128)(2,1)}, bf16[192,1024]{1,0:T(8,128)(2,1)S(1)}, u32[]{:S(2)}, u32[]{:S(2)}) collective-permute-start(bf16[192,1024]{1,0:T(8,128)(2,1)} %bitcast.26), channel_id=1, source_target_pairs={{0,1},{1,0},{2,3},{3,2},{4,5},{5,4},{6,7},{7,6},{8,9},{9,8},{10,11... | collective-permute-start | bytes 1179656 | tf_op jit(solution)/shard_map/ppermute | solution.py:245
  20.3 5.5 %collective-permute-start.3 = (bf16[144,1024]{1,0:T(8,128)(2,1)S(1)}, bf16[144,1024]{1,0:T(8,128)(2,1)S(1)}, u32[]{:S(2)}, u32[]{:S(2)}) collective-permute-start(bf16[144,1024]{1,0:T(8,128)(2,1)S(1)} %pad_maximum_fusion.t0_ref.refs_0_), channel_id=1, source_target_pairs={{0,12},{2,14},{4,0},{6,2},{8,4},{10,6},{12,8},{14,10},{1,13},{3,15... | collective-permute-start | bytes 884744 | tf_op jit(solution)/shard_map/ppermute | solution.py:245
  25.8 1.9 %collective-permute-start.4 = (bf16[144,1024]{1,0:T(8,128)(2,1)S(1)}, bf16[144,1024]{1,0:T(8,128)(2,1)S(1)}, u32[]{:S(2)}, u32[]{:S(2)}) collective-permute-start(bf16[144,1024]{1,0:T(8,128)(2,1)S(1)} %constant_dynamic-update-slice_fusion.t1_ref.refs_1_), channel_id=1, source_target_pairs={{0,4},{2,6},{4,8},{6,10},{8,12},{10,14},{12,0},{14,2},{1,5},{3,7},... | collective-permute-start | bytes 884744 | tf_op jit(solution)/shard_map/ppermute | solution.py:245
  31.8 6.6 %all-to-all-start = ((bf16[16,40,128]{2,1,0:T(8,128)(2,1)}), bf16[16,40,128]{2,1,0:T(8,128)(2,1)S(1)}, u32[]{:S(2)}, u32[]{:S(2)}) async-start(bf16[16,40,128]{2,1,0:T(8,128)(2,1)} %shard_map.68), calls=%async_computation | async-start | bytes 327680 | tf_op jit(solution)/shard_map/all_to_all | solution.py:249
  38.4 3.3 %collective-permute-start.20 = (bf16[144,1024]{1,0:T(8,128)(2,1)S(1)}, bf16[144,1024]{1,0:T(8,128)(2,1)S(1)}, u32[]{:S(2)}, u32[]{:S(2)}) collective-permute-start(bf16[144,1024]{1,0:T(8,128)(2,1)S(1)} %constant_dynamic-update-slice_fusion.t1_ref.refs_1_), channel_id=1, source_target_pairs={{0,1},{1,0},{2,3},{3,2},{4,5},{5,4},{6,7},{7,6},{8,9},{9,8},{10,11... | collective-permute-start | bytes 884744 | tf_op jit(solution)/shard_map/ppermute | solution.py:245
  41.8 2.1 %shard_map.67 = (bf16[8,72,128]{2,1,0:T(8,128)(2,1)S(1)}, bf16[8,72,64]{2,1,0:T(8,128)(2,1)S(1)}, bf16[8,72,192]{2,1,0:T(8,128)(2,1)}, bf16[4,72,128]{2,1,0:T(8,...) custom-call(s32[3]{0:T(128)S(1)} %pad_add_fusion.place_ref, ...), custom_call_target="tpu_custom_call" | custom-call | flops 452984832 | tf_op jit(solution)/shard_map/pallas_call | solution.py:273
  44.5 2.0 %collective-permute-start.6 = (bf16[8,72,192]{2,1,0:T(8,128)(2,1)}, bf16[8,72,192]{2,1,0:T(8,128)(2,1)}, u32[]{:S(2)}, u32[]{:S(2)}) collective-permute-start(bf16[8,72,192]{2,1,0:T(8,128)(2,1)} %get-tuple-element.26), channel_id=1, source_target_pairs={{0,1},{1,0},{2,3},{3,2},{4,5},{5,4},{6,7},{7,6},{8,9},{9,8},{10,11... | collective-permute-start | bytes 663560 | tf_op jit(solution)/shard_map/ppermute | solution.py:245
  46.6 9.7 %collective-permute-start.7 = (bf16[4,72,128]{2,1,0:T(8,128)(2,1)S(1)}, bf16[4,72,128]{2,1,0:T(8,128)(2,1)S(1)}, u32[]{:S(2)}, u32[]{:S(2)}) collective-permute-start(bf16[4,72,128]{2,1,0:T(8,128)(2,1)S(1)} %get-tuple-element.27), channel_id=1, source_target_pairs={{0,496},{1,497},{16,32},{17,33},{32,16},{33,17},{48,64},{49,65},{6... | collective-permute-start | bytes 221192 | tf_op jit(solution)/shard_map/ppermute | solution.py:355
  56.2 1.9 %collective-permute-start.8 = (bf16[4,72,128]{2,1,0:T(8,128)(2,1)S(1)}, bf16[4,72,128]{2,1,0:T(8,128)(2,1)S(1)}, u32[]{:S(2)}, u32[]{:S(2)}) collective-permute-start(bf16[4,72,128]{2,1,0:T(8,128)(2,1)S(1)} %get-tuple-element.28), channel_id=1, source_target_pairs={{0,16},{16,0},{1,17},{17,1},{2,18},{18,2},{3,19},{19,3},{4,20},{20... | collective-permute-start | bytes 221192 | tf_op jit(solution)/shard_map/ppermute | solution.py:245
  58.2 6.2 %collective-permute-start.9 = (bf16[4,72,128]{2,1,0:T(8,128)(2,1)S(1)}, bf16[4,72,128]{2,1,0:T(8,128)(2,1)S(1)}, u32[]{:S(2)}, u32[]{:S(2)}) collective-permute-start(bf16[4,72,128]{2,1,0:T(8,128)(2,1)S(1)} %get-tuple-element.29), channel_id=1, source_target_pairs={{0,497},{1,496},{16,33},{17,32},{32,17},{33,16},{48,65},{49,64},{6... | collective-permute-start | bytes 221192 | tf_op jit(solution)/shard_map/ppermute | solution.py:355
  64.4 3.5 %collective-permute-start.10 = (bf16[4,72,128]{2,1,0:T(8,128)(2,1)}, bf16[4,72,128]{2,1,0:T(8,128)(2,1)}, u32[]{:S(2)}, u32[]{:S(2)}) collective-permute-start(bf16[4,72,128]{2,1,0:T(8,128)(2,1)} %get-tuple-element.30), channel_id=1, source_target_pairs={{0,17},{1,16},{16,1},{17,0},{32,49},{33,48},{48,33},{49,32},{64,81... | collective-permute-start | bytes 221192 | tf_op jit(solution)/shard_map/ppermute | solution.py:360
  71.1 3.4 %collective-permute-start.21 = (bf16[144,1024]{1,0:T(8,128)(2,1)S(1)}, bf16[144,1024]{1,0:T(8,128)(2,1)S(1)}, u32[]{:S(2)}, u32[]{:S(2)}) collective-permute-start(bf16[144,1024]{1,0:T(8,128)(2,1)S(1)} %collective-permute-done.3.t2_ref.refs_2_), channel_id=1, source_target_pairs={{0,1},{1,0},{2,3},{3,2},{4,5},{5,4},{6,7},{7,6},{8,9},{9,8},{10,11... | collective-permute-start | bytes 884744 | tf_op jit(solution)/shard_map/ppermute | solution.py:245
  80.6 7.7 %shard_map.69 = (bf16[16,40,128]{2,1,0:T(8,128)(2,1)}, f32[16,72,64]{2,1,0:T(8,128)S(1)}, f32[16,72,128]{2,1,0:T(8,128)S(1)}, bf16[8,72,128]{2,1,0:T(8,128)(2,1)S(1)}, bf16[8,72,128]{2,1,0:T(8,128)(2,1)S(1)}) custom-call(s32[3]{0:T(128)S(1)} %pad_add_fusion.place_ref, bf16[8,72,128]{2,1,0:T(8,128)(2,1)S(1)} %get-tuple-element.24.kv_ref, ...), custom_call_target="tpu_custom_call" | custom-call | flops 1019215872 | tf_op jit(solution)/shard_map/pallas_call | solution.py:285
  88.3 2.2 %collective-permute-start.11 = (bf16[8,72,128]{2,1,0:T(8,128)(2,1)S(1)}, bf16[8,72,128]{2,1,0:T(8,128)(2,1)S(1)}, u32[]{:S(2)}, u32[]{:S(2)}) collective-permute-start(bf16[8,72,128]{2,1,0:T(8,128)(2,1)S(1)} %get-tuple-element.34), channel_id=1, source_target_pairs={{0,496},{1,497},{16,32},{17,33},{32,16},{33,17},{48,64},{49,65},{6... | collective-permute-start | bytes 442376 | tf_op jit(solution)/shard_map/ppermute | solution.py:355
  90.5 4.2 %collective-permute-start.12 = (bf16[8,72,128]{2,1,0:T(8,128)(2,1)S(1)}, bf16[8,72,128]{2,1,0:T(8,128)(2,1)S(1)}, u32[]{:S(2)}, u32[]{:S(2)}) collective-permute-start(bf16[8,72,128]{2,1,0:T(8,128)(2,1)S(1)} %get-tuple-element.35), channel_id=1, source_target_pairs={{0,16},{16,0},{1,17},{17,1},{2,18},{18,2},{3,19},{19,3},{4,20},{20... | collective-permute-start | bytes 442376 | tf_op jit(solution)/shard_map/ppermute | solution.py:245
  94.8 2.6 %collective-permute-done.11.far_ref = bf16[8,72,128]{2,1,0:T(8,128)(2,1)S(1)} collective-permute-done((bf16[8,72,128]{2,1,0:T(8,128)(2,1)S(1)}, bf16[8,72,128]{2,1,0:T(8,128)(2,1)S(1)}, u32[]{:S(2)}, u32[]{:S(2)}) %collective-permute-start.11) | collective-permute-done | bytes 147488 | tf_op jit(solution)/shard_map/ppermute | solution.py:355
  99.7 2.3 %shard_map.73 = bf16[32,48,128]{2,1,0:T(8,128)(2,1)} custom-call(s32[3]{0:T(128)S(1)} %pad_add_fusion.place_ref, bf16[16,72,192]{2,1,0:T(8,128)(2,1)S(1)} %get-tuple-element.44.pg_ref, bf16[144,1024]{1,0:T(8,128)(2,1)S(1)} %pad_maximum_fusion.t0_ref.refs_0_, bf16[144,1024]{1,0:T(8,128)(2,1)S(1)} %constant_dynamic-update-slice_fusion.t1_ref.refs_1_, ...), custom_call_target="tpu_custom_call" | custom-call | flops 452984832 | tf_op jit(solution)/shard_map/pallas_call | solution.py:316
  102.0 7.2 %all-to-all-start.2 = ((bf16[32,48,128]{2,1,0:T(8,128)(2,1)}), bf16[32,48,128]{2,1,0:T(8,128)(2,1)}, u32[]{:S(2)}, u32[]{:S(2)}) async-start(bf16[32,48,128]{2,1,0:T(8,128)(2,1)} %shard_map.73), calls=%async_computation.2 | async-start | bytes 786432 | tf_op jit(solution)/shard_map/all_to_all | solution.py:249
  109.2 3.2 %collective-permute-start.13 = (bf16[8,72,192]{2,1,0:T(8,128)(2,1)}, bf16[8,72,192]{2,1,0:T(8,128)(2,1)S(1)}, u32[]{:S(2)}, u32[]{:S(2)}) collective-permute-start(bf16[8,72,192]{2,1,0:T(8,128)(2,1)} %copy-done.7), channel_id=1, source_target_pairs={{0,1},{1,0},{2,3},{3,2},{4,5},{5,4},{6,7},{7,6},{8,9},{9,8},{10,11... | collective-permute-start | bytes 663560 | tf_op jit(solution)/shard_map/ppermute | solution.py:245
  112.4 12.6 %all-to-all-done.2 = bf16[32,48,128]{2,1,0:T(8,128)(2,1)} async-done(((bf16[32,48,128]{2,1,0:T(8,128)(2,1)}), bf16[32,48,128]{2,1,0:T(8,128)(2,1)}, u32[]{:S(2)}, u32[]{:S(2)}) %all-to-all-start.2) | async-done | bytes 393248 | tf_op jit(solution)/shard_map/all_to_all | solution.py:249
  125.0 8.0 %all-to-all-start.1 = ((bf16[16,40,128]{2,1,0:T(8,128)(2,1)}), bf16[16,40,128]{2,1,0:T(8,128)(2,1)S(1)}, u32[]{:S(2)}, u32[]{:S(2)}) async-start(bf16[16,40,128]{2,1,0:T(8,128)(2,1)} %get-tuple-element.31), calls=%async_computation.1 | async-start | bytes 327680 | tf_op jit(solution)/shard_map/all_to_all | solution.py:249
  138.2 5.4 %collective-permute-start.16 = (bf16[144,1024]{1,0:T(8,128)(2,1)}, bf16[144,1024]{1,0:T(8,128)(2,1)}, u32[]{:S(2)}, u32[]{:S(2)}) collective-permute-start(bf16[144,1024]{1,0:T(8,128)(2,1)} %get-tuple-element.42), channel_id=1, source_target_pairs={{0,12},{2,14},{4,0},{6,2},{8,4},{10,6},{12,8},{14,10},{1,13},{3,15... | collective-permute-start | bytes 884744 | tf_op jit(solution)/shard_map/ppermute | solution.py:245
  143.6 1.9 %collective-permute-start.14 = (bf16[144,1024]{1,0:T(8,128)(2,1)}, bf16[144,1024]{1,0:T(8,128)(2,1)S(1)}, u32[]{:S(2)}, u32[]{:S(2)}) collective-permute-start(bf16[144,1024]{1,0:T(8,128)(2,1)} %get-tuple-element.39), channel_id=1, source_target_pairs={{0,4},{2,6},{4,8},{6,10},{8,12},{10,14},{12,0},{14,2},{1,5},{3,7},... | collective-permute-start | bytes 884744 | tf_op jit(solution)/shard_map/ppermute | solution.py:245
  147.4 4.4 %all-to-all-start.3 = ((bf16[32,48,128]{2,1,0:T(8,128)(2,1)}), bf16[32,48,128]{2,1,0:T(8,128)(2,1)S(1)}, u32[]{:S(2)}, u32[]{:S(2)}) async-start(bf16[32,48,128]{2,1,0:T(8,128)(2,1)} %broadcast_in_dim.12), calls=%async_computation.3 | async-start | bytes 786432 | tf_op jit(solution)/shard_map/all_to_all | solution.py:249
  151.8 5.0 %collective-permute-done.16 = bf16[144,1024]{1,0:T(8,128)(2,1)} collective-permute-done((bf16[144,1024]{1,0:T(8,128)(2,1)}, bf16[144,1024]{1,0:T(8,128)(2,1)}, u32[]{:S(2)}, u32[]{:S(2)}) %collective-permute-start.16) | collective-permute-done | bytes 294944 | tf_op jit(solution)/shard_map/ppermute | solution.py:245
  157.9 1.9 %collective-permute-start.18 = (bf16[72,1024]{1,0:T(8,128)(2,1)S(1)}, bf16[72,1024]{1,0:T(8,128)(2,1)S(1)}, u32[]{:S(2)}, u32[]{:S(2)}) collective-permute-start(bf16[72,1024]{1,0:T(8,128)(2,1)S(1)} %get-tuple-element.46), channel_id=1, source_target_pairs={{0,14},{2,0},{4,2},{6,4},{8,6},{10,8},{12,10},{14,12},{1,15},{3,1}... | collective-permute-start | bytes 442376 | tf_op jit(solution)/shard_map/ppermute | solution.py:245
  159.8 6.4 %collective-permute-start.17 = (bf16[72,1024]{1,0:T(8,128)(2,1)S(1)}, bf16[72,1024]{1,0:T(8,128)(2,1)S(1)}, u32[]{:S(2)}, u32[]{:S(2)}) collective-permute-start(bf16[72,1024]{1,0:T(8,128)(2,1)S(1)} %get-tuple-element.45), channel_id=1, source_target_pairs={{0,12},{2,14},{4,0},{6,2},{8,4},{10,6},{12,8},{14,10},{1,13},{3,15... | collective-permute-start | bytes 442376 | tf_op jit(solution)/shard_map/ppermute | solution.py:245
  166.3 3.4 %collective-permute-start.15 = (bf16[72,1024]{1,0:T(8,128)(2,1)S(1)}, bf16[72,1024]{1,0:T(8,128)(2,1)S(1)}, u32[]{:S(2)}, u32[]{:S(2)}) collective-permute-start(bf16[72,1024]{1,0:T(8,128)(2,1)S(1)} %add_convert_fusion.3), channel_id=1, source_target_pairs={{0,2},{2,4},{4,6},{6,8},{8,10},{10,12},{12,14},{14,0},{1,3},{3,5},... | collective-permute-start | bytes 442376 | tf_op jit(solution)/shard_map/ppermute | solution.py:245
  171.0 3.0 %collective-permute-done.15 = bf16[72,1024]{1,0:T(8,128)(2,1)S(1)} collective-permute-done((bf16[72,1024]{1,0:T(8,128)(2,1)S(1)}, bf16[72,1024]{1,0:T(8,128)(2,1)S(1)}, u32[]{:S(2)}, u32[]{:S(2)}) %collective-permute-start.15) | collective-permute-done | bytes 147488 | tf_op jit(solution)/shard_map/ppermute | solution.py:245
  (77 shorter events, 29.0 us)
Async XLA Ops:
  0.6 41.2 %copy-start.2 = (bf16[1,1024,192]{1,2,0:T(8,128)(2,1)S(1)}, bf16[1,1024,192]{1,2,0:T(8,128)(2,1)}, u32[]{:S(2)}) copy-start(bf16[1,1024,192]{1,2,0:T(8,128)(2,1)} %param.6) | copy-start | bytes 1179652
  0.6 18.7 %collective-permute-start = (bf16[72,1024]{1,0:T(8,128)(2,1)}, bf16[72,1024]{1,0:T(8,128)(2,1)S(1)}, u32[]{:S(2)}, u32[]{:S(2)}) collective-permute-start(bf16[72,1024]{1,0:T(8,128)(2,1)} %bitcast.35), channel_id=1, source_target_pairs={{0,14},{2,0},{4,2},{6,4},{8,6},{10,8},{12,10},{14,12},{1,15},{3,1}... | collective-permute-start | bytes 442376 | tf_op jit(solution)/shard_map/ppermute | solution.py:245
  12.3 13.5 %collective-permute-start.1 = (bf16[72,1024]{1,0:T(8,128)(2,1)}, bf16[72,1024]{1,0:T(8,128)(2,1)S(1)}, u32[]{:S(2)}, u32[]{:S(2)}) collective-permute-start(bf16[72,1024]{1,0:T(8,128)(2,1)} %bitcast.36), channel_id=1, source_target_pairs={{0,2},{2,4},{4,6},{6,8},{8,10},{10,12},{12,14},{14,0},{1,3},{3,5},... | collective-permute-start | bytes 442376 | tf_op jit(solution)/shard_map/ppermute | solution.py:245
  14.2 11.6 %collective-permute-start.2 = (bf16[72,1024]{1,0:T(8,128)(2,1)}, bf16[72,1024]{1,0:T(8,128)(2,1)S(1)}, u32[]{:S(2)}, u32[]{:S(2)}) collective-permute-start(bf16[72,1024]{1,0:T(8,128)(2,1)} %bitcast.37), channel_id=1, source_target_pairs={{0,4},{2,6},{4,8},{6,10},{8,12},{10,14},{12,0},{14,2},{1,5},{3,7},... | collective-permute-start | bytes 442376 | tf_op jit(solution)/shard_map/ppermute | solution.py:245
  16.1 25.7 %collective-permute-start.5 = (bf16[192,1024]{1,0:T(8,128)(2,1)}, bf16[192,1024]{1,0:T(8,128)(2,1)S(1)}, u32[]{:S(2)}, u32[]{:S(2)}) collective-permute-start(bf16[192,1024]{1,0:T(8,128)(2,1)} %bitcast.26), channel_id=1, source_target_pairs={{0,1},{1,0},{2,3},{3,2},{4,5},{5,4},{6,7},{7,6},{8,9},{9,8},{10,11... | collective-permute-start | bytes 1179656 | tf_op jit(solution)/shard_map/ppermute | solution.py:245
  20.3 21.5 %collective-permute-start.3 = (bf16[144,1024]{1,0:T(8,128)(2,1)S(1)}, bf16[144,1024]{1,0:T(8,128)(2,1)S(1)}, u32[]{:S(2)}, u32[]{:S(2)}) collective-permute-start(bf16[144,1024]{1,0:T(8,128)(2,1)S(1)} %pad_maximum_fusion.t0_ref.refs_0_), channel_id=1, source_target_pairs={{0,12},{2,14},{4,0},{6,2},{8,4},{10,6},{12,8},{14,10},{1,13},{3,15... | collective-permute-start | bytes 884744 | tf_op jit(solution)/shard_map/ppermute | solution.py:245
  25.8 16.0 %collective-permute-start.4 = (bf16[144,1024]{1,0:T(8,128)(2,1)S(1)}, bf16[144,1024]{1,0:T(8,128)(2,1)S(1)}, u32[]{:S(2)}, u32[]{:S(2)}) collective-permute-start(bf16[144,1024]{1,0:T(8,128)(2,1)S(1)} %constant_dynamic-update-slice_fusion.t1_ref.refs_1_), channel_id=1, source_target_pairs={{0,4},{2,6},{4,8},{6,10},{8,12},{10,14},{12,0},{14,2},{1,5},{3,7},... | collective-permute-start | bytes 884744 | tf_op jit(solution)/shard_map/ppermute | solution.py:245
  27.7 1.6 copy-start
  31.8 45.2 %all-to-all-start = ((bf16[16,40,128]{2,1,0:T(8,128)(2,1)}), bf16[16,40,128]{2,1,0:T(8,128)(2,1)S(1)}, u32[]{:S(2)}, u32[]{:S(2)}) async-start(bf16[16,40,128]{2,1,0:T(8,128)(2,1)} %shard_map.68), calls=%async_computation | async-start | bytes 327680 | tf_op jit(solution)/shard_map/all_to_all | solution.py:249
  38.4 26.0 %collective-permute-start.20 = (bf16[144,1024]{1,0:T(8,128)(2,1)S(1)}, bf16[144,1024]{1,0:T(8,128)(2,1)S(1)}, u32[]{:S(2)}, u32[]{:S(2)}) collective-permute-start(bf16[144,1024]{1,0:T(8,128)(2,1)S(1)} %constant_dynamic-update-slice_fusion.t1_ref.refs_1_), channel_id=1, source_target_pairs={{0,1},{1,0},{2,3},{3,2},{4,5},{5,4},{6,7},{7,6},{8,9},{9,8},{10,11... | collective-permute-start | bytes 884744 | tf_op jit(solution)/shard_map/ppermute | solution.py:245
  44.5 32.5 %collective-permute-start.6 = (bf16[8,72,192]{2,1,0:T(8,128)(2,1)}, bf16[8,72,192]{2,1,0:T(8,128)(2,1)}, u32[]{:S(2)}, u32[]{:S(2)}) collective-permute-start(bf16[8,72,192]{2,1,0:T(8,128)(2,1)} %get-tuple-element.26), channel_id=1, source_target_pairs={{0,1},{1,0},{2,3},{3,2},{4,5},{5,4},{6,7},{7,6},{8,9},{9,8},{10,11... | collective-permute-start | bytes 663560 | tf_op jit(solution)/shard_map/ppermute | solution.py:245
  46.6 21.4 %collective-permute-start.7 = (bf16[4,72,128]{2,1,0:T(8,128)(2,1)S(1)}, bf16[4,72,128]{2,1,0:T(8,128)(2,1)S(1)}, u32[]{:S(2)}, u32[]{:S(2)}) collective-permute-start(bf16[4,72,128]{2,1,0:T(8,128)(2,1)S(1)} %get-tuple-element.27), channel_id=1, source_target_pairs={{0,496},{1,497},{16,32},{17,33},{32,16},{33,17},{48,64},{49,65},{6... | collective-permute-start | bytes 221192 | tf_op jit(solution)/shard_map/ppermute | solution.py:355
  56.2 14.2 %collective-permute-start.8 = (bf16[4,72,128]{2,1,0:T(8,128)(2,1)S(1)}, bf16[4,72,128]{2,1,0:T(8,128)(2,1)S(1)}, u32[]{:S(2)}, u32[]{:S(2)}) collective-permute-start(bf16[4,72,128]{2,1,0:T(8,128)(2,1)S(1)} %get-tuple-element.28), channel_id=1, source_target_pairs={{0,16},{16,0},{1,17},{17,1},{2,18},{18,2},{3,19},{19,3},{4,20},{20... | collective-permute-start | bytes 221192 | tf_op jit(solution)/shard_map/ppermute | solution.py:245
  58.2 16.3 %collective-permute-start.9 = (bf16[4,72,128]{2,1,0:T(8,128)(2,1)S(1)}, bf16[4,72,128]{2,1,0:T(8,128)(2,1)S(1)}, u32[]{:S(2)}, u32[]{:S(2)}) collective-permute-start(bf16[4,72,128]{2,1,0:T(8,128)(2,1)S(1)} %get-tuple-element.29), channel_id=1, source_target_pairs={{0,497},{1,496},{16,33},{17,32},{32,17},{33,16},{48,65},{49,64},{6... | collective-permute-start | bytes 221192 | tf_op jit(solution)/shard_map/ppermute | solution.py:355
  64.4 12.6 %collective-permute-start.10 = (bf16[4,72,128]{2,1,0:T(8,128)(2,1)}, bf16[4,72,128]{2,1,0:T(8,128)(2,1)}, u32[]{:S(2)}, u32[]{:S(2)}) collective-permute-start(bf16[4,72,128]{2,1,0:T(8,128)(2,1)} %get-tuple-element.30), channel_id=1, source_target_pairs={{0,17},{1,16},{16,1},{17,0},{32,49},{33,48},{48,33},{49,32},{64,81... | collective-permute-start | bytes 221192 | tf_op jit(solution)/shard_map/ppermute | solution.py:360
  68.6 30.4 %collective-permute-start.19 = (bf16[144,1024]{1,0:T(8,128)(2,1)S(1)}, bf16[144,1024]{1,0:T(8,128)(2,1)S(1)}, u32[]{:S(2)}, u32[]{:S(2)}) collective-permute-start(bf16[144,1024]{1,0:T(8,128)(2,1)S(1)} %pad_maximum_fusion.t0_ref.refs_0_), channel_id=1, source_target_pairs={{0,1},{1,0},{2,3},{3,2},{4,5},{5,4},{6,7},{7,6},{8,9},{9,8},{10,11... | collective-permute-start | bytes 884744 | tf_op jit(solution)/shard_map/ppermute | solution.py:245
  71.1 27.9 %collective-permute-start.21 = (bf16[144,1024]{1,0:T(8,128)(2,1)S(1)}, bf16[144,1024]{1,0:T(8,128)(2,1)S(1)}, u32[]{:S(2)}, u32[]{:S(2)}) collective-permute-start(bf16[144,1024]{1,0:T(8,128)(2,1)S(1)} %collective-permute-done.3.t2_ref.refs_2_), channel_id=1, source_target_pairs={{0,1},{1,0},{2,3},{3,2},{4,5},{5,4},{6,7},{7,6},{8,9},{9,8},{10,11... | collective-permute-start | bytes 884744 | tf_op jit(solution)/shard_map/ppermute | solution.py:245
  75.1 23.9 %collective-permute-start.22 = (bf16[144,1024]{1,0:T(8,128)(2,1)S(1)}, bf16[144,1024]{1,0:T(8,128)(2,1)S(1)}, u32[]{:S(2)}, u32[]{:S(2)}) collective-permute-start(bf16[144,1024]{1,0:T(8,128)(2,1)S(1)} %collective-permute-done.20.refs_5_), channel_id=1, source_target_pairs={{0,4},{2,6},{4,8},{6,10},{8,12},{10,14},{12,0},{14,2},{1,5},{3,7},... | collective-permute-start | bytes 884744 | tf_op jit(solution)/shard_map/ppermute | solution.py:245
  88.3 9.0 %collective-permute-start.11 = (bf16[8,72,128]{2,1,0:T(8,128)(2,1)S(1)}, bf16[8,72,128]{2,1,0:T(8,128)(2,1)S(1)}, u32[]{:S(2)}, u32[]{:S(2)}) collective-permute-start(bf16[8,72,128]{2,1,0:T(8,128)(2,1)S(1)} %get-tuple-element.34), channel_id=1, source_target_pairs={{0,496},{1,497},{16,32},{17,33},{32,16},{33,17},{48,64},{49,65},{6... | collective-permute-start | bytes 442376 | tf_op jit(solution)/shard_map/ppermute | solution.py:355
  90.5 6.8 %collective-permute-start.12 = (bf16[8,72,128]{2,1,0:T(8,128)(2,1)S(1)}, bf16[8,72,128]{2,1,0:T(8,128)(2,1)S(1)}, u32[]{:S(2)}, u32[]{:S(2)}) collective-permute-start(bf16[8,72,128]{2,1,0:T(8,128)(2,1)S(1)} %get-tuple-element.35), channel_id=1, source_target_pairs={{0,16},{16,0},{1,17},{17,1},{2,18},{18,2},{3,19},{19,3},{4,20},{20... | collective-permute-start | bytes 442376 | tf_op jit(solution)/shard_map/ppermute | solution.py:245
  102.0 23.0 %all-to-all-start.2 = ((bf16[32,48,128]{2,1,0:T(8,128)(2,1)}), bf16[32,48,128]{2,1,0:T(8,128)(2,1)}, u32[]{:S(2)}, u32[]{:S(2)}) async-start(bf16[32,48,128]{2,1,0:T(8,128)(2,1)} %shard_map.73), calls=%async_computation.2 | async-start | bytes 786432 | tf_op jit(solution)/shard_map/all_to_all | solution.py:249
  109.2 23.8 %collective-permute-start.13 = (bf16[8,72,192]{2,1,0:T(8,128)(2,1)}, bf16[8,72,192]{2,1,0:T(8,128)(2,1)S(1)}, u32[]{:S(2)}, u32[]{:S(2)}) collective-permute-start(bf16[8,72,192]{2,1,0:T(8,128)(2,1)} %copy-done.7), channel_id=1, source_target_pairs={{0,1},{1,0},{2,3},{3,2},{4,5},{5,4},{6,7},{7,6},{8,9},{9,8},{10,11... | collective-permute-start | bytes 663560 | tf_op jit(solution)/shard_map/ppermute | solution.py:245
  125.0 21.6 %all-to-all-start.1 = ((bf16[16,40,128]{2,1,0:T(8,128)(2,1)}), bf16[16,40,128]{2,1,0:T(8,128)(2,1)S(1)}, u32[]{:S(2)}, u32[]{:S(2)}) async-start(bf16[16,40,128]{2,1,0:T(8,128)(2,1)} %get-tuple-element.31), calls=%async_computation.1 | async-start | bytes 327680 | tf_op jit(solution)/shard_map/all_to_all | solution.py:249
  133.7 1.0 copy-start.6
  134.7 1.0 copy-start.9
  135.7 34.0 %copy-start.1 = (bf16[16,64,1024]{2,1,0:T(8,128)(2,1)S(1)}, bf16[16,64,1024]{2,1,0:T(8,128)(2,1)}, u32[]{:S(2)}) copy-start(bf16[16,64,1024]{2,1,0:T(8,128)(2,1)} %weight_ref.1) | copy-start | bytes 6291460
  138.2 18.6 %collective-permute-start.16 = (bf16[144,1024]{1,0:T(8,128)(2,1)}, bf16[144,1024]{1,0:T(8,128)(2,1)}, u32[]{:S(2)}, u32[]{:S(2)}) collective-permute-start(bf16[144,1024]{1,0:T(8,128)(2,1)} %get-tuple-element.42), channel_id=1, source_target_pairs={{0,12},{2,14},{4,0},{6,2},{8,4},{10,6},{12,8},{14,10},{1,13},{3,15... | collective-permute-start | bytes 884744 | tf_op jit(solution)/shard_map/ppermute | solution.py:245
  143.6 22.6 %collective-permute-start.14 = (bf16[144,1024]{1,0:T(8,128)(2,1)}, bf16[144,1024]{1,0:T(8,128)(2,1)S(1)}, u32[]{:S(2)}, u32[]{:S(2)}) collective-permute-start(bf16[144,1024]{1,0:T(8,128)(2,1)} %get-tuple-element.39), channel_id=1, source_target_pairs={{0,4},{2,6},{4,8},{6,10},{8,12},{10,14},{12,0},{14,2},{1,5},{3,7},... | collective-permute-start | bytes 884744 | tf_op jit(solution)/shard_map/ppermute | solution.py:245
  147.4 27.4 %all-to-all-start.3 = ((bf16[32,48,128]{2,1,0:T(8,128)(2,1)}), bf16[32,48,128]{2,1,0:T(8,128)(2,1)S(1)}, u32[]{:S(2)}, u32[]{:S(2)}) async-start(bf16[32,48,128]{2,1,0:T(8,128)(2,1)} %broadcast_in_dim.12), calls=%async_computation.3 | async-start | bytes 786432 | tf_op jit(solution)/shard_map/all_to_all | solution.py:249
  157.9 13.0 %collective-permute-start.18 = (bf16[72,1024]{1,0:T(8,128)(2,1)S(1)}, bf16[72,1024]{1,0:T(8,128)(2,1)S(1)}, u32[]{:S(2)}, u32[]{:S(2)}) collective-permute-start(bf16[72,1024]{1,0:T(8,128)(2,1)S(1)} %get-tuple-element.46), channel_id=1, source_target_pairs={{0,14},{2,0},{4,2},{6,4},{8,6},{10,8},{12,10},{14,12},{1,15},{3,1}... | collective-permute-start | bytes 442376 | tf_op jit(solution)/shard_map/ppermute | solution.py:245
  159.8 11.1 %collective-permute-start.17 = (bf16[72,1024]{1,0:T(8,128)(2,1)S(1)}, bf16[72,1024]{1,0:T(8,128)(2,1)S(1)}, u32[]{:S(2)}, u32[]{:S(2)}) collective-permute-start(bf16[72,1024]{1,0:T(8,128)(2,1)S(1)} %get-tuple-element.45), channel_id=1, source_target_pairs={{0,12},{2,14},{4,0},{6,2},{8,4},{10,6},{12,8},{14,10},{1,13},{3,15... | collective-permute-start | bytes 442376 | tf_op jit(solution)/shard_map/ppermute | solution.py:245
  166.3 7.7 %collective-permute-start.15 = (bf16[72,1024]{1,0:T(8,128)(2,1)S(1)}, bf16[72,1024]{1,0:T(8,128)(2,1)S(1)}, u32[]{:S(2)}, u32[]{:S(2)}) collective-permute-start(bf16[72,1024]{1,0:T(8,128)(2,1)S(1)} %add_convert_fusion.3), channel_id=1, source_target_pairs={{0,2},{2,4},{4,6},{6,8},{8,10},{10,12},{12,14},{14,0},{1,3},{3,5},... | collective-permute-start | bytes 442376 | tf_op jit(solution)/shard_map/ppermute | solution.py:245
  (13 other events, 9.8 us)

commit v7 on v6

--- a/solution.py
+++ b/solution.py
@@ -29,7 +29,7 @@
     return lax.dot_general(a, b, (((0,), (0,)), ((), ())), preferred_element_type=F32)
 
 
-def call(body, outs, scratch=(), smem=(), n_in=1, flops=0, moved=0):
+def call(body, outs, scratch=(), smem=(), n_in=1, flops=0, moved=0, grant=56):
     specs = [
         pl.BlockSpec(memory_space=pltpu.SMEM if i in smem else pltpu.VMEM) for i in range(n_in)
     ]
@@ -40,7 +40,7 @@
         out_specs=[pl.BlockSpec(memory_space=pltpu.VMEM) for _ in outs],
         scratch_shapes=list(scratch),
         cost_estimate=pl.CostEstimate(flops=flops, bytes_accessed=moved, transcendentals=0),
-        compiler_params=pltpu.CompilerParams(vmem_limit_bytes=12 << 20),
+        compiler_params=pltpu.CompilerParams(vmem_limit_bytes=grant << 20),
     )
 
 
@@ -277,6 +277,7 @@
         scratch=[pltpu.VMEM((8, TOK, 128), F32)] * 2,
         smem=(0,),
         n_in=7,
+        grant=12,
         flops=2 * 1152 * 192 * width,
     )(place, *tokens, own, other)
     far, near = send_far(far), shift(near, "core", 2, 1)
@@ -337,12 +338,15 @@
     shares = [s0, up[TOK:], shift(s1, "z", 8, 1)] + shares
     summed = jnp.sum(pieces.astype(F32), axis=0).astype(BF16)
     copies = exchange(jnp.broadcast_to(summed[None], (32, 48, 128)), LON)
-    (mixed,) = call(mix_kernel, [((TOK, width), BF16)], n_in=2, flops=2 * TOK * width * width)(
+    (mixed,) = call(
+        mix_kernel, [((TOK, width), BF16)], n_in=2, flops=2 * TOK * width * width, grant=12
+    )(
         token_att, out_weight.reshape(width, width)
     )
+    grad = copies.reshape(4, 8, 48, 128).transpose(0, 2, 1, 3).reshape(3 * HD, width).astype(F32)
+    grad, *shares = lax.optimization_barrier((grad, *shares))
     latent_grad = sum(s.astype(F32) for s in shares).astype(BF16)
-    grad = copies.reshape(4, 8, 48, 128).transpose(0, 2, 1, 3).reshape(3 * HD, width)
-    qkv_grad = jnp.swapaxes(grad, 0, 1).astype(F32)[None]
+    qkv_grad = jnp.swapaxes(grad, 0, 1)[None]
     return mixed.reshape(latents.shape), latent_grad.reshape(latents.shape), qkv_grad
 
 

time: 178 us -> 186 us (1.045)
  blocking collectives: 0 us -> 24 us
  waiting for transfers between devices: 23.2 us -> 14.1 us
  local copies, waits for them, and re-layouts: 15.4 us -> 6.54 us
  Pallas kernels: 17.7 us -> 23.4 us
  other arithmetic: 4.06 us -> 2.02 us
  starting transfers between devices: 115 us -> 113 us
    all_to_all x0 -> x1, blocking collectives: none -> 24 us  [exchange(): return lax.all_to_all(value, axis, 0, 0, tiled=True)]
    all_to_all x4 -> x3, waiting for transfers between devices: 12.6 us -> 0.01 us  [exchange(): return lax.all_to_all(value, axis, 0, 0, tiled=True)]
    unnamed x38 -> x56, local copies, waits for them, and re-layouts: 14.3 us -> 5.47 us
    ppermute x3, starting transfers between devices: 18.1 us -> 10.1 us  [send_far(): return lax.ppermute(value, LON + ('yl',), routes)]
    all_to_all x4 -> x3, starting transfers between devices: 26.2 us -> 18.9 us  [exchange(): return lax.all_to_all(value, axis, 0, 0, tiled=True)]
    ppermute x19, starting transfers between devices: 66.8 us -> 74 us  [shift(): lax.ppermute(value, axis, [(i, (i + distance) % size) for i in range(size)])]
    ppermute x1, starting transfers between devices: 3.48 us -> 10.3 us  [send_near(): return lax.ppermute(value, LON + ('yl',), routes)]
    ppermute x19, waiting for transfers between devices: 8.05 us -> 14.1 us  [shift(): lax.ppermute(value, axis, [(i, (i + distance) % size) for i in range(size)])]
  transfers between devices with their start and end apart: 27 -> 26, of which waited for: 4 -> 5; matrix products, arithmetic and copies ran while one was open for 3% -> 2% of each run, Pallas kernels for 9% -> 11%
where the time goes in v7:
time: 186 us; the launch traced here: 185 us
  starting transfers between devices  113 us (61%)
  blocking collectives  24 us (13%)
  Pallas kernels  23.4 us (13%)
  waiting for transfers between devices  14.1 us (8%)
  local copies, waits for them, and re-layouts  6.54 us (4%)
  other arithmetic  2.02 us (1%)
    ppermute x19, starting transfers between devices, shift(): lax.ppermute(value, axis, [(i, (i + distance) % size) for i in range(size)])  74 us
    all_to_all x1, blocking collectives, exchange(): return lax.all_to_all(value, axis, 0, 0, tiled=True)  24 us
    all_to_all x3, starting transfers between devices, exchange(): return lax.all_to_all(value, axis, 0, 0, tiled=True)  18.9 us
    ppermute x19, waiting for transfers between devices, shift(): lax.ppermute(value, axis, [(i, (i + distance) % size) for i in range(size)])  14.1 us
    ppermute x1, starting transfers between devices, send_near(): return lax.ppermute(value, LON + ('yl',), routes)  10.3 us
    ppermute x3, starting transfers between devices, send_far(): return lax.ppermute(value, LON + ('yl',), routes)  10.1 us
    pallas_call x1, Pallas kernels, step(): call(attend_kernel, [((RANKS, 40, 128), BF16), ((RANKS, TOK, HD), F32), (...  8.33 us
    unnamed x56, local copies, waits for them, and re-layouts  5.47 us
  transfers between devices with their start and end apart: 26, of which 5 were waited for; matrix products, arithmetic and copies ran while one was open for 2% of the time, Pallas kernels for 11%

profile of v7, /device:TPU:1, one launch (start us, length us, event | category | flops | bytes accessed | tf_op | source)
XLA Modules:
  0.0 184.6 jit_solution(14009949282794452285)
XLA Ops:
  0.6 11.6 %collective-permute-start = (bf16[72,1024]{1,0:T(8,128)(2,1)}, bf16[72,1024]{1,0:T(8,128)(2,1)S(1)}, u32[]{:S(2)}, u32[]{:S(2)}) collective-permute-start(bf16[72,1024]{1,0:T(8,128)(2,1)} %bitcast.33), channel_id=1, source_target_pairs={{0,14},{2,0},{4,2},{6,4},{8,6},{10,8},{12,10},{14,12},{1,15},{3,1}... | collective-permute-start | bytes 442376 | tf_op jit(solution)/shard_map/ppermute | solution.py:245
  12.3 1.9 %collective-permute-start.1 = (bf16[72,1024]{1,0:T(8,128)(2,1)}, bf16[72,1024]{1,0:T(8,128)(2,1)S(1)}, u32[]{:S(2)}, u32[]{:S(2)}) collective-permute-start(bf16[72,1024]{1,0:T(8,128)(2,1)} %bitcast.34), channel_id=1, source_target_pairs={{0,2},{2,4},{4,6},{6,8},{8,10},{10,12},{12,14},{14,0},{1,3},{3,5},... | collective-permute-start | bytes 442376 | tf_op jit(solution)/shard_map/ppermute | solution.py:245
  16.1 3.2 %collective-permute-start.5 = (bf16[192,1024]{1,0:T(8,128)(2,1)}, bf16[192,1024]{1,0:T(8,128)(2,1)S(1)}, u32[]{:S(2)}, u32[]{:S(2)}) collective-permute-start(bf16[192,1024]{1,0:T(8,128)(2,1)} %bitcast.24), channel_id=1, source_target_pairs={{0,1},{1,0},{2,3},{3,2},{4,5},{5,4},{6,7},{7,6},{8,9},{9,8},{10,11... | collective-permute-start | bytes 1179656 | tf_op jit(solution)/shard_map/ppermute | solution.py:245
  20.3 5.5 %collective-permute-start.3 = (bf16[144,1024]{1,0:T(8,128)(2,1)S(1)}, bf16[144,1024]{1,0:T(8,128)(2,1)S(1)}, u32[]{:S(2)}, u32[]{:S(2)}) collective-permute-start(bf16[144,1024]{1,0:T(8,128)(2,1)S(1)} %pad_maximum_fusion.t0_ref.refs_0_), channel_id=1, source_target_pairs={{0,12},{2,14},{4,0},{6,2},{8,4},{10,6},{12,8},{14,10},{1,13},{3,15... | collective-permute-start | bytes 884744 | tf_op jit(solution)/shard_map/ppermute | solution.py:245
  25.8 1.9 %collective-permute-start.4 = (bf16[144,1024]{1,0:T(8,128)(2,1)S(1)}, bf16[144,1024]{1,0:T(8,128)(2,1)S(1)}, u32[]{:S(2)}, u32[]{:S(2)}) collective-permute-start(bf16[144,1024]{1,0:T(8,128)(2,1)S(1)} %constant_dynamic-update-slice_fusion.t1_ref.refs_1_), channel_id=1, source_target_pairs={{0,4},{2,6},{4,8},{6,10},{8,12},{10,14},{12,0},{14,2},{1,5},{3,7},... | collective-permute-start | bytes 884744 | tf_op jit(solution)/shard_map/ppermute | solution.py:245
  27.8 3.3 %shard_map.68 = bf16[16,40,128]{2,1,0:T(8,128)(2,1)} custom-call(bf16[72,1024]{1,0:T(8,128)(2,1)} %bitcast.30, bf16[16,64,1024]{2,1,0:T(8,128)(2,1)} %weight_ref.1), custom_call_target="tpu_custom_call" | custom-call | flops 150994944 | tf_op jit(solution)/shard_map/pallas_call | solution.py:268
  31.0 6.6 %all-to-all-start = ((bf16[16,40,128]{2,1,0:T(8,128)(2,1)}), bf16[16,40,128]{2,1,0:T(8,128)(2,1)S(1)}, u32[]{:S(2)}, u32[]{:S(2)}) async-start(bf16[16,40,128]{2,1,0:T(8,128)(2,1)} %shard_map.68), calls=%async_computation | async-start | bytes 327680 | tf_op jit(solution)/shard_map/all_to_all | solution.py:249
  37.6 3.3 %collective-permute-start.14 = (bf16[144,1024]{1,0:T(8,128)(2,1)S(1)}, bf16[144,1024]{1,0:T(8,128)(2,1)S(1)}, u32[]{:S(2)}, u32[]{:S(2)}) collective-permute-start(bf16[144,1024]{1,0:T(8,128)(2,1)S(1)} %constant_dynamic-update-slice_fusion.t1_ref.refs_1_), channel_id=1, source_target_pairs={{0,1},{1,0},{2,3},{3,2},{4,5},{5,4},{6,7},{7,6},{8,9},{9,8},{10,11... | collective-permute-start | bytes 884744 | tf_op jit(solution)/shard_map/ppermute | solution.py:245
  43.8 2.0 %collective-permute-start.6 = (bf16[8,72,192]{2,1,0:T(8,128)(2,1)S(1)}, bf16[8,72,192]{2,1,0:T(8,128)(2,1)S(1)}, u32[]{:S(2)}, u32[]{:S(2)}) collective-permute-start(bf16[8,72,192]{2,1,0:T(8,128)(2,1)S(1)} %get-tuple-element.32), channel_id=1, source_target_pairs={{0,1},{1,0},{2,3},{3,2},{4,5},{5,4},{6,7},{7,6},{8,9},{9,8},{10,11... | collective-permute-start | bytes 663560 | tf_op jit(solution)/shard_map/ppermute | solution.py:245
  45.8 10.3 %collective-permute-start.10 = (bf16[4,72,128]{2,1,0:T(8,128)(2,1)S(1)}, bf16[4,72,128]{2,1,0:T(8,128)(2,1)S(1)}, u32[]{:S(2)}, u32[]{:S(2)}) collective-permute-start(bf16[4,72,128]{2,1,0:T(8,128)(2,1)S(1)} %get-tuple-element.36), channel_id=1, source_target_pairs={{0,17},{1,16},{16,1},{17,0},{32,49},{33,48},{48,33},{49,32},{64,81... | collective-permute-start | bytes 221192 | tf_op jit(solution)/shard_map/ppermute | solution.py:364
  56.1 3.2 %collective-permute-start.7 = (bf16[4,72,128]{2,1,0:T(8,128)(2,1)S(1)}, bf16[4,72,128]{2,1,0:T(8,128)(2,1)S(1)}, u32[]{:S(2)}, u32[]{:S(2)}) collective-permute-start(bf16[4,72,128]{2,1,0:T(8,128)(2,1)S(1)} %get-tuple-element.33), channel_id=1, source_target_pairs={{0,496},{1,497},{16,32},{17,33},{32,16},{33,17},{48,64},{49,65},{6... | collective-permute-start | bytes 221192 | tf_op jit(solution)/shard_map/ppermute | solution.py:359
  59.4 6.4 %collective-permute-start.8 = (bf16[4,72,128]{2,1,0:T(8,128)(2,1)S(1)}, bf16[4,72,128]{2,1,0:T(8,128)(2,1)}, u32[]{:S(2)}, u32[]{:S(2)}) collective-permute-start(bf16[4,72,128]{2,1,0:T(8,128)(2,1)S(1)} %get-tuple-element.34), channel_id=1, source_target_pairs={{0,16},{16,0},{1,17},{17,1},{2,18},{18,2},{3,19},{19,3},{4,20},{20... | collective-permute-start | bytes 221192 | tf_op jit(solution)/shard_map/ppermute | solution.py:245
  65.8 1.9 %collective-permute-start.9 = (bf16[4,72,128]{2,1,0:T(8,128)(2,1)S(1)}, bf16[4,72,128]{2,1,0:T(8,128)(2,1)S(1)}, u32[]{:S(2)}, u32[]{:S(2)}) collective-permute-start(bf16[4,72,128]{2,1,0:T(8,128)(2,1)S(1)} %get-tuple-element.35), channel_id=1, source_target_pairs={{0,497},{1,496},{16,33},{17,32},{32,17},{33,16},{48,65},{49,64},{6... | collective-permute-start | bytes 221192 | tf_op jit(solution)/shard_map/ppermute | solution.py:359
  67.8 2.9 %collective-permute-start.13 = (bf16[144,1024]{1,0:T(8,128)(2,1)S(1)}, bf16[144,1024]{1,0:T(8,128)(2,1)S(1)}, u32[]{:S(2)}, u32[]{:S(2)}) collective-permute-start(bf16[144,1024]{1,0:T(8,128)(2,1)S(1)} %pad_maximum_fusion.t0_ref.refs_0_), channel_id=1, source_target_pairs={{0,1},{1,0},{2,3},{3,2},{4,5},{5,4},{6,7},{7,6},{8,9},{9,8},{10,11... | collective-permute-start | bytes 884744 | tf_op jit(solution)/shard_map/ppermute | solution.py:245
  70.7 2.4 %collective-permute-start.15 = (bf16[144,1024]{1,0:T(8,128)(2,1)S(1)}, bf16[144,1024]{1,0:T(8,128)(2,1)S(1)}, u32[]{:S(2)}, u32[]{:S(2)}) collective-permute-start(bf16[144,1024]{1,0:T(8,128)(2,1)S(1)} %collective-permute-done.3.t2_ref.refs_2_), channel_id=1, source_target_pairs={{0,1},{1,0},{2,3},{3,2},{4,5},{5,4},{6,7},{7,6},{8,9},{9,8},{10,11... | collective-permute-start | bytes 884744 | tf_op jit(solution)/shard_map/ppermute | solution.py:245
  73.1 1.9 %collective-permute-start.16 = (bf16[144,1024]{1,0:T(8,128)(2,1)S(1)}, bf16[144,1024]{1,0:T(8,128)(2,1)S(1)}, u32[]{:S(2)}, u32[]{:S(2)}) collective-permute-start(bf16[144,1024]{1,0:T(8,128)(2,1)S(1)} %collective-permute-done.14.refs_5_), channel_id=1, source_target_pairs={{0,4},{2,6},{4,8},{6,10},{8,12},{10,14},{12,0},{14,2},{1,5},{3,7},... | collective-permute-start | bytes 884744 | tf_op jit(solution)/shard_map/ppermute | solution.py:245
  75.9 8.3 %shard_map.69 = (bf16[16,40,128]{2,1,0:T(8,128)(2,1)}, f32[16,72,64]{2,1,0:T(8,128)}, f32[16,72,128]{2,1,0:T(8,128)}, bf16[8,72,128]{2,1,0:T(8,128)(2,1)}, bf16[8,72,128]{2,1,0:T(8,128)(2,1)}) custom-call(s32[3]{0:T(128)} %copy-done.7, bf16[8,72,128]{2,1,0:T(8,128)(2,1)} %copy-done.8, bf16[8,72,64]{2,1,0:T(8,128)(2,1)} %copy-done.9, ...), custom_call_target="tpu_custom_call" | custom-call | flops 1019215872 | tf_op jit(solution)/shard_map/pallas_call | solution.py:286
  84.3 4.9 %collective-permute-start.11 = (bf16[8,72,128]{2,1,0:T(8,128)(2,1)}, bf16[8,72,128]{2,1,0:T(8,128)(2,1)S(1)}, u32[]{:S(2)}, u32[]{:S(2)}) collective-permute-start(bf16[8,72,128]{2,1,0:T(8,128)(2,1)} %get-tuple-element.40), channel_id=1, source_target_pairs={{0,496},{1,497},{16,32},{17,33},{32,16},{33,17},{48,64},{49,65},{6... | collective-permute-start | bytes 442376 | tf_op jit(solution)/shard_map/ppermute | solution.py:359
  89.2 5.6 %collective-permute-start.12 = (bf16[8,72,128]{2,1,0:T(8,128)(2,1)}, bf16[8,72,128]{2,1,0:T(8,128)(2,1)S(1)}, u32[]{:S(2)}, u32[]{:S(2)}) collective-permute-start(bf16[8,72,128]{2,1,0:T(8,128)(2,1)} %get-tuple-element.41), channel_id=1, source_target_pairs={{0,16},{16,0},{1,17},{17,1},{2,18},{18,2},{3,19},{19,3},{4,20},{20... | collective-permute-start | bytes 442376 | tf_op jit(solution)/shard_map/ppermute | solution.py:245
  96.6 2.6 %shard_map.71 = (bf16[16,72,192]{2,1,0:T(8,128)(2,1)}, bf16[8,72,192]{2,1,0:T(8,128)(2,1)}, bf16[8,72,192]{2,1,0:T(8,128)(2,1)}) custom-call(s32[3]{0:T(128)} %copy-done.7, f32[16,72,64]{2,1,0:T(8,128)} %get-tuple-element.38.dq_ref, f32[16,72,128]{2,1,0:T(8,128)} %get-tuple-element.39.dkv_ref, bf16[8,72,128]{2,1,0:T(8,128)(2,1)} %copy-done.19, ...), custom_call_target="tpu_custom_call" | custom-call | flops 1048576 | tf_op jit(solution)/shard_map/pallas_call | solution.py:308
  100.2 3.6 %shard_map.72 = bf16[32,48,128]{2,1,0:T(8,128)(2,1)} custom-call(s32[3]{0:T(128)} %copy-done.7, bf16[16,72,192]{2,1,0:T(8,128)(2,1)} %get-tuple-element.42.pg_ref, bf16[144,1024]{1,0:T(8,128)(2,1)} %copy-done.1, bf16[144,1024]{1,0:T(8,128)(2,1)} %copy-done.2, bf16[144,1024]{1,0:T(8,128)(2,1)} %copy-done.3, bf16[144,1024]{1,0:T(8,128)(2,1)} %copy-done.4, ...), custom_call_target="tpu_custom_call" | custom-call | flops 452984832 | tf_op jit(solution)/shard_map/pallas_call | solution.py:317
  103.8 24.0 %all_to_all.20 = bf16[32,48,128]{2,1,0:T(8,128)(2,1)S(1)} all-to-all(bf16[32,48,128]{2,1,0:T(8,128)(2,1)} %shard_map.72), channel_id=1, replica_groups=mesh['x'=4,'yh'=4,'core'=2,'z'=8,'yl'=2] {'x','yh','core'}, dimensions={0} | all-to-all | bytes 786432 | tf_op jit(solution)/shard_map/all_to_all | solution.py:249
  127.8 5.9 %all-to-all-start.1 = ((bf16[16,40,128]{2,1,0:T(8,128)(2,1)}), bf16[16,40,128]{2,1,0:T(8,128)(2,1)S(1)}, u32[]{:S(2)}, u32[]{:S(2)}) async-start(bf16[16,40,128]{2,1,0:T(8,128)(2,1)} %get-tuple-element.37), calls=%async_computation.1 | async-start | bytes 327680 | tf_op jit(solution)/shard_map/all_to_all | solution.py:249
  133.7 3.3 %collective-permute-start.17 = (bf16[8,72,192]{2,1,0:T(8,128)(2,1)S(1)}, bf16[8,72,192]{2,1,0:T(8,128)(2,1)S(1)}, u32[]{:S(2)}, u32[]{:S(2)}) collective-permute-start(bf16[8,72,192]{2,1,0:T(8,128)(2,1)S(1)} %copy-done.22), channel_id=1, source_target_pairs={{0,1},{1,0},{2,3},{3,2},{4,5},{5,4},{6,7},{7,6},{8,9},{9,8},{10,11... | collective-permute-start | bytes 663560 | tf_op jit(solution)/shard_map/ppermute | solution.py:245
  137.0 7.2 %collective-permute-done.17.got_ref = bf16[8,72,192]{2,1,0:T(8,128)(2,1)S(1)} collective-permute-done((bf16[8,72,192]{2,1,0:T(8,128)(2,1)S(1)}, bf16[8,72,192]{2,1,0:T(8,128)(2,1)S(1)}, u32[]{:S(2)}, u32[]{:S(2)}) %collective-permute-start.17) | collective-permute-done | bytes 221216 | tf_op jit(solution)/shard_map/ppermute | solution.py:245
  144.9 2.8 %shard_map.73 = (bf16[144,1024]{1,0:T(8,128)(2,1)}, bf16[144,1024]{1,0:T(8,128)(2,1)}, bf16[72,1024]{1,0:T(8,128)(2,1)}, bf16[72,1024]{1,0:T(8,128)(2,1)}, bf16[...) custom-call(s32[3]{0:T(128)} %copy-done.7, bf16[8,72,192]{2,1,0:T(8,128)(2,1)} %get-tuple-element.43.mine_ref, ...), custom_call_target="tpu_custom_call" | custom-call | flops 452984832 | tf_op jit(solution)/shard_map/pallas_call | solution.py:325
  147.7 4.9 %collective-permute-start.20 = (bf16[144,1024]{1,0:T(8,128)(2,1)}, bf16[144,1024]{1,0:T(8,128)(2,1)S(1)}, u32[]{:S(2)}, u32[]{:S(2)}) collective-permute-start(bf16[144,1024]{1,0:T(8,128)(2,1)} %get-tuple-element.49), channel_id=1, source_target_pairs={{0,12},{2,14},{4,0},{6,2},{8,4},{10,6},{12,8},{14,10},{1,13},{3,15... | collective-permute-start | bytes 884744 | tf_op jit(solution)/shard_map/ppermute | solution.py:245
  153.5 6.4 %all-to-all-start.3 = ((bf16[32,48,128]{2,1,0:T(8,128)(2,1)}), bf16[32,48,128]{2,1,0:T(8,128)(2,1)S(1)}, u32[]{:S(2)}, u32[]{:S(2)}) async-start(bf16[32,48,128]{2,1,0:T(8,128)(2,1)} %broadcast_in_dim.4), calls=%async_computation.3 | async-start | bytes 786432 | tf_op jit(solution)/shard_map/all_to_all | solution.py:249
  163.2 2.5 %collective-permute-done.20 = bf16[144,1024]{1,0:T(8,128)(2,1)S(1)} collective-permute-done((bf16[144,1024]{1,0:T(8,128)(2,1)}, bf16[144,1024]{1,0:T(8,128)(2,1)S(1)}, u32[]{:S(2)}, u32[]{:S(2)}) %collective-permute-start.20) | collective-permute-done | bytes 294944 | tf_op jit(solution)/shard_map/ppermute | solution.py:245
  165.8 6.2 %collective-permute-start.21 = (bf16[72,1024]{1,0:T(8,128)(2,1)S(1)}, bf16[72,1024]{1,0:T(8,128)(2,1)S(1)}, u32[]{:S(2)}, u32[]{:S(2)}) collective-permute-start(bf16[72,1024]{1,0:T(8,128)(2,1)S(1)} %get-tuple-element.58), channel_id=1, source_target_pairs={{0,12},{2,14},{4,0},{6,2},{8,4},{10,6},{12,8},{14,10},{1,13},{3,15... | collective-permute-start | bytes 442376 | tf_op jit(solution)/shard_map/ppermute | solution.py:245
  172.0 1.9 %collective-permute-start.22 = (bf16[72,1024]{1,0:T(8,128)(2,1)S(1)}, bf16[72,1024]{1,0:T(8,128)(2,1)S(1)}, u32[]{:S(2)}, u32[]{:S(2)}) collective-permute-start(bf16[72,1024]{1,0:T(8,128)(2,1)S(1)} %get-tuple-element.57), channel_id=1, source_target_pairs={{0,14},{2,0},{4,2},{6,4},{8,6},{10,8},{12,10},{14,12},{1,15},{3,1}... | collective-permute-start | bytes 442376 | tf_op jit(solution)/shard_map/ppermute | solution.py:245
  175.8 5.3 %collective-permute-start.19 = (bf16[72,1024]{1,0:T(8,128)(2,1)S(1)}, bf16[72,1024]{1,0:T(8,128)(2,1)S(1)}, u32[]{:S(2)}, u32[]{:S(2)}) collective-permute-start(bf16[72,1024]{1,0:T(8,128)(2,1)S(1)} %add_convert_fusion.3), channel_id=1, source_target_pairs={{0,2},{2,4},{4,6},{6,8},{8,10},{10,12},{12,14},{14,0},{1,3},{3,5},... | collective-permute-start | bytes 442376 | tf_op jit(solution)/shard_map/ppermute | solution.py:245
  (95 shorter events, 19.5 us)
Async XLA Ops:
  0.6 40.4 %copy-start.5 = (bf16[1,1024,192]{1,2,0:T(8,128)(2,1)S(1)}, bf16[1,1024,192]{1,2,0:T(8,128)(2,1)}, u32[]{:S(2)}) copy-start(bf16[1,1024,192]{1,2,0:T(8,128)(2,1)} %param.6) | copy-start | bytes 1179652
  0.6 18.7 %collective-permute-start = (bf16[72,1024]{1,0:T(8,128)(2,1)}, bf16[72,1024]{1,0:T(8,128)(2,1)S(1)}, u32[]{:S(2)}, u32[]{:S(2)}) collective-permute-start(bf16[72,1024]{1,0:T(8,128)(2,1)} %bitcast.33), channel_id=1, source_target_pairs={{0,14},{2,0},{4,2},{6,4},{8,6},{10,8},{12,10},{14,12},{1,15},{3,1}... | collective-permute-start | bytes 442376 | tf_op jit(solution)/shard_map/ppermute | solution.py:245
  12.3 13.5 %collective-permute-start.1 = (bf16[72,1024]{1,0:T(8,128)(2,1)}, bf16[72,1024]{1,0:T(8,128)(2,1)S(1)}, u32[]{:S(2)}, u32[]{:S(2)}) collective-permute-start(bf16[72,1024]{1,0:T(8,128)(2,1)} %bitcast.34), channel_id=1, source_target_pairs={{0,2},{2,4},{4,6},{6,8},{8,10},{10,12},{12,14},{14,0},{1,3},{3,5},... | collective-permute-start | bytes 442376 | tf_op jit(solution)/shard_map/ppermute | solution.py:245
  14.2 11.6 %collective-permute-start.2 = (bf16[72,1024]{1,0:T(8,128)(2,1)}, bf16[72,1024]{1,0:T(8,128)(2,1)S(1)}, u32[]{:S(2)}, u32[]{:S(2)}) collective-permute-start(bf16[72,1024]{1,0:T(8,128)(2,1)} %bitcast.35), channel_id=1, source_target_pairs={{0,4},{2,6},{4,8},{6,10},{8,12},{10,14},{12,0},{14,2},{1,5},{3,7},... | collective-permute-start | bytes 442376 | tf_op jit(solution)/shard_map/ppermute | solution.py:245
  16.1 24.9 %collective-permute-start.5 = (bf16[192,1024]{1,0:T(8,128)(2,1)}, bf16[192,1024]{1,0:T(8,128)(2,1)S(1)}, u32[]{:S(2)}, u32[]{:S(2)}) collective-permute-start(bf16[192,1024]{1,0:T(8,128)(2,1)} %bitcast.24), channel_id=1, source_target_pairs={{0,1},{1,0},{2,3},{3,2},{4,5},{5,4},{6,7},{7,6},{8,9},{9,8},{10,11... | collective-permute-start | bytes 1179656 | tf_op jit(solution)/shard_map/ppermute | solution.py:245
  20.3 47.5 %copy-start.1 = (bf16[144,1024]{1,0:T(8,128)(2,1)}, bf16[144,1024]{1,0:T(8,128)(2,1)S(1)}, u32[]{:S(2)}) copy-start(bf16[144,1024]{1,0:T(8,128)(2,1)S(1)} %pad_maximum_fusion.t0_ref.refs_0_) | copy-start | bytes 884740
  20.3 20.7 %collective-permute-start.3 = (bf16[144,1024]{1,0:T(8,128)(2,1)S(1)}, bf16[144,1024]{1,0:T(8,128)(2,1)S(1)}, u32[]{:S(2)}, u32[]{:S(2)}) collective-permute-start(bf16[144,1024]{1,0:T(8,128)(2,1)S(1)} %pad_maximum_fusion.t0_ref.refs_0_), channel_id=1, source_target_pairs={{0,12},{2,14},{4,0},{6,2},{8,4},{10,6},{12,8},{14,10},{1,13},{3,15... | collective-permute-start | bytes 884744 | tf_op jit(solution)/shard_map/ppermute | solution.py:245
  25.8 15.2 %collective-permute-start.4 = (bf16[144,1024]{1,0:T(8,128)(2,1)S(1)}, bf16[144,1024]{1,0:T(8,128)(2,1)S(1)}, u32[]{:S(2)}, u32[]{:S(2)}) collective-permute-start(bf16[144,1024]{1,0:T(8,128)(2,1)S(1)} %constant_dynamic-update-slice_fusion.t1_ref.refs_1_), channel_id=1, source_target_pairs={{0,4},{2,6},{4,8},{6,10},{8,12},{10,14},{12,0},{14,2},{1,5},{3,7},... | collective-permute-start | bytes 884744 | tf_op jit(solution)/shard_map/ppermute | solution.py:245
  31.0 44.0 %all-to-all-start = ((bf16[16,40,128]{2,1,0:T(8,128)(2,1)}), bf16[16,40,128]{2,1,0:T(8,128)(2,1)S(1)}, u32[]{:S(2)}, u32[]{:S(2)}) async-start(bf16[16,40,128]{2,1,0:T(8,128)(2,1)} %shard_map.68), calls=%async_computation | async-start | bytes 327680 | tf_op jit(solution)/shard_map/all_to_all | solution.py:249
  37.6 28.2 %collective-permute-start.14 = (bf16[144,1024]{1,0:T(8,128)(2,1)S(1)}, bf16[144,1024]{1,0:T(8,128)(2,1)S(1)}, u32[]{:S(2)}, u32[]{:S(2)}) collective-permute-start(bf16[144,1024]{1,0:T(8,128)(2,1)S(1)} %constant_dynamic-update-slice_fusion.t1_ref.refs_1_), channel_id=1, source_target_pairs={{0,1},{1,0},{2,3},{3,2},{4,5},{5,4},{6,7},{7,6},{8,9},{9,8},{10,11... | collective-permute-start | bytes 884744 | tf_op jit(solution)/shard_map/ppermute | solution.py:245
  41.0 43.3 %copy-start.6 = (bf16[192,1024]{1,0:T(8,128)(2,1)}, bf16[192,1024]{1,0:T(8,128)(2,1)S(1)}, u32[]{:S(2)}) copy-start(bf16[192,1024]{1,0:T(8,128)(2,1)S(1)} %collective-permute-done.5.other_ref) | copy-start | bytes 1179652
  41.0 43.2 %copy-start.3 = (bf16[144,1024]{1,0:T(8,128)(2,1)}, bf16[144,1024]{1,0:T(8,128)(2,1)S(1)}, u32[]{:S(2)}) copy-start(bf16[144,1024]{1,0:T(8,128)(2,1)S(1)} %collective-permute-done.3.t2_ref.refs_2_) | copy-start | bytes 884740
  41.0 43.2 %copy-start.4 = (bf16[144,1024]{1,0:T(8,128)(2,1)}, bf16[144,1024]{1,0:T(8,128)(2,1)S(1)}, u32[]{:S(2)}) copy-start(bf16[144,1024]{1,0:T(8,128)(2,1)S(1)} %collective-permute-done.4.t3_ref.refs_3_) | copy-start | bytes 884740
  43.8 31.3 %collective-permute-start.6 = (bf16[8,72,192]{2,1,0:T(8,128)(2,1)S(1)}, bf16[8,72,192]{2,1,0:T(8,128)(2,1)S(1)}, u32[]{:S(2)}, u32[]{:S(2)}) collective-permute-start(bf16[8,72,192]{2,1,0:T(8,128)(2,1)S(1)} %get-tuple-element.32), channel_id=1, source_target_pairs={{0,1},{1,0},{2,3},{3,2},{4,5},{5,4},{6,7},{7,6},{8,9},{9,8},{10,11... | collective-permute-start | bytes 663560 | tf_op jit(solution)/shard_map/ppermute | solution.py:245
  45.8 21.9 %collective-permute-start.10 = (bf16[4,72,128]{2,1,0:T(8,128)(2,1)S(1)}, bf16[4,72,128]{2,1,0:T(8,128)(2,1)S(1)}, u32[]{:S(2)}, u32[]{:S(2)}) collective-permute-start(bf16[4,72,128]{2,1,0:T(8,128)(2,1)S(1)} %get-tuple-element.36), channel_id=1, source_target_pairs={{0,17},{1,16},{16,1},{17,0},{32,49},{33,48},{48,33},{49,32},{64,81... | collective-permute-start | bytes 221192 | tf_op jit(solution)/shard_map/ppermute | solution.py:364
  56.1 14.6 %collective-permute-start.7 = (bf16[4,72,128]{2,1,0:T(8,128)(2,1)S(1)}, bf16[4,72,128]{2,1,0:T(8,128)(2,1)S(1)}, u32[]{:S(2)}, u32[]{:S(2)}) collective-permute-start(bf16[4,72,128]{2,1,0:T(8,128)(2,1)S(1)} %get-tuple-element.33), channel_id=1, source_target_pairs={{0,496},{1,497},{16,32},{17,33},{32,16},{33,17},{48,64},{49,65},{6... | collective-permute-start | bytes 221192 | tf_op jit(solution)/shard_map/ppermute | solution.py:359
  59.4 13.8 %collective-permute-start.8 = (bf16[4,72,128]{2,1,0:T(8,128)(2,1)S(1)}, bf16[4,72,128]{2,1,0:T(8,128)(2,1)}, u32[]{:S(2)}, u32[]{:S(2)}) collective-permute-start(bf16[4,72,128]{2,1,0:T(8,128)(2,1)S(1)} %get-tuple-element.34), channel_id=1, source_target_pairs={{0,16},{16,0},{1,17},{17,1},{2,18},{18,2},{3,19},{19,3},{4,20},{20... | collective-permute-start | bytes 221192 | tf_op jit(solution)/shard_map/ppermute | solution.py:245
  65.8 9.2 %collective-permute-start.9 = (bf16[4,72,128]{2,1,0:T(8,128)(2,1)S(1)}, bf16[4,72,128]{2,1,0:T(8,128)(2,1)S(1)}, u32[]{:S(2)}, u32[]{:S(2)}) collective-permute-start(bf16[4,72,128]{2,1,0:T(8,128)(2,1)S(1)} %get-tuple-element.35), channel_id=1, source_target_pairs={{0,497},{1,496},{16,33},{17,32},{32,17},{33,16},{48,65},{49,64},{6... | collective-permute-start | bytes 221192 | tf_op jit(solution)/shard_map/ppermute | solution.py:359
  67.8 31.5 %collective-permute-start.13 = (bf16[144,1024]{1,0:T(8,128)(2,1)S(1)}, bf16[144,1024]{1,0:T(8,128)(2,1)S(1)}, u32[]{:S(2)}, u32[]{:S(2)}) collective-permute-start(bf16[144,1024]{1,0:T(8,128)(2,1)S(1)} %pad_maximum_fusion.t0_ref.refs_0_), channel_id=1, source_target_pairs={{0,1},{1,0},{2,3},{3,2},{4,5},{5,4},{6,7},{7,6},{8,9},{9,8},{10,11... | collective-permute-start | bytes 884744 | tf_op jit(solution)/shard_map/ppermute | solution.py:245
  70.7 28.5 %collective-permute-start.15 = (bf16[144,1024]{1,0:T(8,128)(2,1)S(1)}, bf16[144,1024]{1,0:T(8,128)(2,1)S(1)}, u32[]{:S(2)}, u32[]{:S(2)}) collective-permute-start(bf16[144,1024]{1,0:T(8,128)(2,1)S(1)} %collective-permute-done.3.t2_ref.refs_2_), channel_id=1, source_target_pairs={{0,1},{1,0},{2,3},{3,2},{4,5},{5,4},{6,7},{7,6},{8,9},{9,8},{10,11... | collective-permute-start | bytes 884744 | tf_op jit(solution)/shard_map/ppermute | solution.py:245
  73.1 26.2 %collective-permute-start.16 = (bf16[144,1024]{1,0:T(8,128)(2,1)S(1)}, bf16[144,1024]{1,0:T(8,128)(2,1)S(1)}, u32[]{:S(2)}, u32[]{:S(2)}) collective-permute-start(bf16[144,1024]{1,0:T(8,128)(2,1)S(1)} %collective-permute-done.14.refs_5_), channel_id=1, source_target_pairs={{0,4},{2,6},{4,8},{6,10},{8,12},{10,14},{12,0},{14,2},{1,5},{3,7},... | collective-permute-start | bytes 884744 | tf_op jit(solution)/shard_map/ppermute | solution.py:245
  84.3 10.5 %collective-permute-start.11 = (bf16[8,72,128]{2,1,0:T(8,128)(2,1)}, bf16[8,72,128]{2,1,0:T(8,128)(2,1)S(1)}, u32[]{:S(2)}, u32[]{:S(2)}) collective-permute-start(bf16[8,72,128]{2,1,0:T(8,128)(2,1)} %get-tuple-element.40), channel_id=1, source_target_pairs={{0,496},{1,497},{16,32},{17,33},{32,16},{33,17},{48,64},{49,65},{6... | collective-permute-start | bytes 442376 | tf_op jit(solution)/shard_map/ppermute | solution.py:359
  89.2 6.8 %collective-permute-start.12 = (bf16[8,72,128]{2,1,0:T(8,128)(2,1)}, bf16[8,72,128]{2,1,0:T(8,128)(2,1)S(1)}, u32[]{:S(2)}, u32[]{:S(2)}) collective-permute-start(bf16[8,72,128]{2,1,0:T(8,128)(2,1)} %get-tuple-element.41), channel_id=1, source_target_pairs={{0,16},{16,0},{1,17},{17,1},{2,18},{18,2},{3,19},{19,3},{4,20},{20... | collective-permute-start | bytes 442376 | tf_op jit(solution)/shard_map/ppermute | solution.py:245
  103.8 58.0 %copy-start = (bf16[16,64,1024]{2,1,0:T(8,128)(2,1)S(1)}, bf16[16,64,1024]{2,1,0:T(8,128)(2,1)}, u32[]{:S(2)}) copy-start(bf16[16,64,1024]{2,1,0:T(8,128)(2,1)} %weight_ref.1) | copy-start | bytes 6291460
  127.8 24.9 %all-to-all-start.1 = ((bf16[16,40,128]{2,1,0:T(8,128)(2,1)}), bf16[16,40,128]{2,1,0:T(8,128)(2,1)S(1)}, u32[]{:S(2)}, u32[]{:S(2)}) async-start(bf16[16,40,128]{2,1,0:T(8,128)(2,1)} %get-tuple-element.37), calls=%async_computation.1 | async-start | bytes 327680 | tf_op jit(solution)/shard_map/all_to_all | solution.py:249
  133.7 10.5 %collective-permute-start.17 = (bf16[8,72,192]{2,1,0:T(8,128)(2,1)S(1)}, bf16[8,72,192]{2,1,0:T(8,128)(2,1)S(1)}, u32[]{:S(2)}, u32[]{:S(2)}) collective-permute-start(bf16[8,72,192]{2,1,0:T(8,128)(2,1)S(1)} %copy-done.22), channel_id=1, source_target_pairs={{0,1},{1,0},{2,3},{3,2},{4,5},{5,4},{6,7},{7,6},{8,9},{9,8},{10,11... | collective-permute-start | bytes 663560 | tf_op jit(solution)/shard_map/ppermute | solution.py:245
  147.7 18.0 %collective-permute-start.20 = (bf16[144,1024]{1,0:T(8,128)(2,1)}, bf16[144,1024]{1,0:T(8,128)(2,1)S(1)}, u32[]{:S(2)}, u32[]{:S(2)}) collective-permute-start(bf16[144,1024]{1,0:T(8,128)(2,1)} %get-tuple-element.49), channel_id=1, source_target_pairs={{0,12},{2,14},{4,0},{6,2},{8,4},{10,6},{12,8},{14,10},{1,13},{3,15... | collective-permute-start | bytes 884744 | tf_op jit(solution)/shard_map/ppermute | solution.py:245
  153.5 27.6 %all-to-all-start.3 = ((bf16[32,48,128]{2,1,0:T(8,128)(2,1)}), bf16[32,48,128]{2,1,0:T(8,128)(2,1)S(1)}, u32[]{:S(2)}, u32[]{:S(2)}) async-start(bf16[32,48,128]{2,1,0:T(8,128)(2,1)} %broadcast_in_dim.4), calls=%async_computation.3 | async-start | bytes 786432 | tf_op jit(solution)/shard_map/all_to_all | solution.py:249
  159.9 15.8 %collective-permute-start.18 = (bf16[144,1024]{1,0:T(8,128)(2,1)}, bf16[144,1024]{1,0:T(8,128)(2,1)S(1)}, u32[]{:S(2)}, u32[]{:S(2)}) collective-permute-start(bf16[144,1024]{1,0:T(8,128)(2,1)} %get-tuple-element.46), channel_id=1, source_target_pairs={{0,4},{2,6},{4,8},{6,10},{8,12},{10,14},{12,0},{14,2},{1,5},{3,7},... | collective-permute-start | bytes 884744 | tf_op jit(solution)/shard_map/ppermute | solution.py:245
  165.8 16.7 %collective-permute-start.21 = (bf16[72,1024]{1,0:T(8,128)(2,1)S(1)}, bf16[72,1024]{1,0:T(8,128)(2,1)S(1)}, u32[]{:S(2)}, u32[]{:S(2)}) collective-permute-start(bf16[72,1024]{1,0:T(8,128)(2,1)S(1)} %get-tuple-element.58), channel_id=1, source_target_pairs={{0,12},{2,14},{4,0},{6,2},{8,4},{10,6},{12,8},{14,10},{1,13},{3,15... | collective-permute-start | bytes 442376 | tf_op jit(solution)/shard_map/ppermute | solution.py:245
  172.0 10.4 %collective-permute-start.22 = (bf16[72,1024]{1,0:T(8,128)(2,1)S(1)}, bf16[72,1024]{1,0:T(8,128)(2,1)S(1)}, u32[]{:S(2)}, u32[]{:S(2)}) collective-permute-start(bf16[72,1024]{1,0:T(8,128)(2,1)S(1)} %get-tuple-element.57), channel_id=1, source_target_pairs={{0,14},{2,0},{4,2},{6,4},{8,6},{10,8},{12,10},{14,12},{1,15},{3,1}... | collective-permute-start | bytes 442376 | tf_op jit(solution)/shard_map/ppermute | solution.py:245
  175.8 8.0 %collective-permute-start.19 = (bf16[72,1024]{1,0:T(8,128)(2,1)S(1)}, bf16[72,1024]{1,0:T(8,128)(2,1)S(1)}, u32[]{:S(2)}, u32[]{:S(2)}) collective-permute-start(bf16[72,1024]{1,0:T(8,128)(2,1)S(1)} %add_convert_fusion.3), channel_id=1, source_target_pairs={{0,2},{2,4},{4,6},{6,8},{8,10},{10,12},{12,14},{14,0},{1,3},{3,5},... | collective-permute-start | bytes 442376 | tf_op jit(solution)/shard_map/ppermute | solution.py:245
  (21 other events, 198.9 us)
